TPU v7x, 128 devices: a whole 4x4x4 slice. The times are simulated.
128 devices in a mesh: dp: 32 (over y_lo, z, x), mp: 4 (over y_hi, core).
Axes of the slice: x: 4, y: 4 (y_hi: 2, y_lo: 2; y = y_hi * 2 + y_lo), z: 4, core: 2. Of those that a mesh axis runs over, the one named last changes fastest.
Arguments:
- layer_inputs: bfloat16 [16384, 8192], P('dp', 'mp'), may hold values from -54 to 54
- out_grads: bfloat16 [16384, 28672], P('dp', 'mp'), may hold values from -54 to 54
- loss_mask: int32 [16384], P('dp'), may hold values 0 or 1
- start_in: int32 [64, 8192], P(None, 'mp'), may hold values from -127 to 127
- start_out: int32 [64, 28672], P(None, 'mp'), may hold values from -127 to 127
Outputs:
- features: float32 [64, 4096], P('dp', 'mp')
- basis_in: float32 [64, 8192], P(None, 'mp')
- basis_out: float32 [64, 28672], P(None, 'mp')
All inputs are finite; a program needn't handle non-finite values. No bound on the sum of `loss_mask` on one device may be relied on, other than what follows from the above.
Results may differ from a plain program's by a relative error of at most 0.0065.
Values may be sent and summed in bfloat16 or wider, within the bound.
No kernel may reach another device: no remote copies, remote signals or barrier semaphores. Data moves between devices by JAX's collectives and lax.ppermute only.
A program may use at most 64 MiB of HBM per device.

v0:
```python
import jax
import jax.numpy as jnp
from jax import lax
from jax.sharding import PartitionSpec as P

ITERS = 2
LEN = 256


def coords_of(data, basis_half):
    return lax.dot_general(
        data, basis_half, (((1,), (1,)), ((), ())), preferred_element_type=jnp.float32
    )


def image_of(coords_half, data):
    return lax.dot_general(
        coords_half, data, (((0,), (0,)), ((), ())), preferred_element_type=jnp.float32
    )


def gram_of(image):
    return jnp.dot(image, image.T, precision=lax.Precision.HIGHEST)


def normalize(gram, image):
    lower = jnp.linalg.cholesky(gram)
    return jax.scipy.linalg.solve_triangular(lower, image, lower=True)


def shards(layer_inputs, out_grads, loss_mask, start_in, start_out):
    keep = loss_mask.astype(jnp.float32)[:, None]
    basis_in = start_in.astype(jnp.float32) / 128.0
    basis_out = start_out.astype(jnp.float32) / 128.0
    half_in = basis_in.astype(jnp.bfloat16)
    half_out = basis_out.astype(jnp.bfloat16)
    for step in range(ITERS):
        in_coords = coords_of(layer_inputs, half_in)
        out_coords = coords_of(out_grads, half_out) * keep
        in_coords, out_coords = lax.psum((in_coords, out_coords), "mp")
        in_image = image_of(in_coords.astype(jnp.bfloat16), layer_inputs)
        out_image = image_of(out_coords.astype(jnp.bfloat16), out_grads)
        out_owned = lax.psum_scatter(out_image, "dp", scatter_dimension=1, tiled=True)
        in_whole = lax.psum(in_image, "dp")
        gram_in = lax.psum(gram_of(in_whole), "mp")
        gram_out = lax.psum(gram_of(out_owned), ("dp", "mp"))
        new_in = normalize(gram_in, in_whole)
        new_out = normalize(gram_out, out_owned)
        if step + 1 < ITERS:
            half_in = new_in.astype(jnp.bfloat16)
            half_out = lax.all_gather(new_out.astype(jnp.bfloat16), "dp", axis=1, tiled=True)
        else:
            basis_in = new_in
            basis_out = lax.all_gather(new_out, "dp", axis=1, tiled=True)
    half_in = basis_in.astype(jnp.bfloat16)
    half_out = basis_out.astype(jnp.bfloat16)
    proj_in = coords_of(layer_inputs, half_in)
    proj_out = coords_of(out_grads, half_out) * keep
    rank = half_in.shape[0]
    seq_count = layer_inputs.shape[0] // LEN
    proj_in, proj_out = lax.psum((proj_in, proj_out), "mp")
    block = rank // lax.axis_size("mp")
    first = lax.axis_index("mp") * block
    part_in = lax.dynamic_slice_in_dim(proj_in.astype(jnp.bfloat16), first, block, 1)
    seq_in = part_in.reshape(seq_count, LEN, block)
    seq_out = proj_out.astype(jnp.bfloat16).reshape(seq_count, LEN, rank)
    summed = jnp.einsum("sti,stj->sij", seq_in, seq_out, preferred_element_type=jnp.float32) / LEN
    features = summed.reshape(seq_count, block * rank)
    return (features, basis_in, basis_out)


def solution(mesh):
    in_specs = (P("dp", "mp"), P("dp", "mp"), P("dp"), P(None, "mp"), P(None, "mp"))
    out_specs = (P("dp", "mp"), P(None, "mp"), P(None, "mp"))
    return jax.shard_map(shards, mesh=mesh, in_specs=in_specs, out_specs=out_specs, check_vma=False)
```

profile of v0, /device:TPU:1, one launch (start us, length us, event | category | flops | bytes accessed | tf_op | source)
XLA Modules:
  0.0 1492.7 jit_solution(5499521624738872316)
XLA Ops:
  10.6 15.8 %all-reduce.13 = bf16[512,64]{0,1:T(8,128)(2,1)S(1)} all-reduce(f32[512,64]{0,1:T(8,128)S(1)} %convolution_bitcast_fusion.4), channel_id=1, replica_groups=mesh['dp'=32,'mp'=4] {'mp'}, use_global_device_ids=true, to_apply=%region_0.0 | all-reduce | flops 32768 | bytes 196608 | tf_op jit(solution)/shard_map/psum | solution.py:40
  27.7 6.0 fusion.2
  33.7 285.4 %all-reduce.10.cloned.1.call-done = f32[64,2048]{1,0:T(8,128)} async-done(((f32[64,2048]{1,0:T(8,128)}), f32[64,2048]{1,0:T(8,128)}) %all-reduce.10.cloned.1.call-update) | async-done | bytes 524304 | tf_op jit(solution)/shard_map/psum | solution.py:44
  320.9 34.3 %psum.86 = f32[64,64]{0,1:T(8,128)S(1)} all-reduce(f32[64,64]{0,1:T(8,128)S(1)} %fusion.41), channel_id=1, replica_groups=mesh['dp'=32,'mp'=4] {'mp'}, use_global_device_ids=true, to_apply=%region_2.0 | all-reduce | flops 4096 | bytes 32768 | tf_op jit(solution)/shard_map/psum | solution.py:45
  355.3 5.8 cholesky.74
  369.8 16.8 %all-reduce.14 = (bf16[512,64]{0,1:T(8,128)(2,1)S(1)}, bf16[512,64]{0,1:T(8,128)(2,1)S(1)}) all-reduce(f32[512,64]{0,1:T(8,128)S(1)} %fusion.2, f32[512,64]{0,1:T(8,128)S(1)} %convolution_bitcast_fusion.3), channel_id=1, replica_groups=mesh['dp'=32,'mp'=4] {'mp'}, use_global_device_ids=true, to_apply=%region_9.12 | all-reduce | flops 65536 | bytes 393216 | tf_op jit(solution)/shard_map/psum | solution.py:40
  388.0 7.9 convolution_bitcast_fusion.1
  395.9 281.3 %all-reduce.12.cloned.1.call-done = f32[64,2048]{1,0:T(8,128)} async-done(((f32[64,2048]{1,0:T(8,128)}), f32[64,2048]{1,0:T(8,128)}) %all-reduce.12.cloned.1.call-update) | async-done | bytes 524304 | tf_op jit(solution)/shard_map/psum | solution.py:44
  679.0 167.0 %reduce-scatter.7.cloned.1.call-done = f32[224,64]{1,0:T(8,128)} async-done(((f32[7168,64]{1,0:T(8,128)}), f32[224,64]{1,0:T(8,128)}) %reduce-scatter.7.cloned.1.call-update) | async-done | bytes 57360
  847.4 86.2 %psum.92 = f32[64,64]{0,1:T(8,128)S(1)} all-reduce(f32[64,64]{0,1:T(8,128)S(1)} %fusion.11), channel_id=1, replica_groups=mesh['dp'=32,'mp'=4] {'dp','mp'}, use_global_device_ids=true, to_apply=%region_11.14 | all-reduce | flops 4096 | bytes 32768 | tf_op jit(solution)/shard_map/psum | solution.py:46
  933.6 5.8 cholesky.96
  947.0 69.9 %all-gather = bf16[32,224,64]{1,2,0:T(8,128)(2,1)S(1)} all-gather(bf16[1,224,64]{1,2,0:T(8,128)(2,1)S(1)} %fusion.3), channel_id=1, replica_groups=mesh['dp'=32,'mp'=4] {'dp'}, dimensions={0}, use_global_device_ids=true | all-gather | bytes 946176 | tf_op jit(solution)/shard_map/all_gather | solution.py:51
  1020.2 5.7 fusion.1
  1026.0 28.4 %all-reduce.15 = (bf16[512,64]{0,1:T(8,128)(2,1)S(1)}, f32[64,64]{0,1:T(8,128)S(1)}) all-reduce(f32[512,64]{0,1:T(8,128)S(1)} %fusion.1, f32[64,64]{0,1:T(8,128)S(1)} %fusion.42), channel_id=1, replica_groups=mesh['dp'=32,'mp'=4] {'mp'}, use_global_device_ids=true, to_apply=%region_12.0 | all-reduce | flops 36864 | bytes 229376 | tf_op jit(solution)/shard_map/psum | solution.py:40
  1054.4 7.9 convolution_bitcast_fusion
  1062.4 140.7 %reduce-scatter.9.cloned.1.call-done = f32[224,64]{1,0:T(8,128)} async-done(((f32[7168,64]{1,0:T(8,128)}), f32[224,64]{1,0:T(8,128)}) %reduce-scatter.9.cloned.1.call-update) | async-done | bytes 57360
  1204.4 86.6 %psum.94 = f32[64,64]{0,1:T(8,128)S(1)} all-reduce(f32[64,64]{0,1:T(8,128)S(1)} %fusion.8), channel_id=1, replica_groups=mesh['dp'=32,'mp'=4] {'dp','mp'}, use_global_device_ids=true, to_apply=%region_14.18 | all-reduce | flops 4096 | bytes 32768 | tf_op jit(solution)/shard_map/psum | solution.py:46
  1291.1 5.8 cholesky.107
  1298.3 4.9 custom-call.13
  1305.2 5.8 cholesky.85
  1312.4 4.9 custom-call.11
  1318.7 114.7 %all-gather.4.cloned.1.call-done = f32[32,224,64]{1,2,0:T(8,128)} async-done(((f32[1,224,64]{1,2,0:T(8,128)}), f32[32,224,64]{1,2,0:T(8,128)}) %all-gather.4.cloned.1.call-update) | async-done | bytes 1835024 | tf_op jit(solution)/shard_map/all_gather | solution.py:54
  1441.0 6.0 fusion
  1446.9 38.4 %all-reduce.16 = (bf16[512,64]{0,1:T(8,128)(2,1)S(1)}, bf16[512,64]{0,1:T(8,128)(2,1)S(1)}) all-reduce(f32[512,64]{0,1:T(8,128)S(1)} %fusion, f32[512,64]{0,1:T(8,128)S(1)} %convolution_bitcast_fusion.2), channel_id=1, replica_groups=mesh['dp'=32,'mp'=4] {'mp'}, use_global_device_ids=true, to_apply=%region_15.19 | all-reduce | flops 65536 | bytes 393216 | tf_op jit(solution)/shard_map/psum | solution.py:61
  (61 shorter events, 46.5 us)
Async XLA Ops:
  7.2 1.6 copy-start
  7.2 312.0 %all-reduce.10.cloned.1.call-start = ((), (), s32[]{:S(2)}) async-start(), calls=%async_computation.2 | async-start | bytes 1048576 | tf_op jit(solution)/shard_map/psum | solution.py:44
  10.6 17.1 %copy-start.3 = (s32[512]{0:T(512)S(1)}, s32[512]{0:T(512)}, u32[]{:S(2)}) copy-start(s32[512]{0:T(512)} %param.12) | copy-start | bytes 6148
  27.6 649.6 %all-reduce.12.cloned.1.call-start = ((), (), s32[]{:S(2)}) async-start(), calls=%async_computation.3 | async-start | bytes 1048576 | tf_op jit(solution)/shard_map/psum | solution.py:44
  387.9 458.1 %reduce-scatter.7.cloned.1.call-start = ((), (), s32[]{:S(2)}) async-start(), calls=%async_computation.5 | async-start | bytes 3784704
  395.9 807.2 %reduce-scatter.9.cloned.1.call-start = ((), (), s32[]{:S(2)}) async-start(), calls=%async_computation.6 | async-start | bytes 3784704
  1062.3 255.0 %copy-start.1 = (f32[64,2048]{1,0:T(8,128)S(1)}, f32[64,2048]{1,0:T(8,128)}, u32[]{:S(2)}) copy-start(f32[64,2048]{1,0:T(8,128)} %all-reduce.12.cloned.1.call-done) | copy-start | bytes 1572868
  1062.3 371.1 %all-gather.4.cloned.1.call-start = ((), (), s32[]{:S(2)}) async-start(), calls=%async_computation.4 | async-start | bytes 2162688 | tf_op jit(solution)/shard_map/all_gather | solution.py:54
  1318.0 119.6 %copy-start.2 = (f32[64,2048]{1,0:T(8,128)}, f32[64,2048]{1,0:T(8,128)S(1)}, u32[]{:S(2)}) copy-start(f32[64,2048]{1,0:T(8,128)S(1)} %fusion.30) | copy-start | bytes 1572868
Sparse Core Ops, SparseCore 0:
  27.8 291.3 all-reduce.9
  388.0 289.1 all-reduce.11
  679.6 166.3 reduce-scatter.6
  1062.4 140.6 reduce-scatter.8
  1305.2 128.1 all-gather.3
where the time goes:
time: 1490 us
  waiting for transfers between devices  989 us (66%)
  blocking collectives  376 us (25%)
  matrix products  51.1 us (3%)
  other arithmetic  48.3 us (3%)
    psum x2, waiting for transfers between devices, shards(): in_whole = lax.psum(in_image, 'dp')  567 us
    unnamed x7, waiting for transfers between devices  308 us
    psum x2, blocking collectives, shards(): gram_out = lax.psum(gram_of(out_owned), ('dp', 'mp'))  173 us
    all_gather x1, waiting for transfers between devices, shards(): basis_out = lax.all_gather(new_out, 'dp', axis=1, tiled=True)  115 us
    all_gather x1, blocking collectives, shards(): lax.all_gather(new_out.astype(jnp.bfloat16), 'dp', axis=1, tiled=True)  69.9 us
    psum x3, blocking collectives, shards(): in_coords, out_coords = lax.psum((in_coords, out_coords), 'mp')  61 us
    psum x1, blocking collectives, shards(): proj_in, proj_out = lax.psum((proj_in, proj_out), 'mp')  38.4 us
    psum x1, blocking collectives, shards(): gram_in = lax.psum(gram_of(in_whole), 'mp')  34.3 us
  transfers between devices with their start and end apart: 5, of which 5 were waited for; matrix products, arithmetic and copies ran while one was open for 2% of the time, Pallas kernels for 0%

commit v1 on v0

v1 whole, which is shorter than its diff:
```python
import functools

import jax
import jax.numpy as jnp
from jax import lax
from jax.experimental import pallas as pl
from jax.experimental.pallas import tpu as pltpu
from jax.sharding import PartitionSpec as P

ITERS = 2
LEN = 256
R = 64
ROWS = 16
GROUPS = R // ROWS
NT = (((1,), (1,)), ((), ()))
F32 = jnp.float32
BF16 = jnp.bfloat16


def split3(x):
    a = x.astype(BF16)
    rest = x - a.astype(F32)
    b = rest.astype(BF16)
    c = (rest - b.astype(F32)).astype(BF16)
    return jnp.concatenate([a, b, c], axis=1)


def eliminate(gram):
    n = gram.shape[0]
    col_id = lax.broadcasted_iota(jnp.int32, (n, n), 1)
    row_id = lax.broadcasted_iota(jnp.int32, (n, n), 0)
    eye = (col_id == row_id).astype(F32)
    work = jnp.concatenate([gram, eye], axis=1)
    tiles = [work[8 * i : 8 * i + 8] for i in range(n // 8)]
    sub = lax.broadcasted_iota(jnp.int32, (8, 1), 0)
    for k in range(n - 1):
        t, r = divmod(k, 8)
        row = tiles[t][r : r + 1]
        scaled = row * (1.0 / row[:, k : k + 1])
        for i in range(t, n // 8):
            col = tiles[i][:, k : k + 1]
            if i == t:
                if r == 7:
                    continue
                col = jnp.where(sub > r, col, 0.0)
            tiles[i] = tiles[i] - col * scaled
    work = jnp.concatenate(tiles, axis=0)
    diag = jnp.sum(jnp.where(col_id == row_id, work[:, :n], 0.0), axis=1, keepdims=True)
    return work[:, n:] * (1.0 / jnp.sqrt(diag))


def raw_kernel(first, steps, core, *refs):
    if first:
        bin_ref, bout_ref, min_ref, mout_ref, mask_ref, send, keep, acc = refs
    else:
        img_ref, min_ref, mout_ref, mask_ref, send, keep, acc, gin, gout = refs
    h = pl.program_id(0)

    @pl.when(h == 0)
    def _():
        acc[...] = jnp.zeros_like(acc)
        if not first:
            gin[...] = jnp.zeros_like(gin)
            gout[...] = jnp.zeros_like(gout)

    if first:
        half_in = (bin_ref[...].astype(F32) * (1.0 / 128.0)).astype(BF16)
        half_out = (bout_ref[...].astype(F32) * (1.0 / 128.0)).astype(BF16)
    else:
        wide = min_ref.shape[1]
        img = jnp.concatenate([img_ref[g, 0] for g in range(GROUPS)], axis=0)
        half_in = img[:, :wide]
        half_out = img[:, wide:]
        gin[...] += lax.dot_general(half_in, half_in, NT, preferred_element_type=F32)
        gout[...] += lax.dot_general(half_out, half_out, NT, preferred_element_type=F32)
    acc[:R] += lax.dot_general(half_in, min_ref[...], NT, preferred_element_type=F32)
    acc[R:] += lax.dot_general(half_out, mout_ref[...], NT, preferred_element_type=F32)

    @pl.when(h == steps - 1)
    def _():
        tokens = acc.shape[1] // 2
        mask = mask_ref[...].astype(F32)
        acc[R:] = acc[R:] * mask
        mine = pl.ds(pl.multiple_of(core[0] * tokens, tokens), tokens)
        other = pl.ds(pl.multiple_of((1 - core[0]) * tokens, tokens), tokens)
        keep[: 2 * R] = acc[:, mine]
        send[: 2 * R] = acc[:, other]
        if not first:
            gram = jnp.concatenate([gin[...], gout[...]], axis=1)
            gram = jnp.concatenate([gram[: R // 2], gram[R // 2 :]], axis=1)
            keep[2 * R :] = gram
            send[2 * R :] = gram


def raw_coords(core, image, layer_inputs, out_grads, mask, starts=None):
    first = image is None
    steps = 8
    rows, d_in = layer_inputs.shape
    d_out = out_grads.shape[1]
    w_in, w_out = d_in // steps, d_out // steps
    if first:
        lead = list(starts)
        lead_specs = [
            pl.BlockSpec((R, w_in), lambda h, c: (0, h)),
            pl.BlockSpec((R, w_out), lambda h, c: (0, h)),
        ]
    else:
        lead = [image]
        lead_specs = [pl.BlockSpec((GROUPS, 1, ROWS, w_in + w_out), lambda h, c: (0, h, 0, 0))]
    height = 2 * R if first else 2 * R + R // 2
    shape = jax.ShapeDtypeStruct((height, rows // 2), F32)
    whole = pl.BlockSpec((height, rows // 2), lambda h, c: (0, 0))
    scratch = [pltpu.VMEM((2 * R, rows), F32)]
    if not first:
        scratch += [pltpu.VMEM((R, R), F32)] * 2
    return pl.pallas_call(
        functools.partial(raw_kernel, first, steps),
        out_shape=(shape, shape),
        grid_spec=pltpu.PrefetchScalarGridSpec(
            num_scalar_prefetch=1,
            grid=(steps,),
            in_specs=lead_specs
            + [
                pl.BlockSpec((rows, w_in), lambda h, c: (0, h)),
                pl.BlockSpec((rows, w_out), lambda h, c: (0, h)),
                pl.BlockSpec((1, rows), lambda h, c: (0, 0)),
            ],
            out_specs=(whole, whole),
            scratch_shapes=scratch,
        ),
        name="raw_first" if first else "raw_next",
    )(core, *lead, layer_inputs, out_grads, mask)


def image_kernel(core, mine_ref, other_ref, min_ref, mout_ref, out, coords):
    tokens = mine_ref.shape[1]

    @pl.when(pl.program_id(0) == 0)
    def _():
        coords[:, pl.ds(pl.multiple_of(core[0] * tokens, tokens), tokens)] = mine_ref[...]
        coords[:, pl.ds(pl.multiple_of((1 - core[0]) * tokens, tokens), tokens)] = other_ref[...]

    wide = min_ref.shape[1]
    part_in = jnp.dot(coords[:R], min_ref[...], preferred_element_type=F32).astype(BF16)
    part_out = jnp.dot(coords[R:], mout_ref[...], preferred_element_type=F32).astype(BF16)
    for g in range(GROUPS):
        out[g, 0, :, :wide] = part_in[g * ROWS : (g + 1) * ROWS]
        out[g, 0, :, wide:] = part_out[g * ROWS : (g + 1) * ROWS]


def image_of(core, mine, other, layer_inputs, out_grads):
    steps = 8
    rows, d_in = layer_inputs.shape
    d_out = out_grads.shape[1]
    w_in, w_out = d_in // steps, d_out // steps
    whole = pl.BlockSpec((2 * R, rows // 2), lambda h, c: (0, 0))
    return pl.pallas_call(
        image_kernel,
        out_shape=jax.ShapeDtypeStruct((GROUPS, steps, ROWS, w_in + w_out), BF16),
        grid_spec=pltpu.PrefetchScalarGridSpec(
            num_scalar_prefetch=1,
            grid=(steps,),
            in_specs=[
                whole,
                whole,
                pl.BlockSpec((rows, w_in), lambda h, c: (0, h)),
                pl.BlockSpec((rows, w_out), lambda h, c: (0, h)),
            ],
            out_specs=pl.BlockSpec((GROUPS, 1, ROWS, w_in + w_out), lambda h, c: (0, h, 0, 0)),
            scratch_shapes=[pltpu.VMEM((2 * R, rows), BF16)],
        ),
        name="image",
    )(core, mine, other, layer_inputs, out_grads)


def sum_kernel(parts, out):
    total = parts[0].astype(F32)
    for i in range(1, parts.shape[0]):
        total = total + parts[i].astype(F32)
    half = total.astype(BF16)
    for i in range(parts.shape[0]):
        out[i] = half


def sum_copies(parts):
    return pl.pallas_call(
        sum_kernel,
        out_shape=jax.ShapeDtypeStruct(parts.shape, parts.dtype),
        name="sum_copies",
    )(parts)


def solve_kernel(last, near, far, *refs):
    total = near[...] + far[...]
    gram = total[2 * R :]
    half = gram.shape[1] // 2
    gram = jnp.concatenate([gram[:, :half], gram[:, half:]], axis=0)
    inv_in = eliminate(gram[:, :R])
    inv_out = eliminate(gram[:, R:])
    high = lax.Precision.HIGHEST
    co_in = jnp.dot(inv_in, total[:R], precision=high, preferred_element_type=F32)
    co_out = jnp.dot(inv_out, total[R : 2 * R], precision=high, preferred_element_type=F32)
    if last:
        feat, split = refs
        feat[...] = lax.dot_general(
            co_in.astype(BF16), co_out.astype(BF16), NT, preferred_element_type=F32
        ) * (1.0 / LEN)
        split[0] = split3(inv_in)
        split[1] = split3(inv_out)
    else:
        (coords,) = refs
        coords[:R] = co_in.astype(BF16)
        coords[R:] = co_out.astype(BF16)


def solve(near, far, last):
    if last:
        shape = (
            jax.ShapeDtypeStruct((R, R), F32),
            jax.ShapeDtypeStruct((2, R, 3 * R), BF16),
        )
    else:
        shape = jax.ShapeDtypeStruct((2 * R, near.shape[1]), BF16)
    return pl.pallas_call(
        functools.partial(solve_kernel, last),
        out_shape=shape,
        name="solve_last" if last else "solve",
    )(near, far)


def basis_kernel(split, img_ref, in_ref, out_ref):
    wide = in_ref.shape[1]
    img = jnp.concatenate([img_ref[g, 0] for g in range(GROUPS)] * 3, axis=0)
    in_ref[...] = jnp.dot(split[0], img[:, :wide], preferred_element_type=F32)
    out_ref[...] = jnp.dot(split[1], img[:, wide:], preferred_element_type=F32)


def basis_of(split, image, d_in, d_out):
    steps = image.shape[1]
    w_in, w_out = d_in // steps, d_out // steps
    return pl.pallas_call(
        basis_kernel,
        out_shape=(jax.ShapeDtypeStruct((R, d_in), F32), jax.ShapeDtypeStruct((R, d_out), F32)),
        grid=(steps,),
        in_specs=[
            pl.BlockSpec(split.shape, lambda h: (0, 0, 0)),
            pl.BlockSpec((GROUPS, 1, ROWS, w_in + w_out), lambda h: (0, h, 0, 0)),
        ],
        out_specs=(
            pl.BlockSpec((R, w_in), lambda h: (0, h)),
            pl.BlockSpec((R, w_out), lambda h: (0, h)),
        ),
        name="basis",
    )(split, image)


CORE_SWAP = [(0, 1), (1, 0), (2, 3), (3, 2)]
CHIP_SWAP = [(0, 2), (2, 0), (1, 3), (3, 1)]


def shards(layer_inputs, out_grads, loss_mask, start_in, start_out):
    mp = lax.axis_index("mp")
    core = (mp % 2).reshape(1)
    mask = loss_mask.reshape(1, -1)

    def exchange(send, keep):
        near = keep + lax.ppermute(send, "mp", CORE_SWAP)
        return near, lax.ppermute(near, "mp", CHIP_SWAP)

    send, keep = raw_coords(core, None, layer_inputs, out_grads, mask, (start_in, start_out))
    near, far = exchange(send, keep)
    mine = (near + far).astype(BF16)
    for step in range(ITERS):
        other = lax.ppermute(mine, "mp", CORE_SWAP)
        parts = image_of(core, mine, other, layer_inputs, out_grads)
        grid = parts.shape
        parts = parts.reshape(grid[0] * grid[1], grid[2], grid[3])
        parts = lax.all_to_all(parts, "dp", 0, 0)
        image = lax.all_to_all(sum_copies(parts), "dp", 0, 0).reshape(grid)
        send, keep = raw_coords(core, image, layer_inputs, out_grads, mask)
        near, far = exchange(send, keep)
        if step + 1 < ITERS:
            mine = solve(near, far, False)
    feat, split = solve(near, far, True)
    basis_in, basis_out = basis_of(split, image, layer_inputs.shape[1], out_grads.shape[1])
    block = R // lax.axis_size("mp")
    own = lax.dynamic_slice_in_dim(feat, mp * block, block, 0)
    theirs = lax.dynamic_slice_in_dim(feat, (mp + 1 - 2 * (mp % 2)) * block, block, 0)
    got = lax.ppermute(theirs, "mp", CORE_SWAP)
    own, got = own.reshape(1, -1), got.reshape(1, -1)
    even = mp % 2 == 0
    features = jnp.concatenate([jnp.where(even, own, got), jnp.where(even, got, own)], axis=0)
    return (features, basis_in, basis_out)


def solution(mesh):
    in_specs = (P("dp", "mp"), P("dp", "mp"), P("dp"), P(None, "mp"), P(None, "mp"))
    out_specs = (P("dp", "mp"), P(None, "mp"), P(None, "mp"))
    return jax.shard_map(shards, mesh=mesh, in_specs=in_specs, out_specs=out_specs, check_vma=False)
```

time: 1490 us -> 209 us (0.14)
  waiting for transfers between devices: 989 us -> 17.6 us
  blocking collectives: 376 us -> 93 us
  Pallas kernels: 0 us -> 69.1 us
  matrix products: 51.1 us -> 0 us
  other arithmetic: 48.3 us -> 4.13 us
  starting transfers between devices: 0.21 us -> 19.5 us
    psum x2 -> x0, waiting for transfers between devices: 567 us -> none  [shards(): in_whole = lax.psum(in_image, 'dp')]
    unnamed x7 -> x0, waiting for transfers between devices: 308 us -> none
    psum x7 -> x0, blocking collectives: 306 us -> none  [the longest x2 173 us: shards(): gram_out = lax.psum(gram_of(out_owned), ('dp', 'mp'))]
    all_gather x1 -> x0, waiting for transfers between devices: 115 us -> none  [shards(): basis_out = lax.all_gather(new_out, 'dp', axis=1, tiled=True)]
    all_to_all x0 -> x4, blocking collectives: none -> 93 us  [the longest x2 49.8 us: shards(): parts = lax.all_to_all(parts, 'dp', 0, 0)]
    all_gather x1 -> x0, blocking collectives: 69.9 us -> none  [shards(): lax.all_gather(new_out.astype(jnp.bfloat16), 'dp', axis=1, tiled=True)]
    pallas_call x0 -> x10, Pallas kernels: none -> 69.1 us  [the longest x3 27.1 us: raw_coords(): pl.pallas_call(functools.partial(raw_kernel, first, steps), out_shape=(sh...]
    another operation x20 -> x0, other arithmetic: 48.3 us -> none  [the longest x12 26.1 us: normalize(): lower = jnp.linalg.cholesky(gram)]
  transfers between devices with their start and end apart: 5 -> 9, of which waited for: 5 -> 8; matrix products, arithmetic and copies ran while one was open for 2% -> 0% of each run, Pallas kernels for 0% -> 3%
where the time goes in v1:
time: 209 us; the launch traced here: 208 us
  blocking collectives  93 us (44%)
  Pallas kernels  69.1 us (33%)
  starting transfers between devices  19.5 us (9%)
  waiting for transfers between devices  17.6 us (8%)
  other arithmetic  4.13 us (2%)
  local copies, waits for them, and re-layouts  3.46 us (2%)
    all_to_all x2, blocking collectives, shards(): parts = lax.all_to_all(parts, 'dp', 0, 0)  49.8 us
    all_to_all x2, blocking collectives, shards(): image = lax.all_to_all(sum_copies(parts), 'dp', 0, 0).reshape(grid)  43.2 us
    pallas_call x3, Pallas kernels, raw_coords(): pl.pallas_call(functools.partial(raw_kernel, first, steps), out_shape=(sh...  27.1 us
    pallas_call x2, Pallas kernels, image_of(): pl.pallas_call(image_kernel, out_shape=jax.ShapeDtypeStruct((GROUPS, step...  16.2 us
    pallas_call x2, Pallas kernels, solve(): pl.pallas_call(functools.partial(solve_kernel, last), out_shape=shape, na...  14.8 us
    ppermute x3, waiting for transfers between devices, exchange(): return (near, lax.ppermute(near, 'mp', CHIP_SWAP))  11.9 us
    ppermute x3, starting transfers between devices, exchange(): return (near, lax.ppermute(near, 'mp', CHIP_SWAP))  8.49 us
    ppermute x3, starting transfers between devices, exchange(): near = keep + lax.ppermute(send, 'mp', CORE_SWAP)  7.38 us
  transfers between devices with their start and end apart: 9, of which 8 were waited for; matrix products, arithmetic and copies ran while one was open for 0% of the time, Pallas kernels for 3%

profile of v1, /device:TPU:1, one launch (start us, length us, event | category | flops | bytes accessed | tf_op | source)
XLA Modules:
  0.0 207.5 jit_solution(10629897870441522239)
XLA Ops:
  0.6 9.1 %raw_first.1 = (f32[128,256]{1,0:T(8,128)}, f32[128,256]{1,0:T(8,128)}) custom-call(s32[1]{0:T(128)} %bitcast.core, s32[64,2048]{1,0:T(8,128)} %refs_0_.1, s32[64,7168]{1,0:T(8,128)} %refs_1_.3, bf16[512,2048]{1,0:T(8,128)(2,1)} %refs_1_.5, bf16[512,7168]{1,0:T(8,128)(2,1)} %refs_2_.5, s32[1,512]{1,0:T(1,128)} %bitcast.11), custom_call_target="tpu_custom_call" | custom-call | tf_op jit(solution)/shard_map/raw_first/pallas_call | solution.py:116
  9.7 1.4 collective-permute-start
  13.2 3.1 %collective-permute-start.1 = (f32[128,256]{1,0:T(8,128)S(1)}, f32[128,256]{1,0:T(8,128)S(1)}, u32[]{:S(2)}, u32[]{:S(2)}) collective-permute-start(f32[128,256]{1,0:T(8,128)S(1)} %add.28), channel_id=1, source_target_pairs={{0,2},{2,0},{1,3},{3,1},{4,6},{6,4},{5,7},{7,5},{8,10},{10,8},{9,1... | collective-permute-start | bytes 393224 | tf_op jit(solution)/shard_map/ppermute | solution.py:268
  16.3 3.3 %collective-permute-done.1 = f32[128,256]{1,0:T(8,128)S(1)} collective-permute-done((f32[128,256]{1,0:T(8,128)S(1)}, f32[128,256]{1,0:T(8,128)S(1)}, u32[]{:S(2)}, u32[]{:S(2)}) %collective-permute-start.1) | collective-permute-done | bytes 131104 | tf_op jit(solution)/shard_map/ppermute | solution.py:268
  22.4 8.1 %image.2 = bf16[4,8,16,1152]{3,2,1,0:T(8,128)(2,1)} custom-call(s32[1]{0:T(128)} %bitcast.core, bf16[128,256]{1,0:T(8,128)(2,1)} %copy-done.2, bf16[128,256]{1,0:T(8,128)(2,1)} %copy-done.5, bf16[512,2048]{1,0:T(8,128)(2,1)} %refs_1_.5, bf16[512,7168]{1,0:T(8,128)(2,1)} %refs_2_.5), custom_call_target="tpu_custom_call" | custom-call | tf_op jit(solution)/shard_map/image/pallas_call | solution.py:157
  30.5 27.0 %all_to_all.20.parts = bf16[32,16,1152]{2,1,0:T(8,128)(2,1)} all-to-all(bf16[32,16,1152]{2,1,0:T(8,128)(2,1)} %bitcast.9), channel_id=1, replica_groups=mesh['dp'=32,'mp'=4] {'dp'}, dimensions={0} | all-to-all | bytes 2359296 | tf_op jit(solution)/shard_map/all_to_all | solution.py:278
  57.5 2.5 %sum_copies.2 = bf16[32,16,1152]{2,1,0:T(8,128)(2,1)} custom-call(bf16[32,16,1152]{2,1,0:T(8,128)(2,1)} %all_to_all.20.parts), custom_call_target="tpu_custom_call" | custom-call | tf_op jit(solution)/shard_map/sum_copies/pallas_call | solution.py:186
  60.0 21.5 %all_to_all.21 = bf16[32,16,1152]{2,1,0:T(8,128)(2,1)} all-to-all(bf16[32,16,1152]{2,1,0:T(8,128)(2,1)} %sum_copies.2), channel_id=1, replica_groups=mesh['dp'=32,'mp'=4] {'dp'}, dimensions={0} | all-to-all | bytes 2359296 | tf_op jit(solution)/shard_map/all_to_all | solution.py:279
  81.5 9.0 %raw_next.2 = (f32[160,256]{1,0:T(8,128)}, f32[160,256]{1,0:T(8,128)}) custom-call(s32[1]{0:T(128)} %bitcast.core, bf16[4,8,16,1152]{3,2,1,0:T(8,128)(2,1)} %bitcast.8, bf16[512,2048]{1,0:T(8,128)(2,1)} %refs_1_.5, bf16[512,7168]{1,0:T(8,128)(2,1)} %refs_2_.5, s32[1,512]{1,0:T(1,128)} %bitcast.12), custom_call_target="tpu_custom_call" | custom-call | tf_op jit(solution)/shard_map/raw_next/pallas_call | solution.py:116
  90.5 3.1 %collective-permute-start.3 = (f32[160,256]{1,0:T(8,128)}, f32[160,256]{1,0:T(8,128)S(1)}, u32[]{:S(2)}, u32[]{:S(2)}) collective-permute-start(f32[160,256]{1,0:T(8,128)} %get-tuple-element.16), channel_id=1, source_target_pairs={{0,1},{1,0},{2,3},{3,2},{4,5},{5,4},{6,7},{7,6},{8,9},{9,8},{10,11... | collective-permute-start | bytes 491528 | tf_op jit(solution)/shard_map/ppermute | solution.py:267
  93.6 1.2 collective-permute-done.3
  95.8 2.7 %collective-permute-start.4 = (f32[160,256]{1,0:T(8,128)S(1)}, f32[160,256]{1,0:T(8,128)S(1)}, u32[]{:S(2)}, u32[]{:S(2)}) collective-permute-start(f32[160,256]{1,0:T(8,128)S(1)} %add.30.near), channel_id=1, source_target_pairs={{0,2},{2,0},{1,3},{3,1},{4,6},{6,4},{5,7},{7,5},{8,10},{10,8},{9,1... | collective-permute-start | bytes 491528 | tf_op jit(solution)/shard_map/ppermute | solution.py:268
  98.5 4.3 %collective-permute-done.4.far = f32[160,256]{1,0:T(8,128)S(1)} collective-permute-done((f32[160,256]{1,0:T(8,128)S(1)}, f32[160,256]{1,0:T(8,128)S(1)}, u32[]{:S(2)}, u32[]{:S(2)}) %collective-permute-start.4) | collective-permute-done | bytes 163872 | tf_op jit(solution)/shard_map/ppermute | solution.py:268
  103.4 7.3 %solve.1.mine_ref = bf16[128,256]{1,0:T(8,128)(2,1)} custom-call(f32[160,256]{1,0:T(8,128)} %copy-done.1, f32[160,256]{1,0:T(8,128)} %copy-done.4), custom_call_target="tpu_custom_call" | custom-call | tf_op jit(solution)/shard_map/solve/pallas_call | solution.py:224
  113.7 8.1 %image.3 = bf16[4,8,16,1152]{3,2,1,0:T(8,128)(2,1)} custom-call(s32[1]{0:T(128)} %bitcast.core, bf16[128,256]{1,0:T(8,128)(2,1)} %solve.1.mine_ref, bf16[128,256]{1,0:T(8,128)(2,1)} %copy-done.6, bf16[512,2048]{1,0:T(8,128)(2,1)} %refs_1_.5, bf16[512,7168]{1,0:T(8,128)(2,1)} %refs_2_.5), custom_call_target="tpu_custom_call" | custom-call | tf_op jit(solution)/shard_map/image/pallas_call | solution.py:157
  121.8 22.8 %all_to_all.22.parts = bf16[32,16,1152]{2,1,0:T(8,128)(2,1)} all-to-all(bf16[32,16,1152]{2,1,0:T(8,128)(2,1)} %bitcast.10), channel_id=1, replica_groups=mesh['dp'=32,'mp'=4] {'dp'}, dimensions={0} | all-to-all | bytes 2359296 | tf_op jit(solution)/shard_map/all_to_all | solution.py:278
  144.7 2.5 %sum_copies.3 = bf16[32,16,1152]{2,1,0:T(8,128)(2,1)} custom-call(bf16[32,16,1152]{2,1,0:T(8,128)(2,1)} %all_to_all.22.parts), custom_call_target="tpu_custom_call" | custom-call | tf_op jit(solution)/shard_map/sum_copies/pallas_call | solution.py:186
  147.1 21.7 %all_to_all.23 = bf16[32,16,1152]{2,1,0:T(8,128)(2,1)} all-to-all(bf16[32,16,1152]{2,1,0:T(8,128)(2,1)} %sum_copies.3), channel_id=1, replica_groups=mesh['dp'=32,'mp'=4] {'dp'}, dimensions={0} | all-to-all | bytes 2359296 | tf_op jit(solution)/shard_map/all_to_all | solution.py:279
  168.8 9.0 %raw_next.3 = (f32[160,256]{1,0:T(8,128)}, f32[160,256]{1,0:T(8,128)}) custom-call(s32[1]{0:T(128)} %bitcast.core, bf16[4,8,16,1152]{3,2,1,0:T(8,128)(2,1)} %bitcast.6, bf16[512,2048]{1,0:T(8,128)(2,1)} %refs_1_.5, bf16[512,7168]{1,0:T(8,128)(2,1)} %refs_2_.5, s32[1,512]{1,0:T(1,128)} %bitcast.13), custom_call_target="tpu_custom_call" | custom-call | tf_op jit(solution)/shard_map/raw_next/pallas_call | solution.py:116
  177.8 2.9 %collective-permute-start.6 = (f32[160,256]{1,0:T(8,128)}, f32[160,256]{1,0:T(8,128)S(1)}, u32[]{:S(2)}, u32[]{:S(2)}) collective-permute-start(f32[160,256]{1,0:T(8,128)} %get-tuple-element.18), channel_id=1, source_target_pairs={{0,1},{1,0},{2,3},{3,2},{4,5},{5,4},{6,7},{7,6},{8,9},{9,8},{10,11... | collective-permute-start | bytes 491528 | tf_op jit(solution)/shard_map/ppermute | solution.py:267
  182.9 2.7 %collective-permute-start.7 = (f32[160,256]{1,0:T(8,128)S(1)}, f32[160,256]{1,0:T(8,128)S(1)}, u32[]{:S(2)}, u32[]{:S(2)}) collective-permute-start(f32[160,256]{1,0:T(8,128)S(1)} %add.31.near), channel_id=1, source_target_pairs={{0,2},{2,0},{1,3},{3,1},{4,6},{6,4},{5,7},{7,5},{8,10},{10,8},{9,1... | collective-permute-start | bytes 491528 | tf_op jit(solution)/shard_map/ppermute | solution.py:268
  185.6 4.3 %collective-permute-done.7.far = f32[160,256]{1,0:T(8,128)S(1)} collective-permute-done((f32[160,256]{1,0:T(8,128)S(1)}, f32[160,256]{1,0:T(8,128)S(1)}, u32[]{:S(2)}, u32[]{:S(2)}) %collective-permute-start.7) | collective-permute-done | bytes 163872 | tf_op jit(solution)/shard_map/ppermute | solution.py:268
  190.6 7.4 %solve_last.1 = (f32[64,64]{1,0:T(8,128)}, bf16[2,64,192]{2,1,0:T(8,128)(2,1)}) custom-call(f32[160,256]{1,0:T(8,128)} %copy-done, f32[160,256]{1,0:T(8,128)} %copy-done.3), custom_call_target="tpu_custom_call" | custom-call | tf_op jit(solution)/shard_map/solve_last/pallas_call | solution.py:224
  199.9 6.1 %basis.1 = (f32[64,2048]{1,0:T(8,128)}, f32[64,7168]{1,0:T(8,128)}) custom-call(bf16[2,64,192]{2,1,0:T(8,128)(2,1)} %get-tuple-element.20.split, bf16[4,8,16,1152]{3,2,1,0:T(8,128)(2,1)} %bitcast.7), custom_call_target="tpu_custom_call" | custom-call | tf_op jit(solution)/shard_map/basis/pallas_call | solution.py:241
  (31 shorter events, 15.7 us)
Async XLA Ops:
  9.7 2.6 %collective-permute-start = (f32[128,256]{1,0:T(8,128)}, f32[128,256]{1,0:T(8,128)S(1)}, u32[]{:S(2)}, u32[]{:S(2)}) collective-permute-start(f32[128,256]{1,0:T(8,128)} %get-tuple-element.14), channel_id=1, source_target_pairs={{0,1},{1,0},{2,3},{3,2},{4,5},{5,4},{6,7},{7,6},{8,9},{9,8},{10,11... | collective-permute-start | bytes 393224 | tf_op jit(solution)/shard_map/ppermute | solution.py:267
  13.2 6.4 %collective-permute-start.1 = (f32[128,256]{1,0:T(8,128)S(1)}, f32[128,256]{1,0:T(8,128)S(1)}, u32[]{:S(2)}, u32[]{:S(2)}) collective-permute-start(f32[128,256]{1,0:T(8,128)S(1)} %add.28), channel_id=1, source_target_pairs={{0,2},{2,0},{1,3},{3,1},{4,6},{6,4},{5,7},{7,5},{8,10},{10,8},{9,1... | collective-permute-start | bytes 393224 | tf_op jit(solution)/shard_map/ppermute | solution.py:268
  19.6 2.2 %copy-start.2 = (bf16[128,256]{1,0:T(8,128)(2,1)}, bf16[128,256]{1,0:T(8,128)(2,1)S(1)}, u32[]{:S(2)}) copy-start(bf16[128,256]{1,0:T(8,128)(2,1)S(1)} %add_convert_fusion.mine_ref) | copy-start | bytes 196612
  19.6 2.1 %collective-permute-start.2 = (bf16[128,256]{1,0:T(8,128)(2,1)S(1)}, bf16[128,256]{1,0:T(8,128)(2,1)S(1)}, u32[]{:S(2)}, u32[]{:S(2)}) collective-permute-start(bf16[128,256]{1,0:T(8,128)(2,1)S(1)} %add_convert_fusion.mine_ref), channel_id=1, source_target_pairs={{0,1},{1,0},{2,3},{3,2},{4,5},{5,4},{6,7},{7,6},{8,9},{9,8},{10,11... | collective-permute-start | bytes 196616 | tf_op jit(solution)/shard_map/ppermute | solution.py:274
  21.8 0.6 copy-start.5
  90.5 4.3 %collective-permute-start.3 = (f32[160,256]{1,0:T(8,128)}, f32[160,256]{1,0:T(8,128)S(1)}, u32[]{:S(2)}, u32[]{:S(2)}) collective-permute-start(f32[160,256]{1,0:T(8,128)} %get-tuple-element.16), channel_id=1, source_target_pairs={{0,1},{1,0},{2,3},{3,2},{4,5},{5,4},{6,7},{7,6},{8,9},{9,8},{10,11... | collective-permute-start | bytes 491528 | tf_op jit(solution)/shard_map/ppermute | solution.py:267
  95.8 7.0 %copy-start.1 = (f32[160,256]{1,0:T(8,128)}, f32[160,256]{1,0:T(8,128)S(1)}, u32[]{:S(2)}) copy-start(f32[160,256]{1,0:T(8,128)S(1)} %add.30.near) | copy-start | bytes 491524
  95.8 7.0 %collective-permute-start.4 = (f32[160,256]{1,0:T(8,128)S(1)}, f32[160,256]{1,0:T(8,128)S(1)}, u32[]{:S(2)}, u32[]{:S(2)}) collective-permute-start(f32[160,256]{1,0:T(8,128)S(1)} %add.30.near), channel_id=1, source_target_pairs={{0,2},{2,0},{1,3},{3,1},{4,6},{6,4},{5,7},{7,5},{8,10},{10,8},{9,1... | collective-permute-start | bytes 491528 | tf_op jit(solution)/shard_map/ppermute | solution.py:268
  102.8 0.7 copy-start.4
  110.8 2.3 %collective-permute-start.5 = (bf16[128,256]{1,0:T(8,128)(2,1)}, bf16[128,256]{1,0:T(8,128)(2,1)S(1)}, u32[]{:S(2)}, u32[]{:S(2)}) collective-permute-start(bf16[128,256]{1,0:T(8,128)(2,1)} %solve.1.mine_ref), channel_id=1, source_target_pairs={{0,1},{1,0},{2,3},{3,2},{4,5},{5,4},{6,7},{7,6},{8,9},{9,8},{10,11... | collective-permute-start | bytes 196616 | tf_op jit(solution)/shard_map/ppermute | solution.py:274
  113.1 0.6 copy-start.6
  177.8 4.1 %collective-permute-start.6 = (f32[160,256]{1,0:T(8,128)}, f32[160,256]{1,0:T(8,128)S(1)}, u32[]{:S(2)}, u32[]{:S(2)}) collective-permute-start(f32[160,256]{1,0:T(8,128)} %get-tuple-element.18), channel_id=1, source_target_pairs={{0,1},{1,0},{2,3},{3,2},{4,5},{5,4},{6,7},{7,6},{8,9},{9,8},{10,11... | collective-permute-start | bytes 491528 | tf_op jit(solution)/shard_map/ppermute | solution.py:267
  182.9 7.0 %copy-start = (f32[160,256]{1,0:T(8,128)}, f32[160,256]{1,0:T(8,128)S(1)}, u32[]{:S(2)}) copy-start(f32[160,256]{1,0:T(8,128)S(1)} %add.31.near) | copy-start | bytes 491524
  182.9 7.0 %collective-permute-start.7 = (f32[160,256]{1,0:T(8,128)S(1)}, f32[160,256]{1,0:T(8,128)S(1)}, u32[]{:S(2)}, u32[]{:S(2)}) collective-permute-start(f32[160,256]{1,0:T(8,128)S(1)} %add.31.near), channel_id=1, source_target_pairs={{0,2},{2,0},{1,3},{3,1},{4,6},{6,4},{5,7},{7,5},{8,10},{10,8},{9,1... | collective-permute-start | bytes 491528 | tf_op jit(solution)/shard_map/ppermute | solution.py:268
  189.9 0.7 copy-start.3
  198.7 7.3 %collective-permute-start.8 = (f32[16,64]{1,0:T(8,128)S(1)}, f32[16,64]{1,0:T(8,128)S(1)}, u32[]{:S(2)}, u32[]{:S(2)}) collective-permute-start(f32[16,64]{1,0:T(8,128)S(1)} %constant_dynamic-slice_fusion), channel_id=1, source_target_pairs={{0,1},{1,0},{2,3},{3,2},{4,5},{5,4},{6,7},{7,6},{8,9},{9,8},{10,11... | collective-permute-start | bytes 12296 | tf_op jit(solution)/shard_map/ppermute | solution.py:289

commit v2 on v1

v2 whole, which is shorter than its diff:
```python
import functools

import jax
import jax.numpy as jnp
from jax import lax
from jax.experimental import pallas as pl
from jax.experimental.pallas import tpu as pltpu
from jax.sharding import PartitionSpec as P

ITERS = 2
LEN = 256
R = 64
ROWS = 16
GROUPS = R // ROWS
NT = (((1,), (1,)), ((), ()))
F32 = jnp.float32
BF16 = jnp.bfloat16


def split3(x):
    a = x.astype(BF16)
    rest = x - a.astype(F32)
    b = rest.astype(BF16)
    c = (rest - b.astype(F32)).astype(BF16)
    return jnp.concatenate([a, b, c], axis=1)


def eliminate(gram):
    n = gram.shape[0]
    col_id = lax.broadcasted_iota(jnp.int32, (n, n), 1)
    row_id = lax.broadcasted_iota(jnp.int32, (n, n), 0)
    eye = (col_id == row_id).astype(F32)
    work = jnp.concatenate([gram, eye], axis=1)
    tiles = [work[8 * i : 8 * i + 8] for i in range(n // 8)]
    sub = lax.broadcasted_iota(jnp.int32, (8, 1), 0)
    for k in range(n - 1):
        t, r = divmod(k, 8)
        row = tiles[t][r : r + 1]
        scaled = row * (1.0 / row[:, k : k + 1])
        for i in range(t, n // 8):
            col = tiles[i][:, k : k + 1]
            if i == t:
                if r == 7:
                    continue
                col = jnp.where(sub > r, col, 0.0)
            tiles[i] = tiles[i] - col * scaled
    work = jnp.concatenate(tiles, axis=0)
    diag = jnp.sum(jnp.where(col_id == row_id, work[:, :n], 0.0), axis=1, keepdims=True)
    return work[:, n:] * (1.0 / jnp.sqrt(diag))


def params(mib):
    return pltpu.CompilerParams(vmem_limit_bytes=mib << 20)


VMEM = pl.BlockSpec(memory_space=pltpu.VMEM)
SMEM = pl.BlockSpec(memory_space=pltpu.SMEM)
HBM = pl.BlockSpec(memory_space=pltpu.HBM)


def halves(place, tokens):
    core = place[0] & 1
    mine = pl.ds(pl.multiple_of(core * tokens, tokens), tokens)
    other = pl.ds(pl.multiple_of((1 - core) * tokens, tokens), tokens)
    return mine, other


def first_kernel(place, bin_hbm, bout_hbm, min_hbm, mout_hbm, mask_hbm, *refs):
    send, keep, mins, mouts, mask, bins, bouts, ints, acc, sems, mask_sem = refs
    steps = sems.shape[0]
    pairs = ((bin_hbm, bins), (min_hbm, mins), (bout_hbm, bouts), (mout_hbm, mouts))

    def columns(ref, h):
        width = ref.shape[1] // steps
        return slice(h * width, (h + 1) * width)

    copies = []
    for h in range(steps):
        for n, (src, dst) in enumerate(pairs):
            cols = columns(dst, h)
            copy = pltpu.make_async_copy(src.at[:, cols], dst.at[:, cols], sems.at[h, n])
            copy.start()
            copies.append(copy)
    mask_copy = pltpu.make_async_copy(mask_hbm, ints, mask_sem)
    mask_copy.start()
    for h in range(steps):
        for n, (base, basis, data) in enumerate([(0, bins, mins), (R, bouts, mouts)]):
            copies[4 * h + 2 * n].wait()
            copies[4 * h + 2 * n + 1].wait()
            cols = columns(basis, h)
            half = (basis[:, cols].astype(F32) * (1.0 / 128.0)).astype(BF16)
            part = lax.dot_general(half, data[:, cols], NT, preferred_element_type=F32)
            if h == 0:
                acc[base : base + R] = part
            else:
                acc[base : base + R] += part
    mask_copy.wait()
    mask[...] = ints[...].astype(F32)
    acc[R:] = acc[R:] * mask[...]
    mine, other = halves(place, acc.shape[1] // 2)
    keep[...] = acc[:, mine]
    send[...] = acc[:, other]


def raw_first(place, *whole):
    start_in, start_out, layer_inputs, out_grads, mask = whole
    rows = layer_inputs.shape[0]
    shape = jax.ShapeDtypeStruct((2 * R, rows // 2), F32)
    return pl.pallas_call(
        first_kernel,
        out_shape=(
            shape,
            shape,
            jax.ShapeDtypeStruct(layer_inputs.shape, BF16),
            jax.ShapeDtypeStruct(out_grads.shape, BF16),
            jax.ShapeDtypeStruct(mask.shape, F32),
        ),
        in_specs=[SMEM, HBM, HBM, HBM, HBM, HBM],
        out_specs=(VMEM,) * 5,
        scratch_shapes=[
            pltpu.VMEM(start_in.shape, jnp.int32),
            pltpu.VMEM(start_out.shape, jnp.int32),
            pltpu.VMEM(mask.shape, jnp.int32),
            pltpu.VMEM((2 * R, rows), F32),
            pltpu.SemaphoreType.DMA((8, 4)),
            pltpu.SemaphoreType.DMA,
        ],
        compiler_params=params(8),
        name="raw_first",
    )(place, *(pltpu.with_memory_space_constraint(x, pltpu.HBM) for x in whole))


def next_kernel(place, img_ref, min_ref, mout_ref, mask_ref, send, keep, img_in, img_out, acc):
    steps = img_ref.shape[1]
    w_in = img_in.shape[1] // steps
    w_out = img_out.shape[1] // steps
    for h in range(steps):
        for g in range(GROUPS):
            rows = slice(g * ROWS, (g + 1) * ROWS)
            img_in[rows, h * w_in : (h + 1) * w_in] = img_ref[g, h, :, :w_in]
            img_out[rows, h * w_out : (h + 1) * w_out] = img_ref[g, h, :, w_in:]
    half_in, half_out = img_in[...], img_out[...]
    gram_in = lax.dot_general(half_in, half_in, NT, preferred_element_type=F32)
    gram_out = lax.dot_general(half_out, half_out, NT, preferred_element_type=F32)
    acc[:R] = lax.dot_general(half_in, min_ref[...], NT, preferred_element_type=F32)
    raw_out = lax.dot_general(half_out, mout_ref[...], NT, preferred_element_type=F32)
    acc[R:] = raw_out * mask_ref[...]
    mine, other = halves(place, acc.shape[1] // 2)
    keep[: 2 * R] = acc[:, mine]
    send[: 2 * R] = acc[:, other]
    gram = jnp.concatenate([gram_in, gram_out], axis=1)
    gram = jnp.concatenate([gram[: R // 2], gram[R // 2 :]], axis=1)
    keep[2 * R :] = gram
    send[2 * R :] = gram


def raw_next(place, image, layer_inputs, out_grads, mask):
    rows, d_in = layer_inputs.shape
    d_out = out_grads.shape[1]
    shape = jax.ShapeDtypeStruct((2 * R + R // 2, rows // 2), F32)
    return pl.pallas_call(
        next_kernel,
        out_shape=(shape, shape),
        in_specs=[SMEM, VMEM, VMEM, VMEM, VMEM],
        out_specs=(VMEM, VMEM),
        scratch_shapes=[
            pltpu.VMEM((R, d_in), BF16),
            pltpu.VMEM((R, d_out), BF16),
            pltpu.VMEM((2 * R, rows), F32),
        ],
        compiler_params=params(8),
        name="raw_next",
    )(place, image, layer_inputs, out_grads, mask)


def add_kernel(a, b, out):
    out[...] = (a[...] + b[...]).astype(out.dtype)


def add(a, b, dtype=F32):
    return pl.pallas_call(
        add_kernel,
        out_shape=jax.ShapeDtypeStruct(a.shape, dtype),
        in_specs=[VMEM, VMEM],
        out_specs=VMEM,
        compiler_params=params(4),
        name="add",
    )(a, b)


def image_kernel(place, mine_ref, other_ref, min_ref, mout_ref, out, coords):
    mine, other = halves(place, mine_ref.shape[1])
    coords[:, mine] = mine_ref[...]
    coords[:, other] = other_ref[...]
    steps = out.shape[1]
    w_in = min_ref.shape[1] // steps
    w_out = mout_ref.shape[1] // steps
    part_in = jnp.dot(coords[:R], min_ref[...], preferred_element_type=F32).astype(BF16)
    part_out = jnp.dot(coords[R:], mout_ref[...], preferred_element_type=F32).astype(BF16)
    for h in range(steps):
        for g in range(GROUPS):
            rows = slice(g * ROWS, (g + 1) * ROWS)
            out[g, h, :, :w_in] = part_in[rows, h * w_in : (h + 1) * w_in]
            out[g, h, :, w_in:] = part_out[rows, h * w_out : (h + 1) * w_out]


def image_of(place, mine, other, layer_inputs, out_grads):
    steps = 8
    rows, d_in = layer_inputs.shape
    width = (d_in + out_grads.shape[1]) // steps
    return pl.pallas_call(
        image_kernel,
        out_shape=jax.ShapeDtypeStruct((GROUPS, steps, ROWS, width), BF16),
        in_specs=[SMEM, VMEM, VMEM, VMEM, VMEM],
        out_specs=VMEM,
        scratch_shapes=[pltpu.VMEM((2 * R, rows), BF16)],
        compiler_params=params(8),
        name="image",
    )(place, mine, other, layer_inputs, out_grads)


def sum_kernel(parts, out):
    total = parts[0].astype(F32)
    for i in range(1, parts.shape[0]):
        total = total + parts[i].astype(F32)
    half = total.astype(BF16)
    for i in range(parts.shape[0]):
        out[i] = half


def sum_copies(parts):
    return pl.pallas_call(
        sum_kernel,
        out_shape=jax.ShapeDtypeStruct(parts.shape, parts.dtype),
        in_specs=[VMEM],
        out_specs=VMEM,
        compiler_params=params(4),
        name="sum_copies",
    )(parts)


def solve_kernel(last, place, near, far, *refs):
    total = near[...] + far[...]
    gram = total[2 * R :]
    half = gram.shape[1] // 2
    gram = jnp.concatenate([gram[:, :half], gram[:, half:]], axis=0)
    inv_in = eliminate(gram[:, :R])
    inv_out = eliminate(gram[:, R:])
    high = lax.Precision.HIGHEST
    co_in = jnp.dot(inv_in, total[:R], precision=high, preferred_element_type=F32)
    co_out = jnp.dot(inv_out, total[R : 2 * R], precision=high, preferred_element_type=F32)
    if last:
        own, theirs, split, feat = refs
        feat[...] = lax.dot_general(
            co_in.astype(BF16), co_out.astype(BF16), NT, preferred_element_type=F32
        ) * (1.0 / LEN)
        rows = own.shape[0]
        own[...] = feat[pl.ds(pl.multiple_of(place[0] * rows, rows), rows)]
        theirs[...] = feat[pl.ds(pl.multiple_of((place[0] ^ 1) * rows, rows), rows)]
        split[0] = split3(inv_in)
        split[1] = split3(inv_out)
    else:
        (coords,) = refs
        coords[:R] = co_in.astype(BF16)
        coords[R:] = co_out.astype(BF16)


def solve(place, near, far, count):
    last = count is not None
    if last:
        block = jax.ShapeDtypeStruct((R // count, R), F32)
        shape = (block, block, jax.ShapeDtypeStruct((2, R, 3 * R), BF16))
    else:
        shape = jax.ShapeDtypeStruct((2 * R, near.shape[1]), BF16)
    return pl.pallas_call(
        functools.partial(solve_kernel, last),
        out_shape=shape,
        in_specs=[SMEM, VMEM, VMEM],
        out_specs=(VMEM,) * 3 if last else VMEM,
        scratch_shapes=[pltpu.VMEM((R, R), F32)] if last else [],
        compiler_params=params(8),
        name="solve_last" if last else "solve",
    )(place, near, far)


def features_kernel(place, own, got, out):
    rows = own.shape[0]
    own = jnp.concatenate([own[r : r + 1] for r in range(rows)], axis=1)
    got = jnp.concatenate([got[r : r + 1] for r in range(rows)], axis=1)
    even = (place[0] & 1) == 0
    out[0:1] = jnp.where(even, own, got)
    out[1:2] = jnp.where(even, got, own)


def features_of(place, own, got):
    return pl.pallas_call(
        features_kernel,
        out_shape=jax.ShapeDtypeStruct((2, own.size), F32),
        in_specs=[SMEM, VMEM, VMEM],
        out_specs=VMEM,
        compiler_params=params(4),
        name="features",
    )(place, own, got)


def basis_kernel(split, img_ref, in_hbm, out_hbm, b_in, b_out, sems):
    steps = img_ref.shape[1]
    w_in = b_in.shape[1] // steps
    w_out = b_out.shape[1] // steps
    copies = []
    for h in range(steps):
        img = jnp.concatenate([img_ref[g, h] for g in range(GROUPS)] * 3, axis=0)
        cols_in = slice(h * w_in, (h + 1) * w_in)
        cols_out = slice(h * w_out, (h + 1) * w_out)
        b_in[:, cols_in] = jnp.dot(split[0], img[:, :w_in], preferred_element_type=F32)
        b_out[:, cols_out] = jnp.dot(split[1], img[:, w_in:], preferred_element_type=F32)
        for n, (src, dst, cols) in enumerate([(b_in, in_hbm, cols_in), (b_out, out_hbm, cols_out)]):
            copy = pltpu.make_async_copy(src.at[:, cols], dst.at[:, cols], sems.at[h, n])
            copy.start()
            copies.append(copy)
    for copy in copies:
        copy.wait()


def basis_of(split, image, d_in, d_out):
    shapes = ((R, d_in), (R, d_out))
    return pl.pallas_call(
        basis_kernel,
        out_shape=tuple(jax.ShapeDtypeStruct(s, F32) for s in shapes),
        in_specs=[VMEM, VMEM],
        out_specs=(HBM, HBM),
        scratch_shapes=[pltpu.VMEM(s, F32) for s in shapes]
        + [pltpu.SemaphoreType.DMA((image.shape[1], 2))],
        compiler_params=params(8),
        name="basis",
    )(split, image)


CORE_SWAP = [(0, 1), (1, 0), (2, 3), (3, 2)]
CHIP_SWAP = [(0, 2), (2, 0), (1, 3), (3, 1)]


def shards(layer_inputs, out_grads, loss_mask, start_in, start_out):
    place = lax.axis_index("mp").reshape(1)
    mask = loss_mask.reshape(1, -1)
    d_in, d_out = layer_inputs.shape[1], out_grads.shape[1]

    def exchange(send, keep):
        near = add(keep, lax.ppermute(send, "mp", CORE_SWAP))
        return near, lax.ppermute(near, "mp", CHIP_SWAP)

    send, keep, layer_inputs, out_grads, mask = raw_first(
        place, start_in, start_out, layer_inputs, out_grads, mask
    )
    near, far = exchange(send, keep)
    mine = add(near, far, BF16)
    for step in range(ITERS):
        other = lax.ppermute(mine, "mp", CORE_SWAP)
        parts = image_of(place, mine, other, layer_inputs, out_grads)
        grid = parts.shape
        parts = parts.reshape(grid[0] * grid[1], grid[2], grid[3])
        parts = lax.all_to_all(parts, "dp", 0, 0)
        image = lax.all_to_all(sum_copies(parts), "dp", 0, 0).reshape(grid)
        send, keep = raw_next(place, image, layer_inputs, out_grads, mask)
        near, far = exchange(send, keep)
        if step + 1 < ITERS:
            mine = solve(place, near, far, None)
    own, theirs, split = solve(place, near, far, lax.axis_size("mp"))
    got = lax.ppermute(theirs, "mp", CORE_SWAP)
    basis_in, basis_out = basis_of(split, image, d_in, d_out)
    return (features_of(place, own, got), basis_in, basis_out)


def solution(mesh):
    in_specs = (P("dp", "mp"), P("dp", "mp"), P("dp"), P(None, "mp"), P(None, "mp"))
    out_specs = (P("dp", "mp"), P(None, "mp"), P(None, "mp"))
    return jax.shard_map(shards, mesh=mesh, in_specs=in_specs, out_specs=out_specs, check_vma=False)
```

time: 209 us -> 157 us (0.75)
  Pallas kernels: 69.1 us -> 30 us
  other arithmetic: 4.13 us -> 0 us
  local copies, waits for them, and re-layouts: 3.46 us -> 0 us
  blocking collectives: 93 us -> 89.8 us
    pallas_call x6 -> x11, Pallas kernels: 48 us -> 26.2 us  [the longest x2 11.5 us: solve(): pl.pallas_call(functools.partial(solve_kernel, last), out_shape=shape, in...]
    pallas_call x2, Pallas kernels: 16.2 us -> 3.52 us  [image_of(): pl.pallas_call(image_kernel, out_shape=jax.ShapeDtypeStruct((GROUPS, step...]
    pallas_call x2, Pallas kernels: 4.94 us -> 0.37 us  [sum_copies(): pl.pallas_call(sum_kernel, out_shape=jax.ShapeDtypeStruct(parts.shape, pa...]
    add x3 -> x0, other arithmetic: 2.8 us -> none  [exchange(): near = keep + lax.ppermute(send, 'mp', CORE_SWAP)]
    unnamed x14 -> x0, local copies, waits for them, and re-layouts: 2.6 us -> none
  transfers between devices with their start and end apart: 9 -> 9, of which waited for: 8 -> 8; matrix products, arithmetic and copies ran while one was open for 0% -> 0% of each run, Pallas kernels for 3% -> 1%
where the time goes in v2:
time: 157 us
  blocking collectives  89.8 us (57%)
  Pallas kernels  30 us (19%)
  starting transfers between devices  19.8 us (13%)
  waiting for transfers between devices  16.7 us (11%)
    all_to_all x2, blocking collectives, shards(): parts = lax.all_to_all(parts, 'dp', 0, 0)  48.1 us
    all_to_all x2, blocking collectives, shards(): image = lax.all_to_all(sum_copies(parts), 'dp', 0, 0).reshape(grid)  41.7 us
    ppermute x3, waiting for transfers between devices, exchange(): return (near, lax.ppermute(near, 'mp', CHIP_SWAP))  11.8 us
    pallas_call x2, Pallas kernels, solve(): pl.pallas_call(functools.partial(solve_kernel, last), out_shape=shape, in...  11.5 us
    ppermute x3, starting transfers between devices, exchange(): return (near, lax.ppermute(near, 'mp', CHIP_SWAP))  8.51 us
    ppermute x3, starting transfers between devices, exchange(): near = add(keep, lax.ppermute(send, 'mp', CORE_SWAP))  7.49 us
    pallas_call x2, Pallas kernels, raw_next(): pl.pallas_call(next_kernel, out_shape=(shape, shape), in_specs=[SMEM, VME...  6.73 us
    pallas_call x1, Pallas kernels, raw_first(): pl.pallas_call(first_kernel, out_shape=(shape, shape, jax.ShapeDtypeStruc...  5.34 us
  transfers between devices with their start and end apart: 9, of which 8 were waited for; matrix products, arithmetic and copies ran while one was open for 0% of the time, Pallas kernels for 1%

profile of v2, /device:TPU:1, one launch (start us, length us, event | category | flops | bytes accessed | tf_op | source)
XLA Modules:
  0.0 157.1 jit_solution(6761965605452352465)
XLA Ops:
  0.6 5.3 %raw_first.1 = (f32[128,256]{1,0:T(8,128)S(1)}, f32[128,256]{1,0:T(8,128)S(1)}, bf16[512,2048]{1,0:T(8,128)(2,1)S(1)}, bf16[512,7168]{1,0:T(8,128)(2,1)S(1)}, f32[1,512]{1,0:T(1,128)S(1)}) custom-call(s32[1]{0:T(128)} %bitcast.place, s32[64,2048]{1,0:T(8,128)} %bin_hbm.1, s32[64,7168]{1,0:T(8,128)} %bout_hbm.1, bf16[512,2048]{1,0:T(8,128)(2,1)} %min_hbm.1, ...), custom_call_target="tpu_custom_call" | custom-call | tf_op jit(solution)/shard_map/raw_first/pallas_call | solution.py:109
  6.0 1.5 collective-permute-start
  8.4 3.1 %collective-permute-start.1 = (f32[128,256]{1,0:T(8,128)S(1)}, f32[128,256]{1,0:T(8,128)S(1)}, u32[]{:S(2)}, u32[]{:S(2)}) collective-permute-start(f32[128,256]{1,0:T(8,128)S(1)} %add.4.a), channel_id=1, source_target_pairs={{0,2},{2,0},{1,3},{3,1},{4,6},{6,4},{5,7},{7,5},{8,10},{10,8},{9,1... | collective-permute-start | bytes 393224 | tf_op jit(solution)/shard_map/ppermute | solution.py:350
  11.6 3.3 %collective-permute-done.1.b = f32[128,256]{1,0:T(8,128)S(1)} collective-permute-done((f32[128,256]{1,0:T(8,128)S(1)}, f32[128,256]{1,0:T(8,128)S(1)}, u32[]{:S(2)}, u32[]{:S(2)}) %collective-permute-start.1) | collective-permute-done | bytes 131104 | tf_op jit(solution)/shard_map/ppermute | solution.py:350
  14.9 1.2 collective-permute-start.2
  17.0 1.8 %image.2 = bf16[4,8,16,1152]{3,2,1,0:T(8,128)(2,1)S(1)} custom-call(s32[1]{0:T(128)} %bitcast.place, bf16[128,256]{1,0:T(8,128)(2,1)S(1)} %add.5.mine_ref, bf16[128,256]{1,0:T(8,128)(2,1)S(1)} %collective-permute-done.2.other_ref, bf16[512,2048]{1,0:T(8,128)(2,1)S(1)} %get-tuple-element.19.min_ref, bf16[512,7168]{1,0:T(8,128)(2,1)S(1)} %get-tuple-element.20.mout_ref), custom_call_target="tpu_custom_call" | custom-call | tf_op jit(solution)/shard_map/image/pallas_call | solution.py:211
  18.8 26.7 %all_to_all.20.parts = bf16[32,16,1152]{2,1,0:T(8,128)(2,1)S(1)} all-to-all(bf16[32,16,1152]{2,1,0:T(8,128)(2,1)S(1)} %bitcast.9), channel_id=1, replica_groups=mesh['dp'=32,'mp'=4] {'dp'}, dimensions={0} | all-to-all | bytes 2359296 | tf_op jit(solution)/shard_map/all_to_all | solution.py:362
  45.7 20.9 %all_to_all.21 = bf16[32,16,1152]{2,1,0:T(8,128)(2,1)S(1)} all-to-all(bf16[32,16,1152]{2,1,0:T(8,128)(2,1)S(1)} %sum_copies.2), channel_id=1, replica_groups=mesh['dp'=32,'mp'=4] {'dp'}, dimensions={0} | all-to-all | bytes 2359296 | tf_op jit(solution)/shard_map/all_to_all | solution.py:363
  66.5 3.4 %raw_next.2 = (f32[160,256]{1,0:T(8,128)S(1)}, f32[160,256]{1,0:T(8,128)S(1)}) custom-call(s32[1]{0:T(128)} %bitcast.place, bf16[4,8,16,1152]{3,2,1,0:T(8,128)(2,1)S(1)} %bitcast.8, bf16[512,2048]{1,0:T(8,128)(2,1)S(1)} %get-tuple-element.19.min_ref, bf16[512,7168]{1,0:T(8,128)(2,1)S(1)} %get-tuple-element.20.mout_ref, f32[1,512]{1,0:T(1,128)S(1)} %get-tuple-element.21.mask_ref), custom_call_target="tpu_custom_call" | custom-call | tf_op jit(solution)/shard_map/raw_next/pallas_call | solution.py:161
  69.9 3.0 %collective-permute-start.3 = (f32[160,256]{1,0:T(8,128)S(1)}, f32[160,256]{1,0:T(8,128)S(1)}, u32[]{:S(2)}, u32[]{:S(2)}) collective-permute-start(f32[160,256]{1,0:T(8,128)S(1)} %get-tuple-element.23), channel_id=1, source_target_pairs={{0,1},{1,0},{2,3},{3,2},{4,5},{5,4},{6,7},{7,6},{8,9},{9,8},{10,11... | collective-permute-start | bytes 491528 | tf_op jit(solution)/shard_map/ppermute | solution.py:349
  74.0 2.7 %collective-permute-start.4 = (f32[160,256]{1,0:T(8,128)S(1)}, f32[160,256]{1,0:T(8,128)S(1)}, u32[]{:S(2)}, u32[]{:S(2)}) collective-permute-start(f32[160,256]{1,0:T(8,128)S(1)} %add.6.near), channel_id=1, source_target_pairs={{0,2},{2,0},{1,3},{3,1},{4,6},{6,4},{5,7},{7,5},{8,10},{10,8},{9,1... | collective-permute-start | bytes 491528 | tf_op jit(solution)/shard_map/ppermute | solution.py:350
  76.7 4.3 %collective-permute-done.4.far = f32[160,256]{1,0:T(8,128)S(1)} collective-permute-done((f32[160,256]{1,0:T(8,128)S(1)}, f32[160,256]{1,0:T(8,128)S(1)}, u32[]{:S(2)}, u32[]{:S(2)}) %collective-permute-start.4) | collective-permute-done | bytes 163872 | tf_op jit(solution)/shard_map/ppermute | solution.py:350
  80.9 5.7 %solve.1.mine_ref = bf16[128,256]{1,0:T(8,128)(2,1)S(1)} custom-call(s32[1]{0:T(128)} %bitcast.place, f32[160,256]{1,0:T(8,128)S(1)} %add.6.near, f32[160,256]{1,0:T(8,128)S(1)} %collective-permute-done.4.far), custom_call_target="tpu_custom_call" | custom-call | tf_op jit(solution)/shard_map/solve/pallas_call | solution.py:275
  86.7 1.3 collective-permute-start.5
  88.9 1.8 %image.3 = bf16[4,8,16,1152]{3,2,1,0:T(8,128)(2,1)S(1)} custom-call(s32[1]{0:T(128)} %bitcast.place, bf16[128,256]{1,0:T(8,128)(2,1)S(1)} %solve.1.mine_ref, bf16[128,256]{1,0:T(8,128)(2,1)S(1)} %collective-permute-done.5.other_ref, bf16[512,2048]{1,0:T(8,128)(2,1)S(1)} %get-tuple-element.19.min_ref, bf16[512,7168]{1,0:T(8,128)(2,1)S(1)} %get-tuple-element.20.mout_ref), custom_call_target="tpu_custom_call" | custom-call | tf_op jit(solution)/shard_map/image/pallas_call | solution.py:211
  90.6 21.4 %all_to_all.22.parts = bf16[32,16,1152]{2,1,0:T(8,128)(2,1)S(1)} all-to-all(bf16[32,16,1152]{2,1,0:T(8,128)(2,1)S(1)} %bitcast.10), channel_id=1, replica_groups=mesh['dp'=32,'mp'=4] {'dp'}, dimensions={0} | all-to-all | bytes 2359296 | tf_op jit(solution)/shard_map/all_to_all | solution.py:362
  112.2 20.9 %all_to_all.23 = bf16[32,16,1152]{2,1,0:T(8,128)(2,1)S(1)} all-to-all(bf16[32,16,1152]{2,1,0:T(8,128)(2,1)S(1)} %sum_copies.3), channel_id=1, replica_groups=mesh['dp'=32,'mp'=4] {'dp'}, dimensions={0} | all-to-all | bytes 2359296 | tf_op jit(solution)/shard_map/all_to_all | solution.py:363
  133.0 3.4 %raw_next.3 = (f32[160,256]{1,0:T(8,128)S(1)}, f32[160,256]{1,0:T(8,128)S(1)}) custom-call(s32[1]{0:T(128)} %bitcast.place, bf16[4,8,16,1152]{3,2,1,0:T(8,128)(2,1)S(1)} %bitcast.6, bf16[512,2048]{1,0:T(8,128)(2,1)S(1)} %get-tuple-element.19.min_ref, bf16[512,7168]{1,0:T(8,128)(2,1)S(1)} %get-tuple-element.20.mout_ref, f32[1,512]{1,0:T(1,128)S(1)} %get-tuple-element.21.mask_ref), custom_call_target="tpu_custom_call" | custom-call | tf_op jit(solution)/shard_map/raw_next/pallas_call | solution.py:161
  136.4 3.0 %collective-permute-start.6 = (f32[160,256]{1,0:T(8,128)S(1)}, f32[160,256]{1,0:T(8,128)S(1)}, u32[]{:S(2)}, u32[]{:S(2)}) collective-permute-start(f32[160,256]{1,0:T(8,128)S(1)} %get-tuple-element.25), channel_id=1, source_target_pairs={{0,1},{1,0},{2,3},{3,2},{4,5},{5,4},{6,7},{7,6},{8,9},{9,8},{10,11... | collective-permute-start | bytes 491528 | tf_op jit(solution)/shard_map/ppermute | solution.py:349
  140.5 2.7 %collective-permute-start.7 = (f32[160,256]{1,0:T(8,128)S(1)}, f32[160,256]{1,0:T(8,128)S(1)}, u32[]{:S(2)}, u32[]{:S(2)}) collective-permute-start(f32[160,256]{1,0:T(8,128)S(1)} %add.7.near), channel_id=1, source_target_pairs={{0,2},{2,0},{1,3},{3,1},{4,6},{6,4},{5,7},{7,5},{8,10},{10,8},{9,1... | collective-permute-start | bytes 491528 | tf_op jit(solution)/shard_map/ppermute | solution.py:350
  143.2 4.3 %collective-permute-done.7.far = f32[160,256]{1,0:T(8,128)S(1)} collective-permute-done((f32[160,256]{1,0:T(8,128)S(1)}, f32[160,256]{1,0:T(8,128)S(1)}, u32[]{:S(2)}, u32[]{:S(2)}) %collective-permute-start.7) | collective-permute-done | bytes 163872 | tf_op jit(solution)/shard_map/ppermute | solution.py:350
  147.5 5.8 %solve_last.1 = (f32[16,64]{1,0:T(8,128)S(1)}, f32[16,64]{1,0:T(8,128)S(1)}, bf16[2,64,192]{2,1,0:T(8,128)(2,1)S(1)}) custom-call(s32[1]{0:T(128)} %bitcast.place, f32[160,256]{1,0:T(8,128)S(1)} %add.7.near, f32[160,256]{1,0:T(8,128)S(1)} %collective-permute-done.7.far), custom_call_target="tpu_custom_call" | custom-call | tf_op jit(solution)/shard_map/solve_last/pallas_call | solution.py:275
  153.3 1.3 collective-permute-start.8
  154.6 1.8 %basis.1 = (f32[64,2048]{1,0:T(8,128)}, f32[64,7168]{1,0:T(8,128)}) custom-call(bf16[2,64,192]{2,1,0:T(8,128)(2,1)S(1)} %get-tuple-element.28.split, bf16[4,8,16,1152]{3,2,1,0:T(8,128)(2,1)S(1)} %bitcast.7), custom_call_target="tpu_custom_call" | custom-call | tf_op jit(solution)/shard_map/basis/pallas_call | solution.py:327
  (13 shorter events, 6.0 us)
Async XLA Ops:
  6.0 2.4 %collective-permute-start = (f32[128,256]{1,0:T(8,128)S(1)}, f32[128,256]{1,0:T(8,128)S(1)}, u32[]{:S(2)}, u32[]{:S(2)}) collective-permute-start(f32[128,256]{1,0:T(8,128)S(1)} %get-tuple-element.18), channel_id=1, source_target_pairs={{0,1},{1,0},{2,3},{3,2},{4,5},{5,4},{6,7},{7,6},{8,9},{9,8},{10,11... | collective-permute-start | bytes 393224 | tf_op jit(solution)/shard_map/ppermute | solution.py:349
  8.4 6.4 %collective-permute-start.1 = (f32[128,256]{1,0:T(8,128)S(1)}, f32[128,256]{1,0:T(8,128)S(1)}, u32[]{:S(2)}, u32[]{:S(2)}) collective-permute-start(f32[128,256]{1,0:T(8,128)S(1)} %add.4.a), channel_id=1, source_target_pairs={{0,2},{2,0},{1,3},{3,1},{4,6},{6,4},{5,7},{7,5},{8,10},{10,8},{9,1... | collective-permute-start | bytes 393224 | tf_op jit(solution)/shard_map/ppermute | solution.py:350
  14.9 2.1 %collective-permute-start.2 = (bf16[128,256]{1,0:T(8,128)(2,1)S(1)}, bf16[128,256]{1,0:T(8,128)(2,1)S(1)}, u32[]{:S(2)}, u32[]{:S(2)}) collective-permute-start(bf16[128,256]{1,0:T(8,128)(2,1)S(1)} %add.5.mine_ref), channel_id=1, source_target_pairs={{0,1},{1,0},{2,3},{3,2},{4,5},{5,4},{6,7},{7,6},{8,9},{9,8},{10,11... | collective-permute-start | bytes 196616 | tf_op jit(solution)/shard_map/ppermute | solution.py:358
  69.9 4.0 %collective-permute-start.3 = (f32[160,256]{1,0:T(8,128)S(1)}, f32[160,256]{1,0:T(8,128)S(1)}, u32[]{:S(2)}, u32[]{:S(2)}) collective-permute-start(f32[160,256]{1,0:T(8,128)S(1)} %get-tuple-element.23), channel_id=1, source_target_pairs={{0,1},{1,0},{2,3},{3,2},{4,5},{5,4},{6,7},{7,6},{8,9},{9,8},{10,11... | collective-permute-start | bytes 491528 | tf_op jit(solution)/shard_map/ppermute | solution.py:349
  74.0 7.0 %collective-permute-start.4 = (f32[160,256]{1,0:T(8,128)S(1)}, f32[160,256]{1,0:T(8,128)S(1)}, u32[]{:S(2)}, u32[]{:S(2)}) collective-permute-start(f32[160,256]{1,0:T(8,128)S(1)} %add.6.near), channel_id=1, source_target_pairs={{0,2},{2,0},{1,3},{3,1},{4,6},{6,4},{5,7},{7,5},{8,10},{10,8},{9,1... | collective-permute-start | bytes 491528 | tf_op jit(solution)/shard_map/ppermute | solution.py:350
  86.7 2.2 %collective-permute-start.5 = (bf16[128,256]{1,0:T(8,128)(2,1)S(1)}, bf16[128,256]{1,0:T(8,128)(2,1)S(1)}, u32[]{:S(2)}, u32[]{:S(2)}) collective-permute-start(bf16[128,256]{1,0:T(8,128)(2,1)S(1)} %solve.1.mine_ref), channel_id=1, source_target_pairs={{0,1},{1,0},{2,3},{3,2},{4,5},{5,4},{6,7},{7,6},{8,9},{9,8},{10,11... | collective-permute-start | bytes 196616 | tf_op jit(solution)/shard_map/ppermute | solution.py:358
  136.4 4.0 %collective-permute-start.6 = (f32[160,256]{1,0:T(8,128)S(1)}, f32[160,256]{1,0:T(8,128)S(1)}, u32[]{:S(2)}, u32[]{:S(2)}) collective-permute-start(f32[160,256]{1,0:T(8,128)S(1)} %get-tuple-element.25), channel_id=1, source_target_pairs={{0,1},{1,0},{2,3},{3,2},{4,5},{5,4},{6,7},{7,6},{8,9},{9,8},{10,11... | collective-permute-start | bytes 491528 | tf_op jit(solution)/shard_map/ppermute | solution.py:349
  140.5 7.0 %collective-permute-start.7 = (f32[160,256]{1,0:T(8,128)S(1)}, f32[160,256]{1,0:T(8,128)S(1)}, u32[]{:S(2)}, u32[]{:S(2)}) collective-permute-start(f32[160,256]{1,0:T(8,128)S(1)} %add.7.near), channel_id=1, source_target_pairs={{0,2},{2,0},{1,3},{3,1},{4,6},{6,4},{5,7},{7,5},{8,10},{10,8},{9,1... | collective-permute-start | bytes 491528 | tf_op jit(solution)/shard_map/ppermute | solution.py:350
  153.3 3.1 %collective-permute-start.8 = (f32[16,64]{1,0:T(8,128)S(1)}, f32[16,64]{1,0:T(8,128)S(1)}, u32[]{:S(2)}, u32[]{:S(2)}) collective-permute-start(f32[16,64]{1,0:T(8,128)S(1)} %get-tuple-element.27), channel_id=1, source_target_pairs={{0,1},{1,0},{2,3},{3,2},{4,5},{5,4},{6,7},{7,6},{8,9},{9,8},{10,11... | collective-permute-start | bytes 12296 | tf_op jit(solution)/shard_map/ppermute | solution.py:369

commit v3 on v2

--- a/solution.py
+++ b/solution.py
@@ -25,28 +25,65 @@
     return jnp.concatenate([a, b, c], axis=1)
 
 
-def eliminate(gram):
-    n = gram.shape[0]
+PIVOTS = 4
+
+
+def eliminate(grams, size=PIVOTS):
+    n = grams[0].shape[0]
     col_id = lax.broadcasted_iota(jnp.int32, (n, n), 1)
     row_id = lax.broadcasted_iota(jnp.int32, (n, n), 0)
     eye = (col_id == row_id).astype(F32)
-    work = jnp.concatenate([gram, eye], axis=1)
-    tiles = [work[8 * i : 8 * i + 8] for i in range(n // 8)]
     sub = lax.broadcasted_iota(jnp.int32, (8, 1), 0)
-    for k in range(n - 1):
+    works = []
+    for gram in grams:
+        work = jnp.concatenate([gram, eye], axis=1)
+        works.append([work[8 * i : 8 * i + 8] for i in range(n // 8)])
+    for k in range(0, n, size):
         t, r = divmod(k, 8)
-        row = tiles[t][r : r + 1]
-        scaled = row * (1.0 / row[:, k : k + 1])
-        for i in range(t, n // 8):
-            col = tiles[i][:, k : k + 1]
-            if i == t:
-                if r == 7:
-                    continue
-                col = jnp.where(sub > r, col, 0.0)
-            tiles[i] = tiles[i] - col * scaled
-    work = jnp.concatenate(tiles, axis=0)
-    diag = jnp.sum(jnp.where(col_id == row_id, work[:, :n], 0.0), axis=1, keepdims=True)
-    return work[:, n:] * (1.0 / jnp.sqrt(diag))
+        for tiles in works:
+            rows = [tiles[t][r + i : r + i + 1] for i in range(size)]
+            wide = rows[0].shape
+            p = {
+                (i, j): jnp.broadcast_to(rows[i][:, k + j : k + j + 1], wide)
+                for i in range(size)
+                for j in range(i, size)
+            }
+            inv, low = [], {}
+            for i in range(size):
+                inv.append(1.0 / p[i, i])
+                for j in range(i + 1, size):
+                    low[j, i] = p[i, j] * inv[i]
+                for j in range(i + 1, size):
+                    for m in range(j, size):
+                        p[j, m] = p[j, m] - low[j, i] * p[i, m]
+                    rows[j] = rows[j] - low[j, i] * rows[i]
+            s = [None] * size
+            for i in reversed(range(size)):
+                s[i] = rows[i] * inv[i]
+                for j in range(i + 1, size):
+                    s[i] = s[i] - low[j, i] * s[j]
+            for i in range(t, n // 8):
+                tile = tiles[i]
+                if i == t:
+                    new = tile
+                    if r + size < 8:
+                        for j in range(size):
+                            col = jnp.where(sub >= r + size, tile[:, k + j : k + j + 1], 0.0)
+                            new = new - col * s[j]
+                    for j in range(1, size):
+                        new = jnp.where(sub == r + j, rows[j], new)
+                    tiles[i] = new
+                else:
+                    new = tile
+                    for j in range(size):
+                        new = new - tile[:, k + j : k + j + 1] * s[j]
+                    tiles[i] = new
+    out = []
+    for tiles in works:
+        work = jnp.concatenate(tiles, axis=0)
+        diag = jnp.sum(jnp.where(col_id == row_id, work[:, :n], 0.0), axis=1, keepdims=True)
+        out.append(work[:, n:] * (1.0 / jnp.sqrt(diag)))
+    return out
 
 
 def params(mib):
@@ -188,10 +225,16 @@
     )(a, b)
 
 
-def image_kernel(place, mine_ref, other_ref, min_ref, mout_ref, out, coords):
+def image_kernel(place, *refs):
+    *parts, mine_ref, other_ref, min_ref, mout_ref, out, coords = refs
     mine, other = halves(place, mine_ref.shape[1])
-    coords[:, mine] = mine_ref[...]
-    coords[:, other] = other_ref[...]
+    for cols, ref in ((mine, mine_ref), (other, other_ref)):
+        if parts:
+            (inverse,) = parts
+            for base, inv in ((0, inverse[:, :R]), (R, inverse[:, R:])):
+                coords[base : base + R, cols] = exact_dot(inv, ref[base : base + R]).astype(BF16)
+        else:
+            coords[:, cols] = ref[...]
     steps = out.shape[1]
     w_in = min_ref.shape[1] // steps
     w_out = mout_ref.shape[1] // steps
@@ -204,19 +247,19 @@
             out[g, h, :, w_in:] = part_out[rows, h * w_out : (h + 1) * w_out]
 
 
-def image_of(place, mine, other, layer_inputs, out_grads):
+def image_of(place, coords, layer_inputs, out_grads):
     steps = 8
     rows, d_in = layer_inputs.shape
     width = (d_in + out_grads.shape[1]) // steps
     return pl.pallas_call(
         image_kernel,
         out_shape=jax.ShapeDtypeStruct((GROUPS, steps, ROWS, width), BF16),
-        in_specs=[SMEM, VMEM, VMEM, VMEM, VMEM],
+        in_specs=[SMEM] + [VMEM] * (len(coords) + 2),
         out_specs=VMEM,
         scratch_shapes=[pltpu.VMEM((2 * R, rows), BF16)],
         compiler_params=params(8),
         name="image",
-    )(place, mine, other, layer_inputs, out_grads)
+    )(place, *coords, layer_inputs, out_grads)
 
 
 def sum_kernel(parts, out):
@@ -239,47 +282,72 @@
     )(parts)
 
 
-def solve_kernel(last, place, near, far, *refs):
-    total = near[...] + far[...]
-    gram = total[2 * R :]
+def exact_dot(a, b):
+    return jnp.dot(a, b, precision=lax.Precision.HIGHEST, preferred_element_type=F32)
+
+
+def inverses(gram):
     half = gram.shape[1] // 2
     gram = jnp.concatenate([gram[:, :half], gram[:, half:]], axis=0)
-    inv_in = eliminate(gram[:, :R])
-    inv_out = eliminate(gram[:, R:])
-    high = lax.Precision.HIGHEST
-    co_in = jnp.dot(inv_in, total[:R], precision=high, preferred_element_type=F32)
-    co_out = jnp.dot(inv_out, total[R : 2 * R], precision=high, preferred_element_type=F32)
-    if last:
-        own, theirs, split, feat = refs
-        feat[...] = lax.dot_general(
-            co_in.astype(BF16), co_out.astype(BF16), NT, preferred_element_type=F32
-        ) * (1.0 / LEN)
-        rows = own.shape[0]
-        own[...] = feat[pl.ds(pl.multiple_of(place[0] * rows, rows), rows)]
-        theirs[...] = feat[pl.ds(pl.multiple_of((place[0] ^ 1) * rows, rows), rows)]
-        split[0] = split3(inv_in)
-        split[1] = split3(inv_out)
-    else:
-        (coords,) = refs
-        coords[:R] = co_in.astype(BF16)
-        coords[R:] = co_out.astype(BF16)
-
-
-def solve(place, near, far, count):
-    last = count is not None
-    if last:
-        block = jax.ShapeDtypeStruct((R // count, R), F32)
-        shape = (block, block, jax.ShapeDtypeStruct((2, R, 3 * R), BF16))
-    else:
-        shape = jax.ShapeDtypeStruct((2 * R, near.shape[1]), BF16)
-    return pl.pallas_call(
-        functools.partial(solve_kernel, last),
-        out_shape=shape,
+    return eliminate([gram[:, :R], gram[:, R:]])
+
+
+def total_kernel(near, far, raw, gram):
+    raw[...] = near[: 2 * R] + far[: 2 * R]
+    gram[...] = near[2 * R :] + far[2 * R :]
+
+
+def total_of(near, far):
+    tokens = near.shape[1]
+    return pl.pallas_call(
+        total_kernel,
+        out_shape=tuple(jax.ShapeDtypeStruct((n, tokens), F32) for n in (2 * R, R // 2)),
+        in_specs=[VMEM, VMEM],
+        out_specs=(VMEM, VMEM),
+        compiler_params=params(4),
+        name="total",
+    )(near, far)
+
+
+def inverse_kernel(gram, out):
+    out[:, :R], out[:, R:] = inverses(gram[...])
+
+
+def inverse_of(gram):
+    return pl.pallas_call(
+        inverse_kernel,
+        out_shape=jax.ShapeDtypeStruct((R, 2 * R), F32),
+        in_specs=[VMEM],
+        out_specs=VMEM,
+        compiler_params=params(8),
+        cost_estimate=pl.CostEstimate(flops=1 << 22, bytes_accessed=1 << 22, transcendentals=0),
+        name="inverse",
+    )(gram)
+
+
+def last_kernel(place, near, far, own, theirs, split, feat):
+    total = near[...] + far[...]
+    inv_in, inv_out = inverses(total[2 * R :])
+    co_in = exact_dot(inv_in, total[:R]).astype(BF16)
+    co_out = exact_dot(inv_out, total[R : 2 * R]).astype(BF16)
+    feat[...] = lax.dot_general(co_in, co_out, NT, preferred_element_type=F32) * (1.0 / LEN)
+    rows = own.shape[0]
+    own[...] = feat[pl.ds(pl.multiple_of(place[0] * rows, rows), rows)]
+    theirs[...] = feat[pl.ds(pl.multiple_of((place[0] ^ 1) * rows, rows), rows)]
+    split[0] = split3(inv_in)
+    split[1] = split3(inv_out)
+
+
+def last_of(place, near, far, count):
+    block = jax.ShapeDtypeStruct((R // count, R), F32)
+    return pl.pallas_call(
+        last_kernel,
+        out_shape=(block, block, jax.ShapeDtypeStruct((2, R, 3 * R), BF16)),
         in_specs=[SMEM, VMEM, VMEM],
-        out_specs=(VMEM,) * 3 if last else VMEM,
-        scratch_shapes=[pltpu.VMEM((R, R), F32)] if last else [],
-        compiler_params=params(8),
-        name="solve_last" if last else "solve",
+        out_specs=(VMEM,) * 3,
+        scratch_shapes=[pltpu.VMEM((R, R), F32)],
+        compiler_params=params(8),
+        name="last",
     )(place, near, far)
 
 
@@ -354,9 +422,9 @@
     )
     near, far = exchange(send, keep)
     mine = add(near, far, BF16)
+    coords = (mine, lax.ppermute(mine, "mp", CORE_SWAP))
     for step in range(ITERS):
-        other = lax.ppermute(mine, "mp", CORE_SWAP)
-        parts = image_of(place, mine, other, layer_inputs, out_grads)
+        parts = image_of(place, coords, layer_inputs, out_grads)
         grid = parts.shape
         parts = parts.reshape(grid[0] * grid[1], grid[2], grid[3])
         parts = lax.all_to_all(parts, "dp", 0, 0)
@@ -364,8 +432,10 @@
         send, keep = raw_next(place, image, layer_inputs, out_grads, mask)
         near, far = exchange(send, keep)
         if step + 1 < ITERS:
-            mine = solve(place, near, far, None)
-    own, theirs, split = solve(place, near, far, lax.axis_size("mp"))
+            raw, gram = total_of(near, far)
+            other = lax.ppermute(raw, "mp", CORE_SWAP)
+            coords = (inverse_of(gram), raw, other)
+    own, theirs, split = last_of(place, near, far, lax.axis_size("mp"))
     got = lax.ppermute(theirs, "mp", CORE_SWAP)
     basis_in, basis_out = basis_of(split, image, d_in, d_out)
     return (features_of(place, own, got), basis_in, basis_out)

time: 157 us -> 151 us (0.962)
  Pallas kernels: 30 us -> 24.9 us
    pallas_call x2 -> x3, Pallas kernels: 11.5 us -> 6.06 us  [the longest x1 3.27 us: last_of(): pl.pallas_call(last_kernel, out_shape=(block, block, jax.ShapeDtypeStruct...]
  transfers between devices with their start and end apart: 9 -> 9, of which waited for: 8 -> 7; matrix products, arithmetic and copies ran while one was open for 0% -> 0% of each run, Pallas kernels for 1% -> 3%
where the time goes in v3:
time: 151 us
  blocking collectives  90 us (60%)
  Pallas kernels  24.9 us (16%)
  starting transfers between devices  19.7 us (13%)
  waiting for transfers between devices  15.8 us (10%)
    all_to_all x2, blocking collectives, shards(): parts = lax.all_to_all(parts, 'dp', 0, 0)  48.3 us
    all_to_all x2, blocking collectives, shards(): image = lax.all_to_all(sum_copies(parts), 'dp', 0, 0).reshape(grid)  41.7 us
    ppermute x3, waiting for transfers between devices, exchange(): return (near, lax.ppermute(near, 'mp', CHIP_SWAP))  11.8 us
    ppermute x3, starting transfers between devices, exchange(): return (near, lax.ppermute(near, 'mp', CHIP_SWAP))  8.51 us
    ppermute x3, starting transfers between devices, exchange(): near = add(keep, lax.ppermute(send, 'mp', CORE_SWAP))  7.38 us
    pallas_call x2, Pallas kernels, raw_next(): pl.pallas_call(next_kernel, out_shape=(shape, shape), in_specs=[SMEM, VME...  6.73 us
    pallas_call x1, Pallas kernels, raw_first(): pl.pallas_call(first_kernel, out_shape=(shape, shape, jax.ShapeDtypeStruc...  5.34 us
    pallas_call x2, Pallas kernels, image_of(): pl.pallas_call(image_kernel, out_shape=jax.ShapeDtypeStruct((GROUPS, step...  3.83 us
  transfers between devices with their start and end apart: 9, of which 7 were waited for; matrix products, arithmetic and copies ran while one was open for 0% of the time, Pallas kernels for 3%

profile of v3, /device:TPU:1, one launch (start us, length us, event | category | flops | bytes accessed | tf_op | source)
XLA Modules:
  0.0 151.1 jit_solution(1785558041740884065)
XLA Ops:
  0.6 5.3 %raw_first.1 = (f32[128,256]{1,0:T(8,128)S(1)}, f32[128,256]{1,0:T(8,128)S(1)}, bf16[512,2048]{1,0:T(8,128)(2,1)S(1)}, bf16[512,7168]{1,0:T(8,128)(2,1)S(1)}, f32[1,512]{1,0:T(1,128)S(1)}) custom-call(s32[1]{0:T(128)} %bitcast.place, s32[64,2048]{1,0:T(8,128)} %bin_hbm.1, s32[64,7168]{1,0:T(8,128)} %bout_hbm.1, bf16[512,2048]{1,0:T(8,128)(2,1)} %min_hbm.1, ...), custom_call_target="tpu_custom_call" | custom-call | tf_op jit(solution)/shard_map/raw_first/pallas_call | solution.py:146
  6.0 1.5 collective-permute-start
  8.4 3.1 %collective-permute-start.1 = (f32[128,256]{1,0:T(8,128)S(1)}, f32[128,256]{1,0:T(8,128)S(1)}, u32[]{:S(2)}, u32[]{:S(2)}) collective-permute-start(f32[128,256]{1,0:T(8,128)S(1)} %add.4.a), channel_id=1, source_target_pairs={{0,2},{2,0},{1,3},{3,1},{4,6},{6,4},{5,7},{7,5},{8,10},{10,8},{9,1... | collective-permute-start | bytes 393224 | tf_op jit(solution)/shard_map/ppermute | solution.py:418
  11.6 3.3 %collective-permute-done.1.b = f32[128,256]{1,0:T(8,128)S(1)} collective-permute-done((f32[128,256]{1,0:T(8,128)S(1)}, f32[128,256]{1,0:T(8,128)S(1)}, u32[]{:S(2)}, u32[]{:S(2)}) %collective-permute-start.1) | collective-permute-done | bytes 131104 | tf_op jit(solution)/shard_map/ppermute | solution.py:418
  14.9 1.2 collective-permute-start.2
  17.0 1.8 %image.2 = bf16[4,8,16,1152]{3,2,1,0:T(8,128)(2,1)S(1)} custom-call(s32[1]{0:T(128)} %bitcast.place, bf16[128,256]{1,0:T(8,128)(2,1)S(1)} %add.5.refs_0_, bf16[128,256]{1,0:T(8,128)(2,1)S(1)} %collective-permute-done.2.refs_1_, bf16[512,2048]{1,0:T(8,128)(2,1)S(1)} %get-tuple-element.21.refs_2_.min_ref.refs_3_, ...), custom_call_target="tpu_custom_call" | custom-call | tf_op jit(solution)/shard_map/image/pallas_call | solution.py:254
  18.8 26.7 %all_to_all.20.parts = bf16[32,16,1152]{2,1,0:T(8,128)(2,1)S(1)} all-to-all(bf16[32,16,1152]{2,1,0:T(8,128)(2,1)S(1)} %bitcast.10), channel_id=1, replica_groups=mesh['dp'=32,'mp'=4] {'dp'}, dimensions={0} | all-to-all | bytes 2359296 | tf_op jit(solution)/shard_map/all_to_all | solution.py:430
  45.7 20.9 %all_to_all.21 = bf16[32,16,1152]{2,1,0:T(8,128)(2,1)S(1)} all-to-all(bf16[32,16,1152]{2,1,0:T(8,128)(2,1)S(1)} %sum_copies.2), channel_id=1, replica_groups=mesh['dp'=32,'mp'=4] {'dp'}, dimensions={0} | all-to-all | bytes 2359296 | tf_op jit(solution)/shard_map/all_to_all | solution.py:431
  66.5 3.4 %raw_next.2 = (f32[160,256]{1,0:T(8,128)S(1)}, f32[160,256]{1,0:T(8,128)S(1)}) custom-call(s32[1]{0:T(128)} %bitcast.place, bf16[4,8,16,1152]{3,2,1,0:T(8,128)(2,1)S(1)} %bitcast.8, bf16[512,2048]{1,0:T(8,128)(2,1)S(1)} %get-tuple-element.21.refs_2_.min_ref.refs_3_, bf16[512,7168]{1,0:T(8,128)(2,1)S(1)} %get-tuple-element.22.refs_3_.mout_ref.refs_4_, ...), custom_call_target="tpu_custom_call" | custom-call | tf_op jit(solution)/shard_map/raw_next/pallas_call | solution.py:198
  69.9 3.0 %collective-permute-start.3 = (f32[160,256]{1,0:T(8,128)S(1)}, f32[160,256]{1,0:T(8,128)S(1)}, u32[]{:S(2)}, u32[]{:S(2)}) collective-permute-start(f32[160,256]{1,0:T(8,128)S(1)} %get-tuple-element.25), channel_id=1, source_target_pairs={{0,1},{1,0},{2,3},{3,2},{4,5},{5,4},{6,7},{7,6},{8,9},{9,8},{10,11... | collective-permute-start | bytes 491528 | tf_op jit(solution)/shard_map/ppermute | solution.py:417
  74.0 2.7 %collective-permute-start.4 = (f32[160,256]{1,0:T(8,128)S(1)}, f32[160,256]{1,0:T(8,128)S(1)}, u32[]{:S(2)}, u32[]{:S(2)}) collective-permute-start(f32[160,256]{1,0:T(8,128)S(1)} %add.6.near), channel_id=1, source_target_pairs={{0,2},{2,0},{1,3},{3,1},{4,6},{6,4},{5,7},{7,5},{8,10},{10,8},{9,1... | collective-permute-start | bytes 491528 | tf_op jit(solution)/shard_map/ppermute | solution.py:418
  76.7 4.3 %collective-permute-done.4.far = f32[160,256]{1,0:T(8,128)S(1)} collective-permute-done((f32[160,256]{1,0:T(8,128)S(1)}, f32[160,256]{1,0:T(8,128)S(1)}, u32[]{:S(2)}, u32[]{:S(2)}) %collective-permute-start.4) | collective-permute-done | bytes 163872 | tf_op jit(solution)/shard_map/ppermute | solution.py:418
  81.0 1.3 collective-permute-start.5
  82.3 2.8 %inverse.1.refs_0_ = f32[64,128]{1,0:T(8,128)S(1)} custom-call(f32[32,256]{1,0:T(8,128)S(1)} %get-tuple-element.26.gram), custom_call_target="tpu_custom_call" | custom-call | flops 4194304 | bytes 4194304 | tf_op jit(solution)/shard_map/inverse/pallas_call | solution.py:317
  85.1 2.1 %image.3 = bf16[4,8,16,1152]{3,2,1,0:T(8,128)(2,1)S(1)} custom-call(s32[1]{0:T(128)} %bitcast.place, f32[64,128]{1,0:T(8,128)S(1)} %inverse.1.refs_0_, f32[128,256]{1,0:T(8,128)S(1)} %get-tuple-element.27.refs_1_, f32[128,256]{1,0:T(8,128)S(1)} %collective-permute-done.5.refs_2_, bf16[512,2048]{1,0:T(8,128)(2,1)S(1)} %get-tuple-element.21.refs_2_.min_ref.refs_3_, ...), custom_call_target="tpu_custom_call" | custom-call | tf_op jit(solution)/shard_map/image/pallas_call | solution.py:254
  87.1 21.6 %all_to_all.22.parts = bf16[32,16,1152]{2,1,0:T(8,128)(2,1)S(1)} all-to-all(bf16[32,16,1152]{2,1,0:T(8,128)(2,1)S(1)} %bitcast.9), channel_id=1, replica_groups=mesh['dp'=32,'mp'=4] {'dp'}, dimensions={0} | all-to-all | bytes 2359296 | tf_op jit(solution)/shard_map/all_to_all | solution.py:430
  109.0 20.8 %all_to_all.23 = bf16[32,16,1152]{2,1,0:T(8,128)(2,1)S(1)} all-to-all(bf16[32,16,1152]{2,1,0:T(8,128)(2,1)S(1)} %sum_copies.3), channel_id=1, replica_groups=mesh['dp'=32,'mp'=4] {'dp'}, dimensions={0} | all-to-all | bytes 2359296 | tf_op jit(solution)/shard_map/all_to_all | solution.py:431
  129.8 3.4 %raw_next.3 = (f32[160,256]{1,0:T(8,128)S(1)}, f32[160,256]{1,0:T(8,128)S(1)}) custom-call(s32[1]{0:T(128)} %bitcast.place, bf16[4,8,16,1152]{3,2,1,0:T(8,128)(2,1)S(1)} %bitcast.6, bf16[512,2048]{1,0:T(8,128)(2,1)S(1)} %get-tuple-element.21.refs_2_.min_ref.refs_3_, bf16[512,7168]{1,0:T(8,128)(2,1)S(1)} %get-tuple-element.22.refs_3_.mout_ref.refs_4_, ...), custom_call_target="tpu_custom_call" | custom-call | tf_op jit(solution)/shard_map/raw_next/pallas_call | solution.py:198
  133.1 2.9 %collective-permute-start.6 = (f32[160,256]{1,0:T(8,128)S(1)}, f32[160,256]{1,0:T(8,128)S(1)}, u32[]{:S(2)}, u32[]{:S(2)}) collective-permute-start(f32[160,256]{1,0:T(8,128)S(1)} %get-tuple-element.29), channel_id=1, source_target_pairs={{0,1},{1,0},{2,3},{3,2},{4,5},{5,4},{6,7},{7,6},{8,9},{9,8},{10,11... | collective-permute-start | bytes 491528 | tf_op jit(solution)/shard_map/ppermute | solution.py:417
  137.1 2.7 %collective-permute-start.7 = (f32[160,256]{1,0:T(8,128)S(1)}, f32[160,256]{1,0:T(8,128)S(1)}, u32[]{:S(2)}, u32[]{:S(2)}) collective-permute-start(f32[160,256]{1,0:T(8,128)S(1)} %add.7.near), channel_id=1, source_target_pairs={{0,2},{2,0},{1,3},{3,1},{4,6},{6,4},{5,7},{7,5},{8,10},{10,8},{9,1... | collective-permute-start | bytes 491528 | tf_op jit(solution)/shard_map/ppermute | solution.py:418
  139.8 4.3 %collective-permute-done.7.far = f32[160,256]{1,0:T(8,128)S(1)} collective-permute-done((f32[160,256]{1,0:T(8,128)S(1)}, f32[160,256]{1,0:T(8,128)S(1)}, u32[]{:S(2)}, u32[]{:S(2)}) %collective-permute-start.7) | collective-permute-done | bytes 163872 | tf_op jit(solution)/shard_map/ppermute | solution.py:418
  144.1 3.3 %last.1 = (f32[16,64]{1,0:T(8,128)S(1)}, f32[16,64]{1,0:T(8,128)S(1)}, bf16[2,64,192]{2,1,0:T(8,128)(2,1)S(1)}) custom-call(s32[1]{0:T(128)} %bitcast.place, f32[160,256]{1,0:T(8,128)S(1)} %add.7.near, f32[160,256]{1,0:T(8,128)S(1)} %collective-permute-done.7.far), custom_call_target="tpu_custom_call" | custom-call | tf_op jit(solution)/shard_map/last/pallas_call | solution.py:343
  147.3 1.3 collective-permute-start.8
  148.6 1.8 %basis.1 = (f32[64,2048]{1,0:T(8,128)}, f32[64,7168]{1,0:T(8,128)}) custom-call(bf16[2,64,192]{2,1,0:T(8,128)(2,1)S(1)} %get-tuple-element.32.split, bf16[4,8,16,1152]{3,2,1,0:T(8,128)(2,1)S(1)} %bitcast.7), custom_call_target="tpu_custom_call" | custom-call | tf_op jit(solution)/shard_map/basis/pallas_call | solution.py:395
  (14 shorter events, 5.1 us)
Async XLA Ops:
  6.0 2.4 %collective-permute-start = (f32[128,256]{1,0:T(8,128)S(1)}, f32[128,256]{1,0:T(8,128)S(1)}, u32[]{:S(2)}, u32[]{:S(2)}) collective-permute-start(f32[128,256]{1,0:T(8,128)S(1)} %get-tuple-element.20), channel_id=1, source_target_pairs={{0,1},{1,0},{2,3},{3,2},{4,5},{5,4},{6,7},{7,6},{8,9},{9,8},{10,11... | collective-permute-start | bytes 393224 | tf_op jit(solution)/shard_map/ppermute | solution.py:417
  8.4 6.4 %collective-permute-start.1 = (f32[128,256]{1,0:T(8,128)S(1)}, f32[128,256]{1,0:T(8,128)S(1)}, u32[]{:S(2)}, u32[]{:S(2)}) collective-permute-start(f32[128,256]{1,0:T(8,128)S(1)} %add.4.a), channel_id=1, source_target_pairs={{0,2},{2,0},{1,3},{3,1},{4,6},{6,4},{5,7},{7,5},{8,10},{10,8},{9,1... | collective-permute-start | bytes 393224 | tf_op jit(solution)/shard_map/ppermute | solution.py:418
  14.9 2.1 %collective-permute-start.2 = (bf16[128,256]{1,0:T(8,128)(2,1)S(1)}, bf16[128,256]{1,0:T(8,128)(2,1)S(1)}, u32[]{:S(2)}, u32[]{:S(2)}) collective-permute-start(bf16[128,256]{1,0:T(8,128)(2,1)S(1)} %add.5.refs_0_), channel_id=1, source_target_pairs={{0,1},{1,0},{2,3},{3,2},{4,5},{5,4},{6,7},{7,6},{8,9},{9,8},{10,11... | collective-permute-start | bytes 196616 | tf_op jit(solution)/shard_map/ppermute | solution.py:425
  69.9 4.0 %collective-permute-start.3 = (f32[160,256]{1,0:T(8,128)S(1)}, f32[160,256]{1,0:T(8,128)S(1)}, u32[]{:S(2)}, u32[]{:S(2)}) collective-permute-start(f32[160,256]{1,0:T(8,128)S(1)} %get-tuple-element.25), channel_id=1, source_target_pairs={{0,1},{1,0},{2,3},{3,2},{4,5},{5,4},{6,7},{7,6},{8,9},{9,8},{10,11... | collective-permute-start | bytes 491528 | tf_op jit(solution)/shard_map/ppermute | solution.py:417
  74.0 7.0 %collective-permute-start.4 = (f32[160,256]{1,0:T(8,128)S(1)}, f32[160,256]{1,0:T(8,128)S(1)}, u32[]{:S(2)}, u32[]{:S(2)}) collective-permute-start(f32[160,256]{1,0:T(8,128)S(1)} %add.6.near), channel_id=1, source_target_pairs={{0,2},{2,0},{1,3},{3,1},{4,6},{6,4},{5,7},{7,5},{8,10},{10,8},{9,1... | collective-permute-start | bytes 491528 | tf_op jit(solution)/shard_map/ppermute | solution.py:418
  81.0 4.1 %collective-permute-start.5 = (f32[128,256]{1,0:T(8,128)S(1)}, f32[128,256]{1,0:T(8,128)S(1)}, u32[]{:S(2)}, u32[]{:S(2)}) collective-permute-start(f32[128,256]{1,0:T(8,128)S(1)} %get-tuple-element.27.refs_1_), channel_id=1, source_target_pairs={{0,1},{1,0},{2,3},{3,2},{4,5},{5,4},{6,7},{7,6},{8,9},{9,8},{10,11... | collective-permute-start | bytes 393224 | tf_op jit(solution)/shard_map/ppermute | solution.py:436
  133.1 3.9 %collective-permute-start.6 = (f32[160,256]{1,0:T(8,128)S(1)}, f32[160,256]{1,0:T(8,128)S(1)}, u32[]{:S(2)}, u32[]{:S(2)}) collective-permute-start(f32[160,256]{1,0:T(8,128)S(1)} %get-tuple-element.29), channel_id=1, source_target_pairs={{0,1},{1,0},{2,3},{3,2},{4,5},{5,4},{6,7},{7,6},{8,9},{9,8},{10,11... | collective-permute-start | bytes 491528 | tf_op jit(solution)/shard_map/ppermute | solution.py:417
  137.1 7.0 %collective-permute-start.7 = (f32[160,256]{1,0:T(8,128)S(1)}, f32[160,256]{1,0:T(8,128)S(1)}, u32[]{:S(2)}, u32[]{:S(2)}) collective-permute-start(f32[160,256]{1,0:T(8,128)S(1)} %add.7.near), channel_id=1, source_target_pairs={{0,2},{2,0},{1,3},{3,1},{4,6},{6,4},{5,7},{7,5},{8,10},{10,8},{9,1... | collective-permute-start | bytes 491528 | tf_op jit(solution)/shard_map/ppermute | solution.py:418
  147.3 3.1 %collective-permute-start.8 = (f32[16,64]{1,0:T(8,128)S(1)}, f32[16,64]{1,0:T(8,128)S(1)}, u32[]{:S(2)}, u32[]{:S(2)}) collective-permute-start(f32[16,64]{1,0:T(8,128)S(1)} %get-tuple-element.31), channel_id=1, source_target_pairs={{0,1},{1,0},{2,3},{3,2},{4,5},{5,4},{6,7},{7,6},{8,9},{9,8},{10,11... | collective-permute-start | bytes 12296 | tf_op jit(solution)/shard_map/ppermute | solution.py:439

commit v4 on v3

--- a/solution.py
+++ b/solution.py
@@ -25,7 +25,8 @@
     return jnp.concatenate([a, b, c], axis=1)
 
 
-PIVOTS = 4
+PIVOTS = 8
+STAGGER_NS = 8500
 
 
 def eliminate(grams, size=PIVOTS):
@@ -167,7 +168,14 @@
     )(place, *(pltpu.with_memory_space_constraint(x, pltpu.HBM) for x in whole))
 
 
-def next_kernel(place, img_ref, min_ref, mout_ref, mask_ref, send, keep, img_in, img_out, acc):
+def half_coords(tokens, img_in, img_out, min_ref, mout_ref, mask, out):
+    part = lax.dot_general(img_in, min_ref[tokens, :], NT, preferred_element_type=F32)
+    out[:R] = part
+    part = lax.dot_general(img_out, mout_ref[tokens, :], NT, preferred_element_type=F32)
+    out[R : 2 * R] = part * mask[:, tokens]
+
+
+def send_kernel(place, img_ref, min_ref, mout_ref, mask, send, img_in, img_out):
     steps = img_ref.shape[1]
     w_in = img_in.shape[1] // steps
     w_out = img_out.shape[1] // steps
@@ -177,37 +185,64 @@
             img_in[rows, h * w_in : (h + 1) * w_in] = img_ref[g, h, :, :w_in]
             img_out[rows, h * w_out : (h + 1) * w_out] = img_ref[g, h, :, w_in:]
     half_in, half_out = img_in[...], img_out[...]
+    _, other = halves(place, send.shape[1])
+    half_coords(other, half_in, half_out, min_ref, mout_ref, mask, send)
     gram_in = lax.dot_general(half_in, half_in, NT, preferred_element_type=F32)
     gram_out = lax.dot_general(half_out, half_out, NT, preferred_element_type=F32)
-    acc[:R] = lax.dot_general(half_in, min_ref[...], NT, preferred_element_type=F32)
-    raw_out = lax.dot_general(half_out, mout_ref[...], NT, preferred_element_type=F32)
-    acc[R:] = raw_out * mask_ref[...]
-    mine, other = halves(place, acc.shape[1] // 2)
-    keep[: 2 * R] = acc[:, mine]
-    send[: 2 * R] = acc[:, other]
     gram = jnp.concatenate([gram_in, gram_out], axis=1)
-    gram = jnp.concatenate([gram[: R // 2], gram[R // 2 :]], axis=1)
-    keep[2 * R :] = gram
-    send[2 * R :] = gram
-
-
-def raw_next(place, image, layer_inputs, out_grads, mask):
+    send[2 * R :] = jnp.concatenate([gram[: R // 2], gram[R // 2 :]], axis=1)
+
+
+def raw_send(place, image, layer_inputs, out_grads, mask):
     rows, d_in = layer_inputs.shape
     d_out = out_grads.shape[1]
-    shape = jax.ShapeDtypeStruct((2 * R + R // 2, rows // 2), F32)
-    return pl.pallas_call(
-        next_kernel,
-        out_shape=(shape, shape),
+    return pl.pallas_call(
+        send_kernel,
+        out_shape=(
+            jax.ShapeDtypeStruct((2 * R + R // 2, rows // 2), F32),
+            jax.ShapeDtypeStruct((R, d_in), BF16),
+            jax.ShapeDtypeStruct((R, d_out), BF16),
+        ),
         in_specs=[SMEM, VMEM, VMEM, VMEM, VMEM],
-        out_specs=(VMEM, VMEM),
-        scratch_shapes=[
-            pltpu.VMEM((R, d_in), BF16),
-            pltpu.VMEM((R, d_out), BF16),
-            pltpu.VMEM((2 * R, rows), F32),
-        ],
-        compiler_params=params(8),
-        name="raw_next",
+        out_specs=(VMEM,) * 3,
+        compiler_params=params(8),
+        name="raw_send",
     )(place, image, layer_inputs, out_grads, mask)
+
+
+def keep_kernel(place, img_in, img_out, min_ref, mout_ref, mask, keep):
+    mine, _ = halves(place, keep.shape[1])
+    half_coords(mine, img_in[...], img_out[...], min_ref, mout_ref, mask, keep)
+
+
+def raw_keep(place, img_in, img_out, layer_inputs, out_grads, mask):
+    rows = layer_inputs.shape[0]
+    return pl.pallas_call(
+        keep_kernel,
+        out_shape=jax.ShapeDtypeStruct((2 * R, rows // 2), F32),
+        in_specs=[SMEM] + [VMEM] * 5,
+        out_specs=VMEM,
+        compiler_params=params(8),
+        cost_estimate=pl.CostEstimate(flops=1 << 29, bytes_accessed=1 << 22, transcendentals=0),
+        name="raw_keep",
+    )(place, img_in, img_out, layer_inputs, out_grads, mask)
+
+
+def near_kernel(keep, send, got, out):
+    top = keep.shape[0]
+    out[:top] = keep[...] + got[:top]
+    out[top:] = send[top:] + got[top:]
+
+
+def near_of(keep, send, got):
+    return pl.pallas_call(
+        near_kernel,
+        out_shape=jax.ShapeDtypeStruct(send.shape, F32),
+        in_specs=[VMEM] * 3,
+        out_specs=VMEM,
+        compiler_params=params(4),
+        name="near",
+    )(keep, send, got)
 
 
 def add_kernel(a, b, out):
@@ -228,6 +263,11 @@
 def image_kernel(place, *refs):
     *parts, mine_ref, other_ref, min_ref, mout_ref, out, coords = refs
     mine, other = halves(place, mine_ref.shape[1])
+
+    @pl.when((place[0] & 1) == 1)
+    def _():
+        pl.delay(STAGGER_NS)
+
     for cols, ref in ((mine, mine_ref), (other, other_ref)):
         if parts:
             (inverse,) = parts
@@ -371,37 +411,33 @@
     )(place, own, got)
 
 
-def basis_kernel(split, img_ref, in_hbm, out_hbm, b_in, b_out, sems):
-    steps = img_ref.shape[1]
-    w_in = b_in.shape[1] // steps
-    w_out = b_out.shape[1] // steps
+def basis_kernel(split, img_in, img_out, in_hbm, out_hbm, b_in, b_out, sems):
+    steps = sems.shape[0]
     copies = []
     for h in range(steps):
-        img = jnp.concatenate([img_ref[g, h] for g in range(GROUPS)] * 3, axis=0)
-        cols_in = slice(h * w_in, (h + 1) * w_in)
-        cols_out = slice(h * w_out, (h + 1) * w_out)
-        b_in[:, cols_in] = jnp.dot(split[0], img[:, :w_in], preferred_element_type=F32)
-        b_out[:, cols_out] = jnp.dot(split[1], img[:, w_in:], preferred_element_type=F32)
-        for n, (src, dst, cols) in enumerate([(b_in, in_hbm, cols_in), (b_out, out_hbm, cols_out)]):
-            copy = pltpu.make_async_copy(src.at[:, cols], dst.at[:, cols], sems.at[h, n])
+        for n, (img, own, whole) in enumerate([(img_in, b_in, in_hbm), (img_out, b_out, out_hbm)]):
+            width = own.shape[1] // steps
+            cols = slice(h * width, (h + 1) * width)
+            part = jnp.concatenate([img[:, cols]] * 3, axis=0)
+            own[:, cols] = jnp.dot(split[n], part, preferred_element_type=F32)
+            copy = pltpu.make_async_copy(own.at[:, cols], whole.at[:, cols], sems.at[h, n])
             copy.start()
             copies.append(copy)
     for copy in copies:
         copy.wait()
 
 
-def basis_of(split, image, d_in, d_out):
-    shapes = ((R, d_in), (R, d_out))
+def basis_of(split, img_in, img_out):
+    shapes = (img_in.shape, img_out.shape)
     return pl.pallas_call(
         basis_kernel,
         out_shape=tuple(jax.ShapeDtypeStruct(s, F32) for s in shapes),
-        in_specs=[VMEM, VMEM],
+        in_specs=[VMEM] * 3,
         out_specs=(HBM, HBM),
-        scratch_shapes=[pltpu.VMEM(s, F32) for s in shapes]
-        + [pltpu.SemaphoreType.DMA((image.shape[1], 2))],
+        scratch_shapes=[pltpu.VMEM(s, F32) for s in shapes] + [pltpu.SemaphoreType.DMA((4, 2))],
         compiler_params=params(8),
         name="basis",
-    )(split, image)
+    )(split, img_in, img_out)
 
 
 CORE_SWAP = [(0, 1), (1, 0), (2, 3), (3, 2)]
@@ -411,16 +447,11 @@
 def shards(layer_inputs, out_grads, loss_mask, start_in, start_out):
     place = lax.axis_index("mp").reshape(1)
     mask = loss_mask.reshape(1, -1)
-    d_in, d_out = layer_inputs.shape[1], out_grads.shape[1]
-
-    def exchange(send, keep):
-        near = add(keep, lax.ppermute(send, "mp", CORE_SWAP))
-        return near, lax.ppermute(near, "mp", CHIP_SWAP)
-
     send, keep, layer_inputs, out_grads, mask = raw_first(
         place, start_in, start_out, layer_inputs, out_grads, mask
     )
-    near, far = exchange(send, keep)
+    near = add(keep, lax.ppermute(send, "mp", CORE_SWAP))
+    far = lax.ppermute(near, "mp", CHIP_SWAP)
     mine = add(near, far, BF16)
     coords = (mine, lax.ppermute(mine, "mp", CORE_SWAP))
     for step in range(ITERS):
@@ -429,15 +460,18 @@
         parts = parts.reshape(grid[0] * grid[1], grid[2], grid[3])
         parts = lax.all_to_all(parts, "dp", 0, 0)
         image = lax.all_to_all(sum_copies(parts), "dp", 0, 0).reshape(grid)
-        send, keep = raw_next(place, image, layer_inputs, out_grads, mask)
-        near, far = exchange(send, keep)
+        send, img_in, img_out = raw_send(place, image, layer_inputs, out_grads, mask)
+        got = lax.ppermute(send, "mp", CORE_SWAP)
+        keep = raw_keep(place, img_in, img_out, layer_inputs, out_grads, mask)
+        near = near_of(keep, send, got)
+        far = lax.ppermute(near, "mp", CHIP_SWAP)
         if step + 1 < ITERS:
             raw, gram = total_of(near, far)
             other = lax.ppermute(raw, "mp", CORE_SWAP)
             coords = (inverse_of(gram), raw, other)
     own, theirs, split = last_of(place, near, far, lax.axis_size("mp"))
     got = lax.ppermute(theirs, "mp", CORE_SWAP)
-    basis_in, basis_out = basis_of(split, image, d_in, d_out)
+    basis_in, basis_out = basis_of(split, img_in, img_out)
     return (features_of(place, own, got), basis_in, basis_out)
 
 

time: 151 us -> 141 us (0.934)
  blocking collectives: 90 us -> 71.5 us
  Pallas kernels: 24.9 us -> 41.1 us
  starting transfers between devices: 19.7 us -> 14.2 us
  waiting for transfers between devices: 15.8 us -> 13.5 us
    pallas_call x2, Pallas kernels: 3.83 us -> 20.8 us  [image_of(): pl.pallas_call(image_kernel, out_shape=jax.ShapeDtypeStruct((GROUPS, step...]
    all_to_all x2, blocking collectives: 48.3 us -> 38 us  [shards(): parts = lax.all_to_all(parts, 'dp', 0, 0)]
    all_to_all x2, blocking collectives: 41.7 us -> 33.5 us  [shards(): image = lax.all_to_all(sum_copies(parts), 'dp', 0, 0).reshape(grid)]
    ppermute x6, starting transfers between devices: 15.9 us -> 10.1 us  [the longest x3 8.51 us: shards(): far = lax.ppermute(near, 'mp', CHIP_SWAP)]
    ppermute x6, waiting for transfers between devices: 14.9 us -> 12.6 us  [the longest x3 11.6 us: shards(): far = lax.ppermute(near, 'mp', CHIP_SWAP)]
    pallas_call x2 -> x6, Pallas kernels: 6.73 us -> 6.87 us  [the longest x2 3.74 us: raw_send(): pl.pallas_call(send_kernel, out_shape=(jax.ShapeDtypeStruct((2 * R + R //...]
  transfers between devices with their start and end apart: 9 -> 9, of which waited for: 7 -> 5; matrix products, arithmetic and copies ran while one was open for 0% -> 0% of each run, Pallas kernels for 3% -> 5%
where the time goes in v4:
time: 141 us
  blocking collectives  71.5 us (51%)
  Pallas kernels  41.1 us (29%)
  starting transfers between devices  14.2 us (10%)
  waiting for transfers between devices  13.5 us (10%)
    all_to_all x2, blocking collectives, shards(): parts = lax.all_to_all(parts, 'dp', 0, 0)  38 us
    all_to_all x2, blocking collectives, shards(): image = lax.all_to_all(sum_copies(parts), 'dp', 0, 0).reshape(grid)  33.5 us
    pallas_call x2, Pallas kernels, image_of(): pl.pallas_call(image_kernel, out_shape=jax.ShapeDtypeStruct((GROUPS, step...  20.8 us
    ppermute x3, waiting for transfers between devices, shards(): far = lax.ppermute(near, 'mp', CHIP_SWAP)  11.6 us
    ppermute x3, starting transfers between devices, shards(): far = lax.ppermute(near, 'mp', CHIP_SWAP)  8.51 us
    pallas_call x1, Pallas kernels, raw_first(): pl.pallas_call(first_kernel, out_shape=(shape, shape, jax.ShapeDtypeStruc...  5.34 us
    pallas_call x2, Pallas kernels, raw_send(): pl.pallas_call(send_kernel, out_shape=(jax.ShapeDtypeStruct((2 * R + R //...  3.74 us
    pallas_call x2, Pallas kernels, raw_keep(): pl.pallas_call(keep_kernel, out_shape=jax.ShapeDtypeStruct((2 * R, rows /...  3.08 us
  transfers between devices with their start and end apart: 9, of which 5 were waited for; matrix products, arithmetic and copies ran while one was open for 0% of the time, Pallas kernels for 5%

profile of v4, /device:TPU:1, one launch (start us, length us, event | category | flops | bytes accessed | tf_op | source)
XLA Modules:
  0.0 141.1 jit_solution(12210713835522759594)
XLA Ops:
  0.6 5.3 %raw_first.1 = (f32[128,256]{1,0:T(8,128)S(1)}, f32[128,256]{1,0:T(8,128)S(1)}, bf16[512,2048]{1,0:T(8,128)(2,1)S(1)}, bf16[512,7168]{1,0:T(8,128)(2,1)S(1)}, f32[1,512]{1,0:T(1,128)S(1)}) custom-call(s32[1]{0:T(128)} %bitcast.place, s32[64,2048]{1,0:T(8,128)} %bin_hbm.1, s32[64,7168]{1,0:T(8,128)} %bout_hbm.1, bf16[512,2048]{1,0:T(8,128)(2,1)} %min_hbm.1, ...), custom_call_target="tpu_custom_call" | custom-call | tf_op jit(solution)/shard_map/raw_first/pallas_call | solution.py:147
  6.0 1.5 %collective-permute-start = (f32[128,256]{1,0:T(8,128)S(1)}, f32[128,256]{1,0:T(8,128)S(1)}, u32[]{:S(2)}, u32[]{:S(2)}) collective-permute-start(f32[128,256]{1,0:T(8,128)S(1)} %get-tuple-element.22), channel_id=1, source_target_pairs={{0,1},{1,0},{2,3},{3,2},{4,5},{5,4},{6,7},{7,6},{8,9},{9,8},{10,11... | collective-permute-start | bytes 393224 | tf_op jit(solution)/shard_map/ppermute | solution.py:453
  8.4 3.1 %collective-permute-start.1 = (f32[128,256]{1,0:T(8,128)S(1)}, f32[128,256]{1,0:T(8,128)S(1)}, u32[]{:S(2)}, u32[]{:S(2)}) collective-permute-start(f32[128,256]{1,0:T(8,128)S(1)} %add.2.a), channel_id=1, source_target_pairs={{0,2},{2,0},{1,3},{3,1},{4,6},{6,4},{5,7},{7,5},{8,10},{10,8},{9,1... | collective-permute-start | bytes 393224 | tf_op jit(solution)/shard_map/ppermute | solution.py:454
  11.6 3.3 %collective-permute-done.1.b = f32[128,256]{1,0:T(8,128)S(1)} collective-permute-done((f32[128,256]{1,0:T(8,128)S(1)}, f32[128,256]{1,0:T(8,128)S(1)}, u32[]{:S(2)}, u32[]{:S(2)}) %collective-permute-start.1) | collective-permute-done | bytes 131104 | tf_op jit(solution)/shard_map/ppermute | solution.py:454
  14.9 1.2 collective-permute-start.2
  17.0 10.3 %image.2 = bf16[4,8,16,1152]{3,2,1,0:T(8,128)(2,1)S(1)} custom-call(s32[1]{0:T(128)} %bitcast.place, bf16[128,256]{1,0:T(8,128)(2,1)S(1)} %add.3.refs_0_, bf16[128,256]{1,0:T(8,128)(2,1)S(1)} %collective-permute-done.2.refs_1_, bf16[512,2048]{1,0:T(8,128)(2,1)S(1)} %get-tuple-element.23.refs_2_.min_ref.refs_3_, ...), custom_call_target="tpu_custom_call" | custom-call | tf_op jit(solution)/shard_map/image/pallas_call | solution.py:294
  27.3 21.7 %all_to_all.20.parts = bf16[32,16,1152]{2,1,0:T(8,128)(2,1)S(1)} all-to-all(bf16[32,16,1152]{2,1,0:T(8,128)(2,1)S(1)} %bitcast.9), channel_id=1, replica_groups=mesh['dp'=32,'mp'=4] {'dp'}, dimensions={0} | all-to-all | bytes 2359296 | tf_op jit(solution)/shard_map/all_to_all | solution.py:461
  49.1 17.1 %all_to_all.21 = bf16[32,16,1152]{2,1,0:T(8,128)(2,1)S(1)} all-to-all(bf16[32,16,1152]{2,1,0:T(8,128)(2,1)S(1)} %sum_copies.2), channel_id=1, replica_groups=mesh['dp'=32,'mp'=4] {'dp'}, dimensions={0} | all-to-all | bytes 2359296 | tf_op jit(solution)/shard_map/all_to_all | solution.py:462
  66.2 1.9 %raw_send.2 = (f32[160,256]{1,0:T(8,128)S(1)}, bf16[64,2048]{1,0:T(8,128)(2,1)S(1)}, bf16[64,7168]{1,0:T(8,128)(2,1)S(1)}) custom-call(s32[1]{0:T(128)} %bitcast.place, bf16[4,8,16,1152]{3,2,1,0:T(8,128)(2,1)S(1)} %bitcast.6, bf16[512,2048]{1,0:T(8,128)(2,1)S(1)} %get-tuple-element.23.refs_2_.min_ref.refs_3_, ...), custom_call_target="tpu_custom_call" | custom-call | tf_op jit(solution)/shard_map/raw_send/pallas_call | solution.py:199
  68.2 1.5 %raw_keep.2.keep = f32[128,256]{1,0:T(8,128)S(1)} custom-call(s32[1]{0:T(128)} %bitcast.place, bf16[64,2048]{1,0:T(8,128)(2,1)S(1)} %get-tuple-element.26.img_in, bf16[64,7168]{1,0:T(8,128)(2,1)S(1)} %get-tuple-element.27.img_out, bf16[512,2048]{1,0:T(8,128)(2,1)S(1)} %get-tuple-element.23.refs_2_.min_ref.refs_3_, ...), custom_call_target="tpu_custom_call" | custom-call | flops 536870912 | bytes 4194304 | tf_op jit(solution)/shard_map/raw_keep/pallas_call | solution.py:220
  69.7 2.7 %collective-permute-start.4 = (f32[160,256]{1,0:T(8,128)S(1)}, f32[160,256]{1,0:T(8,128)S(1)}, u32[]{:S(2)}, u32[]{:S(2)}) collective-permute-start(f32[160,256]{1,0:T(8,128)S(1)} %near.2), channel_id=1, source_target_pairs={{0,2},{2,0},{1,3},{3,1},{4,6},{6,4},{5,7},{7,5},{8,10},{10,8},{9,1... | collective-permute-start | bytes 491528 | tf_op jit(solution)/shard_map/ppermute | solution.py:467
  72.4 4.1 %collective-permute-done.4.far = f32[160,256]{1,0:T(8,128)S(1)} collective-permute-done((f32[160,256]{1,0:T(8,128)S(1)}, f32[160,256]{1,0:T(8,128)S(1)}, u32[]{:S(2)}, u32[]{:S(2)}) %collective-permute-start.4) | collective-permute-done | bytes 163872 | tf_op jit(solution)/shard_map/ppermute | solution.py:467
  76.6 1.4 %collective-permute-start.5 = (f32[128,256]{1,0:T(8,128)S(1)}, f32[128,256]{1,0:T(8,128)S(1)}, u32[]{:S(2)}, u32[]{:S(2)}) collective-permute-start(f32[128,256]{1,0:T(8,128)S(1)} %get-tuple-element.30.refs_1_), channel_id=1, source_target_pairs={{0,1},{1,0},{2,3},{3,2},{4,5},{5,4},{6,7},{7,6},{8,9},{9,8},{10,11... | collective-permute-start | bytes 393224 | tf_op jit(solution)/shard_map/ppermute | solution.py:470
  78.0 2.3 %inverse.1.refs_0_ = f32[64,128]{1,0:T(8,128)S(1)} custom-call(f32[32,256]{1,0:T(8,128)S(1)} %get-tuple-element.29.gram), custom_call_target="tpu_custom_call" | custom-call | flops 4194304 | bytes 4194304 | tf_op jit(solution)/shard_map/inverse/pallas_call | solution.py:357
  80.3 10.6 %image.3 = bf16[4,8,16,1152]{3,2,1,0:T(8,128)(2,1)S(1)} custom-call(s32[1]{0:T(128)} %bitcast.place, f32[64,128]{1,0:T(8,128)S(1)} %inverse.1.refs_0_, f32[128,256]{1,0:T(8,128)S(1)} %get-tuple-element.30.refs_1_, f32[128,256]{1,0:T(8,128)S(1)} %collective-permute-done.5.refs_2_, bf16[512,2048]{1,0:T(8,128)(2,1)S(1)} %get-tuple-element.23.refs_2_.min_ref.refs_3_, ...), custom_call_target="tpu_custom_call" | custom-call | tf_op jit(solution)/shard_map/image/pallas_call | solution.py:294
  90.9 16.3 %all_to_all.22.parts = bf16[32,16,1152]{2,1,0:T(8,128)(2,1)S(1)} all-to-all(bf16[32,16,1152]{2,1,0:T(8,128)(2,1)S(1)} %bitcast.8), channel_id=1, replica_groups=mesh['dp'=32,'mp'=4] {'dp'}, dimensions={0} | all-to-all | bytes 2359296 | tf_op jit(solution)/shard_map/all_to_all | solution.py:461
  107.5 16.5 %all_to_all.23 = bf16[32,16,1152]{2,1,0:T(8,128)(2,1)S(1)} all-to-all(bf16[32,16,1152]{2,1,0:T(8,128)(2,1)S(1)} %sum_copies.3), channel_id=1, replica_groups=mesh['dp'=32,'mp'=4] {'dp'}, dimensions={0} | all-to-all | bytes 2359296 | tf_op jit(solution)/shard_map/all_to_all | solution.py:462
  123.9 1.9 %raw_send.3 = (f32[160,256]{1,0:T(8,128)S(1)}, bf16[64,2048]{1,0:T(8,128)(2,1)S(1)}, bf16[64,7168]{1,0:T(8,128)(2,1)S(1)}) custom-call(s32[1]{0:T(128)} %bitcast.place, bf16[4,8,16,1152]{3,2,1,0:T(8,128)(2,1)S(1)} %bitcast.7, bf16[512,2048]{1,0:T(8,128)(2,1)S(1)} %get-tuple-element.23.refs_2_.min_ref.refs_3_, ...), custom_call_target="tpu_custom_call" | custom-call | tf_op jit(solution)/shard_map/raw_send/pallas_call | solution.py:199
  125.9 1.5 %raw_keep.3.keep = f32[128,256]{1,0:T(8,128)S(1)} custom-call(s32[1]{0:T(128)} %bitcast.place, bf16[64,2048]{1,0:T(8,128)(2,1)S(1)} %get-tuple-element.31.img_in, bf16[64,7168]{1,0:T(8,128)(2,1)S(1)} %get-tuple-element.32.img_out, bf16[512,2048]{1,0:T(8,128)(2,1)S(1)} %get-tuple-element.23.refs_2_.min_ref.refs_3_, ...), custom_call_target="tpu_custom_call" | custom-call | flops 536870912 | bytes 4194304 | tf_op jit(solution)/shard_map/raw_keep/pallas_call | solution.py:220
  127.5 2.7 %collective-permute-start.7 = (f32[160,256]{1,0:T(8,128)S(1)}, f32[160,256]{1,0:T(8,128)S(1)}, u32[]{:S(2)}, u32[]{:S(2)}) collective-permute-start(f32[160,256]{1,0:T(8,128)S(1)} %near.3), channel_id=1, source_target_pairs={{0,2},{2,0},{1,3},{3,1},{4,6},{6,4},{5,7},{7,5},{8,10},{10,8},{9,1... | collective-permute-start | bytes 491528 | tf_op jit(solution)/shard_map/ppermute | solution.py:467
  130.2 4.1 %collective-permute-done.7.far = f32[160,256]{1,0:T(8,128)S(1)} collective-permute-done((f32[160,256]{1,0:T(8,128)S(1)}, f32[160,256]{1,0:T(8,128)S(1)}, u32[]{:S(2)}, u32[]{:S(2)}) %collective-permute-start.7) | collective-permute-done | bytes 163872 | tf_op jit(solution)/shard_map/ppermute | solution.py:467
  134.3 2.9 %last.1 = (f32[16,64]{1,0:T(8,128)S(1)}, f32[16,64]{1,0:T(8,128)S(1)}, bf16[2,64,192]{2,1,0:T(8,128)(2,1)S(1)}) custom-call(s32[1]{0:T(128)} %bitcast.place, f32[160,256]{1,0:T(8,128)S(1)} %near.3, f32[160,256]{1,0:T(8,128)S(1)} %collective-permute-done.7.far), custom_call_target="tpu_custom_call" | custom-call | tf_op jit(solution)/shard_map/last/pallas_call | solution.py:383
  137.2 1.4 %collective-permute-start.8 = (f32[16,64]{1,0:T(8,128)S(1)}, f32[16,64]{1,0:T(8,128)S(1)}, u32[]{:S(2)}, u32[]{:S(2)}) collective-permute-start(f32[16,64]{1,0:T(8,128)S(1)} %get-tuple-element.35), channel_id=1, source_target_pairs={{0,1},{1,0},{2,3},{3,2},{4,5},{5,4},{6,7},{7,6},{8,9},{9,8},{10,11... | collective-permute-start | bytes 12296 | tf_op jit(solution)/shard_map/ppermute | solution.py:473
  138.7 1.8 %basis.1 = (f32[64,2048]{1,0:T(8,128)}, f32[64,7168]{1,0:T(8,128)}) custom-call(bf16[2,64,192]{2,1,0:T(8,128)(2,1)S(1)} %get-tuple-element.36.split, bf16[64,2048]{1,0:T(8,128)(2,1)S(1)} %get-tuple-element.31.img_in, bf16[64,7168]{1,0:T(8,128)(2,1)S(1)} %get-tuple-element.32.img_out), custom_call_target="tpu_custom_call" | custom-call | tf_op jit(solution)/shard_map/basis/pallas_call | solution.py:432
  (16 shorter events, 3.2 us)
Async XLA Ops:
  6.0 2.4 %collective-permute-start = (f32[128,256]{1,0:T(8,128)S(1)}, f32[128,256]{1,0:T(8,128)S(1)}, u32[]{:S(2)}, u32[]{:S(2)}) collective-permute-start(f32[128,256]{1,0:T(8,128)S(1)} %get-tuple-element.22), channel_id=1, source_target_pairs={{0,1},{1,0},{2,3},{3,2},{4,5},{5,4},{6,7},{7,6},{8,9},{9,8},{10,11... | collective-permute-start | bytes 393224 | tf_op jit(solution)/shard_map/ppermute | solution.py:453
  8.4 6.4 %collective-permute-start.1 = (f32[128,256]{1,0:T(8,128)S(1)}, f32[128,256]{1,0:T(8,128)S(1)}, u32[]{:S(2)}, u32[]{:S(2)}) collective-permute-start(f32[128,256]{1,0:T(8,128)S(1)} %add.2.a), channel_id=1, source_target_pairs={{0,2},{2,0},{1,3},{3,1},{4,6},{6,4},{5,7},{7,5},{8,10},{10,8},{9,1... | collective-permute-start | bytes 393224 | tf_op jit(solution)/shard_map/ppermute | solution.py:454
  14.9 2.1 %collective-permute-start.2 = (bf16[128,256]{1,0:T(8,128)(2,1)S(1)}, bf16[128,256]{1,0:T(8,128)(2,1)S(1)}, u32[]{:S(2)}, u32[]{:S(2)}) collective-permute-start(bf16[128,256]{1,0:T(8,128)(2,1)S(1)} %add.3.refs_0_), channel_id=1, source_target_pairs={{0,1},{1,0},{2,3},{3,2},{4,5},{5,4},{6,7},{7,6},{8,9},{9,8},{10,11... | collective-permute-start | bytes 196616 | tf_op jit(solution)/shard_map/ppermute | solution.py:456
  68.1 1.6 %collective-permute-start.3 = (f32[160,256]{1,0:T(8,128)S(1)}, f32[160,256]{1,0:T(8,128)S(1)}, u32[]{:S(2)}, u32[]{:S(2)}) collective-permute-start(f32[160,256]{1,0:T(8,128)S(1)} %get-tuple-element.28.send), channel_id=1, source_target_pairs={{0,1},{1,0},{2,3},{3,2},{4,5},{5,4},{6,7},{7,6},{8,9},{9,8},{10,11... | collective-permute-start | bytes 491528 | tf_op jit(solution)/shard_map/ppermute | solution.py:464
  69.7 6.8 %collective-permute-start.4 = (f32[160,256]{1,0:T(8,128)S(1)}, f32[160,256]{1,0:T(8,128)S(1)}, u32[]{:S(2)}, u32[]{:S(2)}) collective-permute-start(f32[160,256]{1,0:T(8,128)S(1)} %near.2), channel_id=1, source_target_pairs={{0,2},{2,0},{1,3},{3,1},{4,6},{6,4},{5,7},{7,5},{8,10},{10,8},{9,1... | collective-permute-start | bytes 491528 | tf_op jit(solution)/shard_map/ppermute | solution.py:467
  76.6 3.7 %collective-permute-start.5 = (f32[128,256]{1,0:T(8,128)S(1)}, f32[128,256]{1,0:T(8,128)S(1)}, u32[]{:S(2)}, u32[]{:S(2)}) collective-permute-start(f32[128,256]{1,0:T(8,128)S(1)} %get-tuple-element.30.refs_1_), channel_id=1, source_target_pairs={{0,1},{1,0},{2,3},{3,2},{4,5},{5,4},{6,7},{7,6},{8,9},{9,8},{10,11... | collective-permute-start | bytes 393224 | tf_op jit(solution)/shard_map/ppermute | solution.py:470
  125.8 1.6 %collective-permute-start.6 = (f32[160,256]{1,0:T(8,128)S(1)}, f32[160,256]{1,0:T(8,128)S(1)}, u32[]{:S(2)}, u32[]{:S(2)}) collective-permute-start(f32[160,256]{1,0:T(8,128)S(1)} %get-tuple-element.33.send), channel_id=1, source_target_pairs={{0,1},{1,0},{2,3},{3,2},{4,5},{5,4},{6,7},{7,6},{8,9},{9,8},{10,11... | collective-permute-start | bytes 491528 | tf_op jit(solution)/shard_map/ppermute | solution.py:464
  127.5 6.8 %collective-permute-start.7 = (f32[160,256]{1,0:T(8,128)S(1)}, f32[160,256]{1,0:T(8,128)S(1)}, u32[]{:S(2)}, u32[]{:S(2)}) collective-permute-start(f32[160,256]{1,0:T(8,128)S(1)} %near.3), channel_id=1, source_target_pairs={{0,2},{2,0},{1,3},{3,1},{4,6},{6,4},{5,7},{7,5},{8,10},{10,8},{9,1... | collective-permute-start | bytes 491528 | tf_op jit(solution)/shard_map/ppermute | solution.py:467
  137.2 3.2 %collective-permute-start.8 = (f32[16,64]{1,0:T(8,128)S(1)}, f32[16,64]{1,0:T(8,128)S(1)}, u32[]{:S(2)}, u32[]{:S(2)}) collective-permute-start(f32[16,64]{1,0:T(8,128)S(1)} %get-tuple-element.35), channel_id=1, source_target_pairs={{0,1},{1,0},{2,3},{3,2},{4,5},{5,4},{6,7},{7,6},{8,9},{9,8},{10,11... | collective-permute-start | bytes 12296 | tf_op jit(solution)/shard_map/ppermute | solution.py:473

commit v5 on v4

--- a/solution.py
+++ b/solution.py
@@ -17,12 +17,12 @@
 BF16 = jnp.bfloat16
 
 
-def split3(x):
+def split3(x, axis):
     a = x.astype(BF16)
     rest = x - a.astype(F32)
     b = rest.astype(BF16)
     c = (rest - b.astype(F32)).astype(BF16)
-    return jnp.concatenate([a, b, c], axis=1)
+    return jnp.concatenate([a, b, c], axis=axis)
 
 
 PIVOTS = 8
@@ -228,36 +228,54 @@
     )(place, img_in, img_out, layer_inputs, out_grads, mask)
 
 
-def near_kernel(keep, send, got, out):
+def near_kernel(keep, *refs):
+    *sent, got, near, out = refs
     top = keep.shape[0]
-    out[:top] = keep[...] + got[:top]
-    out[top:] = send[top:] + got[top:]
-
-
-def near_of(keep, send, got):
+    near[:top] = keep[...] + got[:top]
+    out[:top] = near[:top].astype(BF16)
+    if sent:
+        near[top:] = sent[0][top:] + got[top:]
+        out[top:] = split3(near[top:], 0)
+
+
+def near_of(keep, sent, got):
+    top, tokens = keep.shape
+    grams = got.shape[0] - top
     return pl.pallas_call(
         near_kernel,
-        out_shape=jax.ShapeDtypeStruct(send.shape, F32),
-        in_specs=[VMEM] * 3,
-        out_specs=VMEM,
+        out_shape=(
+            jax.ShapeDtypeStruct(got.shape, F32),
+            jax.ShapeDtypeStruct((top + 3 * grams, tokens), BF16),
+        ),
+        in_specs=[VMEM] * (3 if grams else 2),
+        out_specs=(VMEM, VMEM),
         compiler_params=params(4),
         name="near",
-    )(keep, send, got)
-
-
-def add_kernel(a, b, out):
-    out[...] = (a[...] + b[...]).astype(out.dtype)
-
-
-def add(a, b, dtype=F32):
-    return pl.pallas_call(
-        add_kernel,
-        out_shape=jax.ShapeDtypeStruct(a.shape, dtype),
+    )(keep, *([sent] if grams else []), got)
+
+
+def whole_raw(near, far):
+    return near[: 2 * R] + far[: 2 * R].astype(F32)
+
+
+def whole_gram(near, far):
+    a, b, c = (far[2 * R + i * R // 2 : 2 * R + (i + 1) * R // 2].astype(F32) for i in range(3))
+    return near[2 * R :] + (a + b + c)
+
+
+def coords_kernel(near, far, out):
+    out[...] = whole_raw(near, far).astype(BF16)
+
+
+def coords_of(near, far):
+    return pl.pallas_call(
+        coords_kernel,
+        out_shape=jax.ShapeDtypeStruct(far.shape, BF16),
         in_specs=[VMEM, VMEM],
         out_specs=VMEM,
         compiler_params=params(4),
-        name="add",
-    )(a, b)
+        name="coords",
+    )(near, far)
 
 
 def image_kernel(place, *refs):
@@ -333,8 +351,8 @@
 
 
 def total_kernel(near, far, raw, gram):
-    raw[...] = near[: 2 * R] + far[: 2 * R]
-    gram[...] = near[2 * R :] + far[2 * R :]
+    raw[...] = whole_raw(near, far)
+    gram[...] = whole_gram(near, far)
 
 
 def total_of(near, far):
@@ -366,16 +384,16 @@
 
 
 def last_kernel(place, near, far, own, theirs, split, feat):
-    total = near[...] + far[...]
-    inv_in, inv_out = inverses(total[2 * R :])
+    total = whole_raw(near, far)
+    inv_in, inv_out = inverses(whole_gram(near, far))
     co_in = exact_dot(inv_in, total[:R]).astype(BF16)
-    co_out = exact_dot(inv_out, total[R : 2 * R]).astype(BF16)
+    co_out = exact_dot(inv_out, total[R:]).astype(BF16)
     feat[...] = lax.dot_general(co_in, co_out, NT, preferred_element_type=F32) * (1.0 / LEN)
     rows = own.shape[0]
     own[...] = feat[pl.ds(pl.multiple_of(place[0] * rows, rows), rows)]
     theirs[...] = feat[pl.ds(pl.multiple_of((place[0] ^ 1) * rows, rows), rows)]
-    split[0] = split3(inv_in)
-    split[1] = split3(inv_out)
+    split[0] = split3(inv_in, 1)
+    split[1] = split3(inv_out, 1)
 
 
 def last_of(place, near, far, count):
@@ -450,9 +468,8 @@
     send, keep, layer_inputs, out_grads, mask = raw_first(
         place, start_in, start_out, layer_inputs, out_grads, mask
     )
-    near = add(keep, lax.ppermute(send, "mp", CORE_SWAP))
-    far = lax.ppermute(near, "mp", CHIP_SWAP)
-    mine = add(near, far, BF16)
+    near, out = near_of(keep, send, lax.ppermute(send, "mp", CORE_SWAP))
+    mine = coords_of(near, lax.ppermute(out, "mp", CHIP_SWAP))
     coords = (mine, lax.ppermute(mine, "mp", CORE_SWAP))
     for step in range(ITERS):
         parts = image_of(place, coords, layer_inputs, out_grads)
@@ -463,8 +480,8 @@
         send, img_in, img_out = raw_send(place, image, layer_inputs, out_grads, mask)
         got = lax.ppermute(send, "mp", CORE_SWAP)
         keep = raw_keep(place, img_in, img_out, layer_inputs, out_grads, mask)
-        near = near_of(keep, send, got)
-        far = lax.ppermute(near, "mp", CHIP_SWAP)
+        near, out = near_of(keep, send, got)
+        far = lax.ppermute(out, "mp", CHIP_SWAP)
         if step + 1 < ITERS:
             raw, gram = total_of(near, far)
             other = lax.ppermute(raw, "mp", CORE_SWAP)

time: 141 us -> 138 us (0.979)
  waiting for transfers between devices: 13.5 us -> 9.74 us
    ppermute x4, waiting for transfers between devices: 12.6 us -> 8.83 us  [the longest x2 6.19 us: shards(): far = lax.ppermute(out, 'mp', CHIP_SWAP)]
where the time goes in v5:
time: 138 us
  blocking collectives  71.6 us (52%)
  Pallas kernels  41.1 us (30%)
  starting transfers between devices  14.5 us (11%)
  waiting for transfers between devices  9.74 us (7%)
    all_to_all x2, blocking collectives, shards(): parts = lax.all_to_all(parts, 'dp', 0, 0)  38.1 us
    all_to_all x2, blocking collectives, shards(): image = lax.all_to_all(sum_copies(parts), 'dp', 0, 0).reshape(grid)  33.5 us
    pallas_call x2, Pallas kernels, image_of(): pl.pallas_call(image_kernel, out_shape=jax.ShapeDtypeStruct((GROUPS, step...  20.8 us
    ppermute x2, waiting for transfers between devices, shards(): far = lax.ppermute(out, 'mp', CHIP_SWAP)  6.19 us
    ppermute x2, starting transfers between devices, shards(): far = lax.ppermute(out, 'mp', CHIP_SWAP)  5.4 us
    pallas_call x1, Pallas kernels, raw_first(): pl.pallas_call(first_kernel, out_shape=(shape, shape, jax.ShapeDtypeStruc...  5.34 us
    pallas_call x2, Pallas kernels, raw_send(): pl.pallas_call(send_kernel, out_shape=(jax.ShapeDtypeStruct((2 * R + R //...  3.74 us
    ppermute x1, starting transfers between devices, shards(): mine = coords_of(near, lax.ppermute(out, 'mp', CHIP_SWAP))  3.11 us
  transfers between devices with their start and end apart: 9, of which 5 were waited for; matrix products, arithmetic and copies ran while one was open for 0% of the time, Pallas kernels for 5%

profile of v5, /device:TPU:1, one launch (start us, length us, event | category | flops | bytes accessed | tf_op | source)
XLA Modules:
  0.0 137.8 jit_solution(13643802350199483866)
XLA Ops:
  0.6 5.3 %raw_first.1 = (f32[128,256]{1,0:T(8,128)S(1)}, f32[128,256]{1,0:T(8,128)S(1)}, bf16[512,2048]{1,0:T(8,128)(2,1)S(1)}, bf16[512,7168]{1,0:T(8,128)(2,1)S(1)}, f32[1,512]{1,0:T(1,128)S(1)}) custom-call(s32[1]{0:T(128)} %bitcast.place, s32[64,2048]{1,0:T(8,128)} %bin_hbm.1, s32[64,7168]{1,0:T(8,128)} %bout_hbm.1, bf16[512,2048]{1,0:T(8,128)(2,1)} %min_hbm.1, ...), custom_call_target="tpu_custom_call" | custom-call | tf_op jit(solution)/shard_map/raw_first/pallas_call | solution.py:147
  6.0 1.5 %collective-permute-start = (f32[128,256]{1,0:T(8,128)S(1)}, f32[128,256]{1,0:T(8,128)S(1)}, u32[]{:S(2)}, u32[]{:S(2)}) collective-permute-start(f32[128,256]{1,0:T(8,128)S(1)} %get-tuple-element.28), channel_id=1, source_target_pairs={{0,1},{1,0},{2,3},{3,2},{4,5},{5,4},{6,7},{7,6},{8,9},{9,8},{10,11... | collective-permute-start | bytes 393224 | tf_op jit(solution)/shard_map/ppermute | solution.py:471
  8.5 3.1 %collective-permute-start.1 = (bf16[128,256]{1,0:T(8,128)(2,1)S(1)}, bf16[128,256]{1,0:T(8,128)(2,1)S(1)}, u32[]{:S(2)}, u32[]{:S(2)}) collective-permute-start(bf16[128,256]{1,0:T(8,128)(2,1)S(1)} %get-tuple-element.30), channel_id=1, source_target_pairs={{0,2},{2,0},{1,3},{3,1},{4,6},{6,4},{5,7},{7,5},{8,10},{10,8},{9,1... | collective-permute-start | bytes 196616 | tf_op jit(solution)/shard_map/ppermute | solution.py:472
  11.6 1.7 %collective-permute-done.1.far = bf16[128,256]{1,0:T(8,128)(2,1)S(1)} collective-permute-done((bf16[128,256]{1,0:T(8,128)(2,1)S(1)}, bf16[128,256]{1,0:T(8,128)(2,1)S(1)}, u32[]{:S(2)}, u32[]{:S(2)}) %collective-permute-start.1) | collective-permute-done | bytes 65568 | tf_op jit(solution)/shard_map/ppermute | solution.py:472
  13.2 1.5 %collective-permute-start.2 = (bf16[128,256]{1,0:T(8,128)(2,1)S(1)}, bf16[128,256]{1,0:T(8,128)(2,1)S(1)}, u32[]{:S(2)}, u32[]{:S(2)}) collective-permute-start(bf16[128,256]{1,0:T(8,128)(2,1)S(1)} %coords.1.refs_0_), channel_id=1, source_target_pairs={{0,1},{1,0},{2,3},{3,2},{4,5},{5,4},{6,7},{7,6},{8,9},{9,8},{10,11... | collective-permute-start | bytes 196616 | tf_op jit(solution)/shard_map/ppermute | solution.py:473
  15.7 10.3 %image.2 = bf16[4,8,16,1152]{3,2,1,0:T(8,128)(2,1)S(1)} custom-call(s32[1]{0:T(128)} %bitcast.place, bf16[128,256]{1,0:T(8,128)(2,1)S(1)} %coords.1.refs_0_, bf16[128,256]{1,0:T(8,128)(2,1)S(1)} %collective-permute-done.2.refs_1_, bf16[512,2048]{1,0:T(8,128)(2,1)S(1)} %get-tuple-element.31.refs_2_.min_ref.refs_3_, ...), custom_call_target="tpu_custom_call" | custom-call | tf_op jit(solution)/shard_map/image/pallas_call | solution.py:312
  25.9 21.7 %all_to_all.20.parts = bf16[32,16,1152]{2,1,0:T(8,128)(2,1)S(1)} all-to-all(bf16[32,16,1152]{2,1,0:T(8,128)(2,1)S(1)} %bitcast.9), channel_id=1, replica_groups=mesh['dp'=32,'mp'=4] {'dp'}, dimensions={0} | all-to-all | bytes 2359296 | tf_op jit(solution)/shard_map/all_to_all | solution.py:478
  47.9 17.0 %all_to_all.21 = bf16[32,16,1152]{2,1,0:T(8,128)(2,1)S(1)} all-to-all(bf16[32,16,1152]{2,1,0:T(8,128)(2,1)S(1)} %sum_copies.2), channel_id=1, replica_groups=mesh['dp'=32,'mp'=4] {'dp'}, dimensions={0} | all-to-all | bytes 2359296 | tf_op jit(solution)/shard_map/all_to_all | solution.py:479
  64.9 1.9 %raw_send.2 = (f32[160,256]{1,0:T(8,128)S(1)}, bf16[64,2048]{1,0:T(8,128)(2,1)S(1)}, bf16[64,7168]{1,0:T(8,128)(2,1)S(1)}) custom-call(s32[1]{0:T(128)} %bitcast.place, bf16[4,8,16,1152]{3,2,1,0:T(8,128)(2,1)S(1)} %bitcast.6, bf16[512,2048]{1,0:T(8,128)(2,1)S(1)} %get-tuple-element.31.refs_2_.min_ref.refs_3_, ...), custom_call_target="tpu_custom_call" | custom-call | tf_op jit(solution)/shard_map/raw_send/pallas_call | solution.py:199
  66.9 1.5 %raw_keep.2.keep = f32[128,256]{1,0:T(8,128)S(1)} custom-call(s32[1]{0:T(128)} %bitcast.place, bf16[64,2048]{1,0:T(8,128)(2,1)S(1)} %get-tuple-element.34.img_in, bf16[64,7168]{1,0:T(8,128)(2,1)S(1)} %get-tuple-element.35.img_out, bf16[512,2048]{1,0:T(8,128)(2,1)S(1)} %get-tuple-element.31.refs_2_.min_ref.refs_3_, ...), custom_call_target="tpu_custom_call" | custom-call | flops 536870912 | bytes 4194304 | tf_op jit(solution)/shard_map/raw_keep/pallas_call | solution.py:220
  68.5 2.7 %collective-permute-start.4 = (bf16[224,256]{1,0:T(8,128)(2,1)S(1)}, bf16[224,256]{1,0:T(8,128)(2,1)S(1)}, u32[]{:S(2)}, u32[]{:S(2)}) collective-permute-start(bf16[224,256]{1,0:T(8,128)(2,1)S(1)} %get-tuple-element.38), channel_id=1, source_target_pairs={{0,2},{2,0},{1,3},{3,1},{4,6},{6,4},{5,7},{7,5},{8,10},{10,8},{9,1... | collective-permute-start | bytes 344072 | tf_op jit(solution)/shard_map/ppermute | solution.py:484
  71.2 3.1 %collective-permute-done.4.far = bf16[224,256]{1,0:T(8,128)(2,1)S(1)} collective-permute-done((bf16[224,256]{1,0:T(8,128)(2,1)S(1)}, bf16[224,256]{1,0:T(8,128)(2,1)S(1)}, u32[]{:S(2)}, u32[]{:S(2)}) %collective-permute-start.4) | collective-permute-done | bytes 114720 | tf_op jit(solution)/shard_map/ppermute | solution.py:484
  74.3 1.4 %collective-permute-start.5 = (f32[128,256]{1,0:T(8,128)S(1)}, f32[128,256]{1,0:T(8,128)S(1)}, u32[]{:S(2)}, u32[]{:S(2)}) collective-permute-start(f32[128,256]{1,0:T(8,128)S(1)} %get-tuple-element.40.refs_1_), channel_id=1, source_target_pairs={{0,1},{1,0},{2,3},{3,2},{4,5},{5,4},{6,7},{7,6},{8,9},{9,8},{10,11... | collective-permute-start | bytes 393224 | tf_op jit(solution)/shard_map/ppermute | solution.py:487
  75.7 2.3 %inverse.1.refs_0_ = f32[64,128]{1,0:T(8,128)S(1)} custom-call(f32[32,256]{1,0:T(8,128)S(1)} %get-tuple-element.39.gram), custom_call_target="tpu_custom_call" | custom-call | flops 4194304 | bytes 4194304 | tf_op jit(solution)/shard_map/inverse/pallas_call | solution.py:375
  78.0 10.6 %image.3 = bf16[4,8,16,1152]{3,2,1,0:T(8,128)(2,1)S(1)} custom-call(s32[1]{0:T(128)} %bitcast.place, f32[64,128]{1,0:T(8,128)S(1)} %inverse.1.refs_0_, f32[128,256]{1,0:T(8,128)S(1)} %get-tuple-element.40.refs_1_, f32[128,256]{1,0:T(8,128)S(1)} %collective-permute-done.5.refs_2_, bf16[512,2048]{1,0:T(8,128)(2,1)S(1)} %get-tuple-element.31.refs_2_.min_ref.refs_3_, ...), custom_call_target="tpu_custom_call" | custom-call | tf_op jit(solution)/shard_map/image/pallas_call | solution.py:312
  88.6 16.3 %all_to_all.22.parts = bf16[32,16,1152]{2,1,0:T(8,128)(2,1)S(1)} all-to-all(bf16[32,16,1152]{2,1,0:T(8,128)(2,1)S(1)} %bitcast.8), channel_id=1, replica_groups=mesh['dp'=32,'mp'=4] {'dp'}, dimensions={0} | all-to-all | bytes 2359296 | tf_op jit(solution)/shard_map/all_to_all | solution.py:478
  105.1 16.5 %all_to_all.23 = bf16[32,16,1152]{2,1,0:T(8,128)(2,1)S(1)} all-to-all(bf16[32,16,1152]{2,1,0:T(8,128)(2,1)S(1)} %sum_copies.3), channel_id=1, replica_groups=mesh['dp'=32,'mp'=4] {'dp'}, dimensions={0} | all-to-all | bytes 2359296 | tf_op jit(solution)/shard_map/all_to_all | solution.py:479
  121.6 1.9 %raw_send.3 = (f32[160,256]{1,0:T(8,128)S(1)}, bf16[64,2048]{1,0:T(8,128)(2,1)S(1)}, bf16[64,7168]{1,0:T(8,128)(2,1)S(1)}) custom-call(s32[1]{0:T(128)} %bitcast.place, bf16[4,8,16,1152]{3,2,1,0:T(8,128)(2,1)S(1)} %bitcast.7, bf16[512,2048]{1,0:T(8,128)(2,1)S(1)} %get-tuple-element.31.refs_2_.min_ref.refs_3_, ...), custom_call_target="tpu_custom_call" | custom-call | tf_op jit(solution)/shard_map/raw_send/pallas_call | solution.py:199
  123.6 1.5 %raw_keep.3.keep = f32[128,256]{1,0:T(8,128)S(1)} custom-call(s32[1]{0:T(128)} %bitcast.place, bf16[64,2048]{1,0:T(8,128)(2,1)S(1)} %get-tuple-element.41.img_in, bf16[64,7168]{1,0:T(8,128)(2,1)S(1)} %get-tuple-element.42.img_out, bf16[512,2048]{1,0:T(8,128)(2,1)S(1)} %get-tuple-element.31.refs_2_.min_ref.refs_3_, ...), custom_call_target="tpu_custom_call" | custom-call | flops 536870912 | bytes 4194304 | tf_op jit(solution)/shard_map/raw_keep/pallas_call | solution.py:220
  125.2 2.7 %collective-permute-start.7 = (bf16[224,256]{1,0:T(8,128)(2,1)S(1)}, bf16[224,256]{1,0:T(8,128)(2,1)S(1)}, u32[]{:S(2)}, u32[]{:S(2)}) collective-permute-start(bf16[224,256]{1,0:T(8,128)(2,1)S(1)} %get-tuple-element.45), channel_id=1, source_target_pairs={{0,2},{2,0},{1,3},{3,1},{4,6},{6,4},{5,7},{7,5},{8,10},{10,8},{9,1... | collective-permute-start | bytes 344072 | tf_op jit(solution)/shard_map/ppermute | solution.py:484
  127.9 3.1 %collective-permute-done.7.far = bf16[224,256]{1,0:T(8,128)(2,1)S(1)} collective-permute-done((bf16[224,256]{1,0:T(8,128)(2,1)S(1)}, bf16[224,256]{1,0:T(8,128)(2,1)S(1)}, u32[]{:S(2)}, u32[]{:S(2)}) %collective-permute-start.7) | collective-permute-done | bytes 114720 | tf_op jit(solution)/shard_map/ppermute | solution.py:484
  131.0 2.9 %last.1 = (f32[16,64]{1,0:T(8,128)S(1)}, f32[16,64]{1,0:T(8,128)S(1)}, bf16[2,64,192]{2,1,0:T(8,128)(2,1)S(1)}) custom-call(s32[1]{0:T(128)} %bitcast.place, f32[160,256]{1,0:T(8,128)S(1)} %get-tuple-element.44.near, bf16[224,256]{1,0:T(8,128)(2,1)S(1)} %collective-permute-done.7.far), custom_call_target="tpu_custom_call" | custom-call | tf_op jit(solution)/shard_map/last/pallas_call | solution.py:401
  133.9 1.4 %collective-permute-start.8 = (f32[16,64]{1,0:T(8,128)S(1)}, f32[16,64]{1,0:T(8,128)S(1)}, u32[]{:S(2)}, u32[]{:S(2)}) collective-permute-start(f32[16,64]{1,0:T(8,128)S(1)} %get-tuple-element.47), channel_id=1, source_target_pairs={{0,1},{1,0},{2,3},{3,2},{4,5},{5,4},{6,7},{7,6},{8,9},{9,8},{10,11... | collective-permute-start | bytes 12296 | tf_op jit(solution)/shard_map/ppermute | solution.py:490
  135.3 1.8 %basis.1 = (f32[64,2048]{1,0:T(8,128)}, f32[64,7168]{1,0:T(8,128)}) custom-call(bf16[2,64,192]{2,1,0:T(8,128)(2,1)S(1)} %get-tuple-element.48.split, bf16[64,2048]{1,0:T(8,128)(2,1)S(1)} %get-tuple-element.41.img_in, bf16[64,7168]{1,0:T(8,128)(2,1)S(1)} %get-tuple-element.42.img_out), custom_call_target="tpu_custom_call" | custom-call | tf_op jit(solution)/shard_map/basis/pallas_call | solution.py:450
  (16 shorter events, 3.2 us)
Async XLA Ops:
  6.0 2.4 %collective-permute-start = (f32[128,256]{1,0:T(8,128)S(1)}, f32[128,256]{1,0:T(8,128)S(1)}, u32[]{:S(2)}, u32[]{:S(2)}) collective-permute-start(f32[128,256]{1,0:T(8,128)S(1)} %get-tuple-element.28), channel_id=1, source_target_pairs={{0,1},{1,0},{2,3},{3,2},{4,5},{5,4},{6,7},{7,6},{8,9},{9,8},{10,11... | collective-permute-start | bytes 393224 | tf_op jit(solution)/shard_map/ppermute | solution.py:471
  8.5 4.8 %collective-permute-start.1 = (bf16[128,256]{1,0:T(8,128)(2,1)S(1)}, bf16[128,256]{1,0:T(8,128)(2,1)S(1)}, u32[]{:S(2)}, u32[]{:S(2)}) collective-permute-start(bf16[128,256]{1,0:T(8,128)(2,1)S(1)} %get-tuple-element.30), channel_id=1, source_target_pairs={{0,2},{2,0},{1,3},{3,1},{4,6},{6,4},{5,7},{7,5},{8,10},{10,8},{9,1... | collective-permute-start | bytes 196616 | tf_op jit(solution)/shard_map/ppermute | solution.py:472
  13.2 2.4 %collective-permute-start.2 = (bf16[128,256]{1,0:T(8,128)(2,1)S(1)}, bf16[128,256]{1,0:T(8,128)(2,1)S(1)}, u32[]{:S(2)}, u32[]{:S(2)}) collective-permute-start(bf16[128,256]{1,0:T(8,128)(2,1)S(1)} %coords.1.refs_0_), channel_id=1, source_target_pairs={{0,1},{1,0},{2,3},{3,2},{4,5},{5,4},{6,7},{7,6},{8,9},{9,8},{10,11... | collective-permute-start | bytes 196616 | tf_op jit(solution)/shard_map/ppermute | solution.py:473
  66.8 1.6 %collective-permute-start.3 = (f32[160,256]{1,0:T(8,128)S(1)}, f32[160,256]{1,0:T(8,128)S(1)}, u32[]{:S(2)}, u32[]{:S(2)}) collective-permute-start(f32[160,256]{1,0:T(8,128)S(1)} %get-tuple-element.36.refs_0_), channel_id=1, source_target_pairs={{0,1},{1,0},{2,3},{3,2},{4,5},{5,4},{6,7},{7,6},{8,9},{9,8},{10,11... | collective-permute-start | bytes 491528 | tf_op jit(solution)/shard_map/ppermute | solution.py:481
  68.5 5.8 %collective-permute-start.4 = (bf16[224,256]{1,0:T(8,128)(2,1)S(1)}, bf16[224,256]{1,0:T(8,128)(2,1)S(1)}, u32[]{:S(2)}, u32[]{:S(2)}) collective-permute-start(bf16[224,256]{1,0:T(8,128)(2,1)S(1)} %get-tuple-element.38), channel_id=1, source_target_pairs={{0,2},{2,0},{1,3},{3,1},{4,6},{6,4},{5,7},{7,5},{8,10},{10,8},{9,1... | collective-permute-start | bytes 344072 | tf_op jit(solution)/shard_map/ppermute | solution.py:484
  74.3 3.7 %collective-permute-start.5 = (f32[128,256]{1,0:T(8,128)S(1)}, f32[128,256]{1,0:T(8,128)S(1)}, u32[]{:S(2)}, u32[]{:S(2)}) collective-permute-start(f32[128,256]{1,0:T(8,128)S(1)} %get-tuple-element.40.refs_1_), channel_id=1, source_target_pairs={{0,1},{1,0},{2,3},{3,2},{4,5},{5,4},{6,7},{7,6},{8,9},{9,8},{10,11... | collective-permute-start | bytes 393224 | tf_op jit(solution)/shard_map/ppermute | solution.py:487
  123.5 1.6 %collective-permute-start.6 = (f32[160,256]{1,0:T(8,128)S(1)}, f32[160,256]{1,0:T(8,128)S(1)}, u32[]{:S(2)}, u32[]{:S(2)}) collective-permute-start(f32[160,256]{1,0:T(8,128)S(1)} %get-tuple-element.43.refs_0_), channel_id=1, source_target_pairs={{0,1},{1,0},{2,3},{3,2},{4,5},{5,4},{6,7},{7,6},{8,9},{9,8},{10,11... | collective-permute-start | bytes 491528 | tf_op jit(solution)/shard_map/ppermute | solution.py:481
  125.2 5.8 %collective-permute-start.7 = (bf16[224,256]{1,0:T(8,128)(2,1)S(1)}, bf16[224,256]{1,0:T(8,128)(2,1)S(1)}, u32[]{:S(2)}, u32[]{:S(2)}) collective-permute-start(bf16[224,256]{1,0:T(8,128)(2,1)S(1)} %get-tuple-element.45), channel_id=1, source_target_pairs={{0,2},{2,0},{1,3},{3,1},{4,6},{6,4},{5,7},{7,5},{8,10},{10,8},{9,1... | collective-permute-start | bytes 344072 | tf_op jit(solution)/shard_map/ppermute | solution.py:484
  133.9 3.2 %collective-permute-start.8 = (f32[16,64]{1,0:T(8,128)S(1)}, f32[16,64]{1,0:T(8,128)S(1)}, u32[]{:S(2)}, u32[]{:S(2)}) collective-permute-start(f32[16,64]{1,0:T(8,128)S(1)} %get-tuple-element.47), channel_id=1, source_target_pairs={{0,1},{1,0},{2,3},{3,2},{4,5},{5,4},{6,7},{7,6},{8,9},{9,8},{10,11... | collective-permute-start | bytes 12296 | tf_op jit(solution)/shard_map/ppermute | solution.py:490

commit v6 on v5

--- a/solution.py
+++ b/solution.py
@@ -383,79 +383,49 @@
     )(gram)
 
 
-def last_kernel(place, near, far, own, theirs, split, feat):
-    total = whole_raw(near, far)
-    inv_in, inv_out = inverses(whole_gram(near, far))
-    co_in = exact_dot(inv_in, total[:R]).astype(BF16)
-    co_out = exact_dot(inv_out, total[R:]).astype(BF16)
-    feat[...] = lax.dot_general(co_in, co_out, NT, preferred_element_type=F32) * (1.0 / LEN)
-    rows = own.shape[0]
-    own[...] = feat[pl.ds(pl.multiple_of(place[0] * rows, rows), rows)]
-    theirs[...] = feat[pl.ds(pl.multiple_of((place[0] ^ 1) * rows, rows), rows)]
-    split[0] = split3(inv_in, 1)
-    split[1] = split3(inv_out, 1)
-
-
-def last_of(place, near, far, count):
-    block = jax.ShapeDtypeStruct((R // count, R), F32)
-    return pl.pallas_call(
-        last_kernel,
-        out_shape=(block, block, jax.ShapeDtypeStruct((2, R, 3 * R), BF16)),
-        in_specs=[SMEM, VMEM, VMEM],
-        out_specs=(VMEM,) * 3,
-        scratch_shapes=[pltpu.VMEM((R, R), F32)],
-        compiler_params=params(8),
-        name="last",
-    )(place, near, far)
-
-
-def features_kernel(place, own, got, out):
-    rows = own.shape[0]
-    own = jnp.concatenate([own[r : r + 1] for r in range(rows)], axis=1)
-    got = jnp.concatenate([got[r : r + 1] for r in range(rows)], axis=1)
-    even = (place[0] & 1) == 0
-    out[0:1] = jnp.where(even, own, got)
-    out[1:2] = jnp.where(even, got, own)
-
-
-def features_of(place, own, got):
-    return pl.pallas_call(
-        features_kernel,
-        out_shape=jax.ShapeDtypeStruct((2, own.size), F32),
-        in_specs=[SMEM, VMEM, VMEM],
-        out_specs=VMEM,
-        compiler_params=params(4),
-        name="features",
-    )(place, own, got)
-
-
-def basis_kernel(split, img_in, img_out, in_hbm, out_hbm, b_in, b_out, sems):
+def last_kernel(place, inverse, mine, other, img_in, img_out, *refs):
+    feat, in_hbm, out_hbm, b_in, b_out, sems = refs
     steps = sems.shape[0]
     copies = []
-    for h in range(steps):
-        for n, (img, own, whole) in enumerate([(img_in, b_in, in_hbm), (img_out, b_out, out_hbm)]):
-            width = own.shape[1] // steps
+    for n, (img, own, whole) in enumerate([(img_in, b_in, in_hbm), (img_out, b_out, out_hbm)]):
+        split = split3(inverse[:, n * R : (n + 1) * R], 1)
+        width = own.shape[1] // steps
+        for h in range(steps):
             cols = slice(h * width, (h + 1) * width)
             part = jnp.concatenate([img[:, cols]] * 3, axis=0)
-            own[:, cols] = jnp.dot(split[n], part, preferred_element_type=F32)
-            copy = pltpu.make_async_copy(own.at[:, cols], whole.at[:, cols], sems.at[h, n])
-            copy.start()
-            copies.append(copy)
+            own[:, cols] = jnp.dot(split, part, preferred_element_type=F32)
+            copies.append(
+                pltpu.make_async_copy(own.at[:, cols], whole.at[:, cols], sems.at[h, n])
+            )
+            if len(copies) > 1:
+                copies[-2].start()
+    copies[-1].start()
+    block = feat.shape[1] // R
+    inv_in = inverse[pl.ds(pl.multiple_of(place[0] * block, block), block), :][:, :R]
+    found = []
+    for raw in (mine, other):
+        proj_in = exact_dot(inv_in, raw[:R]).astype(BF16)
+        proj_out = exact_dot(inverse[:, R:], raw[R:]).astype(BF16)
+        one = lax.dot_general(proj_in, proj_out, NT, preferred_element_type=F32) * (1.0 / LEN)
+        found.append(jnp.concatenate([one[r : r + 1] for r in range(block)], axis=1))
+    even = (place[0] & 1) == 0
+    feat[0:1] = jnp.where(even, found[0], found[1])
+    feat[1:2] = jnp.where(even, found[1], found[0])
     for copy in copies:
         copy.wait()
 
 
-def basis_of(split, img_in, img_out):
+def last_of(place, coords, img_in, img_out, count):
     shapes = (img_in.shape, img_out.shape)
     return pl.pallas_call(
-        basis_kernel,
-        out_shape=tuple(jax.ShapeDtypeStruct(s, F32) for s in shapes),
-        in_specs=[VMEM] * 3,
-        out_specs=(HBM, HBM),
+        last_kernel,
+        out_shape=tuple(jax.ShapeDtypeStruct(s, F32) for s in ((2, R // count * R), *shapes)),
+        in_specs=[SMEM] + [VMEM] * 5,
+        out_specs=(VMEM, HBM, HBM),
         scratch_shapes=[pltpu.VMEM(s, F32) for s in shapes] + [pltpu.SemaphoreType.DMA((4, 2))],
         compiler_params=params(8),
-        name="basis",
-    )(split, img_in, img_out)
+        name="last",
+    )(place, *coords, img_in, img_out)
 
 
 CORE_SWAP = [(0, 1), (1, 0), (2, 3), (3, 2)]
@@ -482,14 +452,10 @@
         keep = raw_keep(place, img_in, img_out, layer_inputs, out_grads, mask)
         near, out = near_of(keep, send, got)
         far = lax.ppermute(out, "mp", CHIP_SWAP)
-        if step + 1 < ITERS:
-            raw, gram = total_of(near, far)
-            other = lax.ppermute(raw, "mp", CORE_SWAP)
-            coords = (inverse_of(gram), raw, other)
-    own, theirs, split = last_of(place, near, far, lax.axis_size("mp"))
-    got = lax.ppermute(theirs, "mp", CORE_SWAP)
-    basis_in, basis_out = basis_of(split, img_in, img_out)
-    return (features_of(place, own, got), basis_in, basis_out)
+        raw, gram = total_of(near, far)
+        other = lax.ppermute(raw, "mp", CORE_SWAP)
+        coords = (inverse_of(gram), raw, other)
+    return last_of(place, coords, img_in, img_out, lax.axis_size("mp"))
 
 
 def solution(mesh):

time: 138 us -> 138 us (level)
    pallas_call x3 -> x1, Pallas kernels: 5.36 us -> 2.56 us  [last_of(): pl.pallas_call(last_kernel, out_shape=tuple((jax.ShapeDtypeStruct(s, F32)...]
    pallas_call x1 -> x2, Pallas kernels: 2.29 us -> 4.59 us  [inverse_of(): pl.pallas_call(inverse_kernel, out_shape=jax.ShapeDtypeStruct((R, 2 * R),...]
    ppermute x1 -> x2, starting transfers between devices: 1.43 us -> 2.86 us  [shards(): other = lax.ppermute(raw, 'mp', CORE_SWAP)]
    ppermute x1 -> x0, starting transfers between devices: 1.42 us -> none  [shards(): got = lax.ppermute(theirs, 'mp', CORE_SWAP)]
  transfers between devices with their start and end apart: 9 -> 9, of which waited for: 5 -> 5; matrix products, arithmetic and copies ran while one was open for 0% -> 0% of each run, Pallas kernels for 5% -> 6%
where the time goes in v6:
time: 138 us; the launch traced here: 137 us
  blocking collectives  71.6 us (52%)
  Pallas kernels  40.7 us (29%)
  starting transfers between devices  14.5 us (11%)
  waiting for transfers between devices  9.74 us (7%)
    all_to_all x2, blocking collectives, shards(): parts = lax.all_to_all(parts, 'dp', 0, 0)  38.1 us
    all_to_all x2, blocking collectives, shards(): image = lax.all_to_all(sum_copies(parts), 'dp', 0, 0).reshape(grid)  33.5 us
    pallas_call x2, Pallas kernels, image_of(): pl.pallas_call(image_kernel, out_shape=jax.ShapeDtypeStruct((GROUPS, step...  20.8 us
    ppermute x2, waiting for transfers between devices, shards(): far = lax.ppermute(out, 'mp', CHIP_SWAP)  6.19 us
    ppermute x2, starting transfers between devices, shards(): far = lax.ppermute(out, 'mp', CHIP_SWAP)  5.4 us
    pallas_call x1, Pallas kernels, raw_first(): pl.pallas_call(first_kernel, out_shape=(shape, shape, jax.ShapeDtypeStruc...  5.33 us
    pallas_call x2, Pallas kernels, inverse_of(): pl.pallas_call(inverse_kernel, out_shape=jax.ShapeDtypeStruct((R, 2 * R),...  4.59 us
    pallas_call x2, Pallas kernels, raw_send(): pl.pallas_call(send_kernel, out_shape=(jax.ShapeDtypeStruct((2 * R + R //...  3.74 us
  transfers between devices with their start and end apart: 9, of which 5 were waited for; matrix products, arithmetic and copies ran while one was open for 0% of the time, Pallas kernels for 6%

profile of v6, /device:TPU:1, one launch (start us, length us, event | category | flops | bytes accessed | tf_op | source)
XLA Modules:
  0.0 137.4 jit_solution(11597945389315483086)
XLA Ops:
  0.6 5.3 %raw_first.1 = (f32[128,256]{1,0:T(8,128)S(1)}, f32[128,256]{1,0:T(8,128)S(1)}, bf16[512,2048]{1,0:T(8,128)(2,1)S(1)}, bf16[512,7168]{1,0:T(8,128)(2,1)S(1)}, f32[1,512]{1,0:T(1,128)S(1)}) custom-call(s32[1]{0:T(128)} %bitcast.place, s32[64,2048]{1,0:T(8,128)} %bin_hbm.1, s32[64,7168]{1,0:T(8,128)} %bout_hbm.1, bf16[512,2048]{1,0:T(8,128)(2,1)} %min_hbm.1, ...), custom_call_target="tpu_custom_call" | custom-call | tf_op jit(solution)/shard_map/raw_first/pallas_call | solution.py:147
  6.0 1.5 %collective-permute-start = (f32[128,256]{1,0:T(8,128)S(1)}, f32[128,256]{1,0:T(8,128)S(1)}, u32[]{:S(2)}, u32[]{:S(2)}) collective-permute-start(f32[128,256]{1,0:T(8,128)S(1)} %get-tuple-element.25), channel_id=1, source_target_pairs={{0,1},{1,0},{2,3},{3,2},{4,5},{5,4},{6,7},{7,6},{8,9},{9,8},{10,11... | collective-permute-start | bytes 393224 | tf_op jit(solution)/shard_map/ppermute | solution.py:441
  8.5 3.1 %collective-permute-start.1 = (bf16[128,256]{1,0:T(8,128)(2,1)S(1)}, bf16[128,256]{1,0:T(8,128)(2,1)S(1)}, u32[]{:S(2)}, u32[]{:S(2)}) collective-permute-start(bf16[128,256]{1,0:T(8,128)(2,1)S(1)} %get-tuple-element.27), channel_id=1, source_target_pairs={{0,2},{2,0},{1,3},{3,1},{4,6},{6,4},{5,7},{7,5},{8,10},{10,8},{9,1... | collective-permute-start | bytes 196616 | tf_op jit(solution)/shard_map/ppermute | solution.py:442
  11.6 1.7 %collective-permute-done.1.far = bf16[128,256]{1,0:T(8,128)(2,1)S(1)} collective-permute-done((bf16[128,256]{1,0:T(8,128)(2,1)S(1)}, bf16[128,256]{1,0:T(8,128)(2,1)S(1)}, u32[]{:S(2)}, u32[]{:S(2)}) %collective-permute-start.1) | collective-permute-done | bytes 65568 | tf_op jit(solution)/shard_map/ppermute | solution.py:442
  13.2 1.5 %collective-permute-start.2 = (bf16[128,256]{1,0:T(8,128)(2,1)S(1)}, bf16[128,256]{1,0:T(8,128)(2,1)S(1)}, u32[]{:S(2)}, u32[]{:S(2)}) collective-permute-start(bf16[128,256]{1,0:T(8,128)(2,1)S(1)} %coords.1.refs_0_), channel_id=1, source_target_pairs={{0,1},{1,0},{2,3},{3,2},{4,5},{5,4},{6,7},{7,6},{8,9},{9,8},{10,11... | collective-permute-start | bytes 196616 | tf_op jit(solution)/shard_map/ppermute | solution.py:443
  15.7 10.3 %image.2 = bf16[4,8,16,1152]{3,2,1,0:T(8,128)(2,1)S(1)} custom-call(s32[1]{0:T(128)} %bitcast.place, bf16[128,256]{1,0:T(8,128)(2,1)S(1)} %coords.1.refs_0_, bf16[128,256]{1,0:T(8,128)(2,1)S(1)} %collective-permute-done.2.refs_1_, bf16[512,2048]{1,0:T(8,128)(2,1)S(1)} %get-tuple-element.28.refs_2_.min_ref.refs_3_, ...), custom_call_target="tpu_custom_call" | custom-call | tf_op jit(solution)/shard_map/image/pallas_call | solution.py:312
  25.9 21.7 %all_to_all.20.parts = bf16[32,16,1152]{2,1,0:T(8,128)(2,1)S(1)} all-to-all(bf16[32,16,1152]{2,1,0:T(8,128)(2,1)S(1)} %bitcast.9), channel_id=1, replica_groups=mesh['dp'=32,'mp'=4] {'dp'}, dimensions={0} | all-to-all | bytes 2359296 | tf_op jit(solution)/shard_map/all_to_all | solution.py:448
  47.9 17.0 %all_to_all.21 = bf16[32,16,1152]{2,1,0:T(8,128)(2,1)S(1)} all-to-all(bf16[32,16,1152]{2,1,0:T(8,128)(2,1)S(1)} %sum_copies.2), channel_id=1, replica_groups=mesh['dp'=32,'mp'=4] {'dp'}, dimensions={0} | all-to-all | bytes 2359296 | tf_op jit(solution)/shard_map/all_to_all | solution.py:449
  64.9 1.9 %raw_send.2 = (f32[160,256]{1,0:T(8,128)S(1)}, bf16[64,2048]{1,0:T(8,128)(2,1)S(1)}, bf16[64,7168]{1,0:T(8,128)(2,1)S(1)}) custom-call(s32[1]{0:T(128)} %bitcast.place, bf16[4,8,16,1152]{3,2,1,0:T(8,128)(2,1)S(1)} %bitcast.6, bf16[512,2048]{1,0:T(8,128)(2,1)S(1)} %get-tuple-element.28.refs_2_.min_ref.refs_3_, ...), custom_call_target="tpu_custom_call" | custom-call | tf_op jit(solution)/shard_map/raw_send/pallas_call | solution.py:199
  66.9 1.5 %raw_keep.2.keep = f32[128,256]{1,0:T(8,128)S(1)} custom-call(s32[1]{0:T(128)} %bitcast.place, bf16[64,2048]{1,0:T(8,128)(2,1)S(1)} %get-tuple-element.31.img_in, bf16[64,7168]{1,0:T(8,128)(2,1)S(1)} %get-tuple-element.32.img_out, bf16[512,2048]{1,0:T(8,128)(2,1)S(1)} %get-tuple-element.28.refs_2_.min_ref.refs_3_, ...), custom_call_target="tpu_custom_call" | custom-call | flops 536870912 | bytes 4194304 | tf_op jit(solution)/shard_map/raw_keep/pallas_call | solution.py:220
  68.5 2.7 %collective-permute-start.4 = (bf16[224,256]{1,0:T(8,128)(2,1)S(1)}, bf16[224,256]{1,0:T(8,128)(2,1)S(1)}, u32[]{:S(2)}, u32[]{:S(2)}) collective-permute-start(bf16[224,256]{1,0:T(8,128)(2,1)S(1)} %get-tuple-element.35), channel_id=1, source_target_pairs={{0,2},{2,0},{1,3},{3,1},{4,6},{6,4},{5,7},{7,5},{8,10},{10,8},{9,1... | collective-permute-start | bytes 344072 | tf_op jit(solution)/shard_map/ppermute | solution.py:454
  71.2 3.1 %collective-permute-done.4.far = bf16[224,256]{1,0:T(8,128)(2,1)S(1)} collective-permute-done((bf16[224,256]{1,0:T(8,128)(2,1)S(1)}, bf16[224,256]{1,0:T(8,128)(2,1)S(1)}, u32[]{:S(2)}, u32[]{:S(2)}) %collective-permute-start.4) | collective-permute-done | bytes 114720 | tf_op jit(solution)/shard_map/ppermute | solution.py:454
  74.3 1.4 %collective-permute-start.5 = (f32[128,256]{1,0:T(8,128)S(1)}, f32[128,256]{1,0:T(8,128)S(1)}, u32[]{:S(2)}, u32[]{:S(2)}) collective-permute-start(f32[128,256]{1,0:T(8,128)S(1)} %get-tuple-element.37.refs_1_), channel_id=1, source_target_pairs={{0,1},{1,0},{2,3},{3,2},{4,5},{5,4},{6,7},{7,6},{8,9},{9,8},{10,11... | collective-permute-start | bytes 393224 | tf_op jit(solution)/shard_map/ppermute | solution.py:456
  75.7 2.3 %inverse.2.refs_0_ = f32[64,128]{1,0:T(8,128)S(1)} custom-call(f32[32,256]{1,0:T(8,128)S(1)} %get-tuple-element.36.gram), custom_call_target="tpu_custom_call" | custom-call | flops 4194304 | bytes 4194304 | tf_op jit(solution)/shard_map/inverse/pallas_call | solution.py:375
  78.0 10.6 %image.3 = bf16[4,8,16,1152]{3,2,1,0:T(8,128)(2,1)S(1)} custom-call(s32[1]{0:T(128)} %bitcast.place, f32[64,128]{1,0:T(8,128)S(1)} %inverse.2.refs_0_, f32[128,256]{1,0:T(8,128)S(1)} %get-tuple-element.37.refs_1_, f32[128,256]{1,0:T(8,128)S(1)} %collective-permute-done.5.refs_2_, bf16[512,2048]{1,0:T(8,128)(2,1)S(1)} %get-tuple-element.28.refs_2_.min_ref.refs_3_, ...), custom_call_target="tpu_custom_call" | custom-call | tf_op jit(solution)/shard_map/image/pallas_call | solution.py:312
  88.6 16.3 %all_to_all.22.parts = bf16[32,16,1152]{2,1,0:T(8,128)(2,1)S(1)} all-to-all(bf16[32,16,1152]{2,1,0:T(8,128)(2,1)S(1)} %bitcast.8), channel_id=1, replica_groups=mesh['dp'=32,'mp'=4] {'dp'}, dimensions={0} | all-to-all | bytes 2359296 | tf_op jit(solution)/shard_map/all_to_all | solution.py:448
  105.1 16.5 %all_to_all.23 = bf16[32,16,1152]{2,1,0:T(8,128)(2,1)S(1)} all-to-all(bf16[32,16,1152]{2,1,0:T(8,128)(2,1)S(1)} %sum_copies.3), channel_id=1, replica_groups=mesh['dp'=32,'mp'=4] {'dp'}, dimensions={0} | all-to-all | bytes 2359296 | tf_op jit(solution)/shard_map/all_to_all | solution.py:449
  121.6 1.9 %raw_send.3 = (f32[160,256]{1,0:T(8,128)S(1)}, bf16[64,2048]{1,0:T(8,128)(2,1)S(1)}, bf16[64,7168]{1,0:T(8,128)(2,1)S(1)}) custom-call(s32[1]{0:T(128)} %bitcast.place, bf16[4,8,16,1152]{3,2,1,0:T(8,128)(2,1)S(1)} %bitcast.7, bf16[512,2048]{1,0:T(8,128)(2,1)S(1)} %get-tuple-element.28.refs_2_.min_ref.refs_3_, ...), custom_call_target="tpu_custom_call" | custom-call | tf_op jit(solution)/shard_map/raw_send/pallas_call | solution.py:199
  123.6 1.5 %raw_keep.3.keep = f32[128,256]{1,0:T(8,128)S(1)} custom-call(s32[1]{0:T(128)} %bitcast.place, bf16[64,2048]{1,0:T(8,128)(2,1)S(1)} %get-tuple-element.38.img_in, bf16[64,7168]{1,0:T(8,128)(2,1)S(1)} %get-tuple-element.39.img_out, bf16[512,2048]{1,0:T(8,128)(2,1)S(1)} %get-tuple-element.28.refs_2_.min_ref.refs_3_, ...), custom_call_target="tpu_custom_call" | custom-call | flops 536870912 | bytes 4194304 | tf_op jit(solution)/shard_map/raw_keep/pallas_call | solution.py:220
  125.2 2.7 %collective-permute-start.7 = (bf16[224,256]{1,0:T(8,128)(2,1)S(1)}, bf16[224,256]{1,0:T(8,128)(2,1)S(1)}, u32[]{:S(2)}, u32[]{:S(2)}) collective-permute-start(bf16[224,256]{1,0:T(8,128)(2,1)S(1)} %get-tuple-element.42), channel_id=1, source_target_pairs={{0,2},{2,0},{1,3},{3,1},{4,6},{6,4},{5,7},{7,5},{8,10},{10,8},{9,1... | collective-permute-start | bytes 344072 | tf_op jit(solution)/shard_map/ppermute | solution.py:454
  127.9 3.1 %collective-permute-done.7.far = bf16[224,256]{1,0:T(8,128)(2,1)S(1)} collective-permute-done((bf16[224,256]{1,0:T(8,128)(2,1)S(1)}, bf16[224,256]{1,0:T(8,128)(2,1)S(1)}, u32[]{:S(2)}, u32[]{:S(2)}) %collective-permute-start.7) | collective-permute-done | bytes 114720 | tf_op jit(solution)/shard_map/ppermute | solution.py:454
  131.0 1.4 %collective-permute-start.8 = (f32[128,256]{1,0:T(8,128)S(1)}, f32[128,256]{1,0:T(8,128)S(1)}, u32[]{:S(2)}, u32[]{:S(2)}) collective-permute-start(f32[128,256]{1,0:T(8,128)S(1)} %get-tuple-element.44.mine), channel_id=1, source_target_pairs={{0,1},{1,0},{2,3},{3,2},{4,5},{5,4},{6,7},{7,6},{8,9},{9,8},{10,11... | collective-permute-start | bytes 393224 | tf_op jit(solution)/shard_map/ppermute | solution.py:456
  132.4 2.3 %inverse.3 = f32[64,128]{1,0:T(8,128)S(1)} custom-call(f32[32,256]{1,0:T(8,128)S(1)} %get-tuple-element.43.gram), custom_call_target="tpu_custom_call" | custom-call | flops 4194304 | bytes 4194304 | tf_op jit(solution)/shard_map/inverse/pallas_call | solution.py:375
  134.7 2.6 %last.1 = (f32[2,1024]{1,0:T(2,128)}, f32[64,2048]{1,0:T(8,128)}, f32[64,7168]{1,0:T(8,128)}) custom-call(s32[1]{0:T(128)} %bitcast.place, f32[64,128]{1,0:T(8,128)S(1)} %inverse.3, f32[128,256]{1,0:T(8,128)S(1)} %get-tuple-element.44.mine, f32[128,256]{1,0:T(8,128)S(1)} %collective-permute-done.8.other, bf16[64,2048]{1,0:T(8,128)(2,1)S(1)} %get-tuple-element.38.img_in, ...), custom_call_target="tpu_custom_call" | custom-call | tf_op jit(solution)/shard_map/last/pallas_call | solution.py:420
  (16 shorter events, 2.6 us)
Async XLA Ops:
  6.0 2.5 %collective-permute-start = (f32[128,256]{1,0:T(8,128)S(1)}, f32[128,256]{1,0:T(8,128)S(1)}, u32[]{:S(2)}, u32[]{:S(2)}) collective-permute-start(f32[128,256]{1,0:T(8,128)S(1)} %get-tuple-element.25), channel_id=1, source_target_pairs={{0,1},{1,0},{2,3},{3,2},{4,5},{5,4},{6,7},{7,6},{8,9},{9,8},{10,11... | collective-permute-start | bytes 393224 | tf_op jit(solution)/shard_map/ppermute | solution.py:441
  8.5 4.8 %collective-permute-start.1 = (bf16[128,256]{1,0:T(8,128)(2,1)S(1)}, bf16[128,256]{1,0:T(8,128)(2,1)S(1)}, u32[]{:S(2)}, u32[]{:S(2)}) collective-permute-start(bf16[128,256]{1,0:T(8,128)(2,1)S(1)} %get-tuple-element.27), channel_id=1, source_target_pairs={{0,2},{2,0},{1,3},{3,1},{4,6},{6,4},{5,7},{7,5},{8,10},{10,8},{9,1... | collective-permute-start | bytes 196616 | tf_op jit(solution)/shard_map/ppermute | solution.py:442
  13.2 2.4 %collective-permute-start.2 = (bf16[128,256]{1,0:T(8,128)(2,1)S(1)}, bf16[128,256]{1,0:T(8,128)(2,1)S(1)}, u32[]{:S(2)}, u32[]{:S(2)}) collective-permute-start(bf16[128,256]{1,0:T(8,128)(2,1)S(1)} %coords.1.refs_0_), channel_id=1, source_target_pairs={{0,1},{1,0},{2,3},{3,2},{4,5},{5,4},{6,7},{7,6},{8,9},{9,8},{10,11... | collective-permute-start | bytes 196616 | tf_op jit(solution)/shard_map/ppermute | solution.py:443
  66.8 1.6 %collective-permute-start.3 = (f32[160,256]{1,0:T(8,128)S(1)}, f32[160,256]{1,0:T(8,128)S(1)}, u32[]{:S(2)}, u32[]{:S(2)}) collective-permute-start(f32[160,256]{1,0:T(8,128)S(1)} %get-tuple-element.33.refs_0_), channel_id=1, source_target_pairs={{0,1},{1,0},{2,3},{3,2},{4,5},{5,4},{6,7},{7,6},{8,9},{9,8},{10,11... | collective-permute-start | bytes 491528 | tf_op jit(solution)/shard_map/ppermute | solution.py:451
  68.5 5.8 %collective-permute-start.4 = (bf16[224,256]{1,0:T(8,128)(2,1)S(1)}, bf16[224,256]{1,0:T(8,128)(2,1)S(1)}, u32[]{:S(2)}, u32[]{:S(2)}) collective-permute-start(bf16[224,256]{1,0:T(8,128)(2,1)S(1)} %get-tuple-element.35), channel_id=1, source_target_pairs={{0,2},{2,0},{1,3},{3,1},{4,6},{6,4},{5,7},{7,5},{8,10},{10,8},{9,1... | collective-permute-start | bytes 344072 | tf_op jit(solution)/shard_map/ppermute | solution.py:454
  74.3 3.7 %collective-permute-start.5 = (f32[128,256]{1,0:T(8,128)S(1)}, f32[128,256]{1,0:T(8,128)S(1)}, u32[]{:S(2)}, u32[]{:S(2)}) collective-permute-start(f32[128,256]{1,0:T(8,128)S(1)} %get-tuple-element.37.refs_1_), channel_id=1, source_target_pairs={{0,1},{1,0},{2,3},{3,2},{4,5},{5,4},{6,7},{7,6},{8,9},{9,8},{10,11... | collective-permute-start | bytes 393224 | tf_op jit(solution)/shard_map/ppermute | solution.py:456
  123.5 1.6 %collective-permute-start.6 = (f32[160,256]{1,0:T(8,128)S(1)}, f32[160,256]{1,0:T(8,128)S(1)}, u32[]{:S(2)}, u32[]{:S(2)}) collective-permute-start(f32[160,256]{1,0:T(8,128)S(1)} %get-tuple-element.40.refs_0_), channel_id=1, source_target_pairs={{0,1},{1,0},{2,3},{3,2},{4,5},{5,4},{6,7},{7,6},{8,9},{9,8},{10,11... | collective-permute-start | bytes 491528 | tf_op jit(solution)/shard_map/ppermute | solution.py:451
  125.2 5.8 %collective-permute-start.7 = (bf16[224,256]{1,0:T(8,128)(2,1)S(1)}, bf16[224,256]{1,0:T(8,128)(2,1)S(1)}, u32[]{:S(2)}, u32[]{:S(2)}) collective-permute-start(bf16[224,256]{1,0:T(8,128)(2,1)S(1)} %get-tuple-element.42), channel_id=1, source_target_pairs={{0,2},{2,0},{1,3},{3,1},{4,6},{6,4},{5,7},{7,5},{8,10},{10,8},{9,1... | collective-permute-start | bytes 344072 | tf_op jit(solution)/shard_map/ppermute | solution.py:454
  131.0 3.7 %collective-permute-start.8 = (f32[128,256]{1,0:T(8,128)S(1)}, f32[128,256]{1,0:T(8,128)S(1)}, u32[]{:S(2)}, u32[]{:S(2)}) collective-permute-start(f32[128,256]{1,0:T(8,128)S(1)} %get-tuple-element.44.mine), channel_id=1, source_target_pairs={{0,1},{1,0},{2,3},{3,2},{4,5},{5,4},{6,7},{7,6},{8,9},{9,8},{10,11... | collective-permute-start | bytes 393224 | tf_op jit(solution)/shard_map/ppermute | solution.py:456

commit v7 on v6

--- a/solution.py
+++ b/solution.py
@@ -428,6 +428,10 @@
     )(place, *coords, img_in, img_out)
 
 
+ORDER = [
+    29, 19, 20, 13, 4, 12, 23, 7, 22, 0, 10, 11, 8, 1, 2, 9,
+    25, 3, 21, 15, 31, 5, 6, 18, 16, 26, 14, 24, 30, 17, 27, 28,
+]
 CORE_SWAP = [(0, 1), (1, 0), (2, 3), (3, 2)]
 CHIP_SWAP = [(0, 2), (2, 0), (1, 3), (3, 1)]
 
@@ -445,8 +449,8 @@
         parts = image_of(place, coords, layer_inputs, out_grads)
         grid = parts.shape
         parts = parts.reshape(grid[0] * grid[1], grid[2], grid[3])
-        parts = lax.all_to_all(parts, "dp", 0, 0)
-        image = lax.all_to_all(sum_copies(parts), "dp", 0, 0).reshape(grid)
+        parts = lax.all_to_all(parts, "dp", 0, 0, axis_index_groups=[ORDER])
+        image = lax.all_to_all(sum_copies(parts), "dp", 0, 0, axis_index_groups=[ORDER]).reshape(grid)
         send, img_in, img_out = raw_send(place, image, layer_inputs, out_grads, mask)
         got = lax.ppermute(send, "mp", CORE_SWAP)
         keep = raw_keep(place, img_in, img_out, layer_inputs, out_grads, mask)

time: 138 us -> 135 us (0.978)
  blocking collectives: 71.6 us -> 69 us
    all_to_all x4, blocking collectives: 71.6 us -> 69 us  [the longest x2 35.5 us: shards(): parts = lax.all_to_all(parts, 'dp', 0, 0, axis_index_groups=[ORDER])]
where the time goes in v7:
time: 135 us
  blocking collectives  69 us (51%)
  Pallas kernels  40.7 us (30%)
  starting transfers between devices  14.9 us (11%)
  waiting for transfers between devices  9.37 us (7%)
    all_to_all x2, blocking collectives, shards(): parts = lax.all_to_all(parts, 'dp', 0, 0, axis_index_groups=[ORDER])  35.5 us
    all_to_all x2, blocking collectives, shards(): lax.all_to_all(sum_copies(parts), 'dp', 0, 0, axis_index_groups=[ORDER])  33.5 us
    pallas_call x2, Pallas kernels, image_of(): pl.pallas_call(image_kernel, out_shape=jax.ShapeDtypeStruct((GROUPS, step...  20.8 us
    ppermute x2, waiting for transfers between devices, shards(): far = lax.ppermute(out, 'mp', CHIP_SWAP)  5.82 us
    ppermute x2, starting transfers between devices, shards(): far = lax.ppermute(out, 'mp', CHIP_SWAP)  5.77 us
    pallas_call x1, Pallas kernels, raw_first(): pl.pallas_call(first_kernel, out_shape=(shape, shape, jax.ShapeDtypeStruc...  5.33 us
    pallas_call x2, Pallas kernels, inverse_of(): pl.pallas_call(inverse_kernel, out_shape=jax.ShapeDtypeStruct((R, 2 * R),...  4.59 us
    pallas_call x2, Pallas kernels, raw_send(): pl.pallas_call(send_kernel, out_shape=(jax.ShapeDtypeStruct((2 * R + R //...  3.74 us
  transfers between devices with their start and end apart: 9, of which 5 were waited for; matrix products, arithmetic and copies ran while one was open for 0% of the time, Pallas kernels for 6%

profile of v7, /device:TPU:1, one launch (start us, length us, event | category | flops | bytes accessed | tf_op | source)
XLA Modules:
  0.0 134.9 jit_solution(14486176418041186594)
XLA Ops:
  0.6 5.3 %raw_first.1 = (f32[128,256]{1,0:T(8,128)S(1)}, f32[128,256]{1,0:T(8,128)S(1)}, bf16[512,2048]{1,0:T(8,128)(2,1)S(1)}, bf16[512,7168]{1,0:T(8,128)(2,1)S(1)}, f32[1,512]{1,0:T(1,128)S(1)}) custom-call(s32[1]{0:T(128)} %bitcast.place, s32[64,2048]{1,0:T(8,128)} %bin_hbm.1, s32[64,7168]{1,0:T(8,128)} %bout_hbm.1, bf16[512,2048]{1,0:T(8,128)(2,1)} %min_hbm.1, ...), custom_call_target="tpu_custom_call" | custom-call | tf_op jit(solution)/shard_map/raw_first/pallas_call | solution.py:147
  6.0 1.5 %collective-permute-start = (f32[128,256]{1,0:T(8,128)S(1)}, f32[128,256]{1,0:T(8,128)S(1)}, u32[]{:S(2)}, u32[]{:S(2)}) collective-permute-start(f32[128,256]{1,0:T(8,128)S(1)} %get-tuple-element.25), channel_id=1, source_target_pairs={{0,1},{1,0},{2,3},{3,2},{4,5},{5,4},{6,7},{7,6},{8,9},{9,8},{10,11... | collective-permute-start | bytes 393224 | tf_op jit(solution)/shard_map/ppermute | solution.py:445
  8.5 3.1 %collective-permute-start.1 = (bf16[128,256]{1,0:T(8,128)(2,1)S(1)}, bf16[128,256]{1,0:T(8,128)(2,1)S(1)}, u32[]{:S(2)}, u32[]{:S(2)}) collective-permute-start(bf16[128,256]{1,0:T(8,128)(2,1)S(1)} %get-tuple-element.27), channel_id=1, source_target_pairs={{0,2},{2,0},{1,3},{3,1},{4,6},{6,4},{5,7},{7,5},{8,10},{10,8},{9,1... | collective-permute-start | bytes 196616 | tf_op jit(solution)/shard_map/ppermute | solution.py:446
  11.6 1.7 %collective-permute-done.1.far = bf16[128,256]{1,0:T(8,128)(2,1)S(1)} collective-permute-done((bf16[128,256]{1,0:T(8,128)(2,1)S(1)}, bf16[128,256]{1,0:T(8,128)(2,1)S(1)}, u32[]{:S(2)}, u32[]{:S(2)}) %collective-permute-start.1) | collective-permute-done | bytes 65568 | tf_op jit(solution)/shard_map/ppermute | solution.py:446
  13.2 1.5 %collective-permute-start.2 = (bf16[128,256]{1,0:T(8,128)(2,1)S(1)}, bf16[128,256]{1,0:T(8,128)(2,1)S(1)}, u32[]{:S(2)}, u32[]{:S(2)}) collective-permute-start(bf16[128,256]{1,0:T(8,128)(2,1)S(1)} %coords.1.refs_0_), channel_id=1, source_target_pairs={{0,1},{1,0},{2,3},{3,2},{4,5},{5,4},{6,7},{7,6},{8,9},{9,8},{10,11... | collective-permute-start | bytes 196616 | tf_op jit(solution)/shard_map/ppermute | solution.py:447
  15.7 10.3 %image.2 = bf16[4,8,16,1152]{3,2,1,0:T(8,128)(2,1)S(1)} custom-call(s32[1]{0:T(128)} %bitcast.place, bf16[128,256]{1,0:T(8,128)(2,1)S(1)} %coords.1.refs_0_, bf16[128,256]{1,0:T(8,128)(2,1)S(1)} %collective-permute-done.2.refs_1_, bf16[512,2048]{1,0:T(8,128)(2,1)S(1)} %get-tuple-element.28.refs_2_.min_ref.refs_3_, ...), custom_call_target="tpu_custom_call" | custom-call | tf_op jit(solution)/shard_map/image/pallas_call | solution.py:312
  25.9 19.0 %all_to_all.20.parts = bf16[32,16,1152]{2,1,0:T(8,128)(2,1)S(1)} all-to-all(bf16[32,16,1152]{2,1,0:T(8,128)(2,1)S(1)} %bitcast.9), channel_id=1, replica_groups={{116,76,80,52,16,48,92,28,88,0,40,44,32,4,8,36,100,12,84,60,124,20,24,7..., dimensions={0} | all-to-all | bytes 2359296 | tf_op jit(solution)/shard_map/all_to_all | solution.py:452
  45.2 16.9 %all_to_all.21 = bf16[32,16,1152]{2,1,0:T(8,128)(2,1)S(1)} all-to-all(bf16[32,16,1152]{2,1,0:T(8,128)(2,1)S(1)} %sum_copies.2), channel_id=1, replica_groups={{116,76,80,52,16,48,92,28,88,0,40,44,32,4,8,36,100,12,84,60,124,20,24,7..., dimensions={0} | all-to-all | bytes 2359296 | tf_op jit(solution)/shard_map/all_to_all | solution.py:453
  62.0 1.9 %raw_send.2 = (f32[160,256]{1,0:T(8,128)S(1)}, bf16[64,2048]{1,0:T(8,128)(2,1)S(1)}, bf16[64,7168]{1,0:T(8,128)(2,1)S(1)}) custom-call(s32[1]{0:T(128)} %bitcast.place, bf16[4,8,16,1152]{3,2,1,0:T(8,128)(2,1)S(1)} %bitcast.6, bf16[512,2048]{1,0:T(8,128)(2,1)S(1)} %get-tuple-element.28.refs_2_.min_ref.refs_3_, ...), custom_call_target="tpu_custom_call" | custom-call | tf_op jit(solution)/shard_map/raw_send/pallas_call | solution.py:199
  64.0 1.5 %raw_keep.2.keep = f32[128,256]{1,0:T(8,128)S(1)} custom-call(s32[1]{0:T(128)} %bitcast.place, bf16[64,2048]{1,0:T(8,128)(2,1)S(1)} %get-tuple-element.31.img_in, bf16[64,7168]{1,0:T(8,128)(2,1)S(1)} %get-tuple-element.32.img_out, bf16[512,2048]{1,0:T(8,128)(2,1)S(1)} %get-tuple-element.28.refs_2_.min_ref.refs_3_, ...), custom_call_target="tpu_custom_call" | custom-call | flops 536870912 | bytes 4194304 | tf_op jit(solution)/shard_map/raw_keep/pallas_call | solution.py:220
  65.6 2.9 %collective-permute-start.4 = (bf16[224,256]{1,0:T(8,128)(2,1)S(1)}, bf16[224,256]{1,0:T(8,128)(2,1)S(1)}, u32[]{:S(2)}, u32[]{:S(2)}) collective-permute-start(bf16[224,256]{1,0:T(8,128)(2,1)S(1)} %get-tuple-element.35), channel_id=1, source_target_pairs={{0,2},{2,0},{1,3},{3,1},{4,6},{6,4},{5,7},{7,5},{8,10},{10,8},{9,1... | collective-permute-start | bytes 344072 | tf_op jit(solution)/shard_map/ppermute | solution.py:458
  68.5 2.9 %collective-permute-done.4.far = bf16[224,256]{1,0:T(8,128)(2,1)S(1)} collective-permute-done((bf16[224,256]{1,0:T(8,128)(2,1)S(1)}, bf16[224,256]{1,0:T(8,128)(2,1)S(1)}, u32[]{:S(2)}, u32[]{:S(2)}) %collective-permute-start.4) | collective-permute-done | bytes 114720 | tf_op jit(solution)/shard_map/ppermute | solution.py:458
  71.4 1.4 %collective-permute-start.5 = (f32[128,256]{1,0:T(8,128)S(1)}, f32[128,256]{1,0:T(8,128)S(1)}, u32[]{:S(2)}, u32[]{:S(2)}) collective-permute-start(f32[128,256]{1,0:T(8,128)S(1)} %get-tuple-element.37.refs_1_), channel_id=1, source_target_pairs={{0,1},{1,0},{2,3},{3,2},{4,5},{5,4},{6,7},{7,6},{8,9},{9,8},{10,11... | collective-permute-start | bytes 393224 | tf_op jit(solution)/shard_map/ppermute | solution.py:460
  72.8 2.3 %inverse.2.refs_0_ = f32[64,128]{1,0:T(8,128)S(1)} custom-call(f32[32,256]{1,0:T(8,128)S(1)} %get-tuple-element.36.gram), custom_call_target="tpu_custom_call" | custom-call | flops 4194304 | bytes 4194304 | tf_op jit(solution)/shard_map/inverse/pallas_call | solution.py:375
  75.1 10.6 %image.3 = bf16[4,8,16,1152]{3,2,1,0:T(8,128)(2,1)S(1)} custom-call(s32[1]{0:T(128)} %bitcast.place, f32[64,128]{1,0:T(8,128)S(1)} %inverse.2.refs_0_, f32[128,256]{1,0:T(8,128)S(1)} %get-tuple-element.37.refs_1_, f32[128,256]{1,0:T(8,128)S(1)} %collective-permute-done.5.refs_2_, bf16[512,2048]{1,0:T(8,128)(2,1)S(1)} %get-tuple-element.28.refs_2_.min_ref.refs_3_, ...), custom_call_target="tpu_custom_call" | custom-call | tf_op jit(solution)/shard_map/image/pallas_call | solution.py:312
  85.7 16.5 %all_to_all.22.parts = bf16[32,16,1152]{2,1,0:T(8,128)(2,1)S(1)} all-to-all(bf16[32,16,1152]{2,1,0:T(8,128)(2,1)S(1)} %bitcast.8), channel_id=1, replica_groups={{116,76,80,52,16,48,92,28,88,0,40,44,32,4,8,36,100,12,84,60,124,20,24,7..., dimensions={0} | all-to-all | bytes 2359296 | tf_op jit(solution)/shard_map/all_to_all | solution.py:452
  102.4 16.6 %all_to_all.23 = bf16[32,16,1152]{2,1,0:T(8,128)(2,1)S(1)} all-to-all(bf16[32,16,1152]{2,1,0:T(8,128)(2,1)S(1)} %sum_copies.3), channel_id=1, replica_groups={{116,76,80,52,16,48,92,28,88,0,40,44,32,4,8,36,100,12,84,60,124,20,24,7..., dimensions={0} | all-to-all | bytes 2359296 | tf_op jit(solution)/shard_map/all_to_all | solution.py:453
  119.0 1.9 %raw_send.3 = (f32[160,256]{1,0:T(8,128)S(1)}, bf16[64,2048]{1,0:T(8,128)(2,1)S(1)}, bf16[64,7168]{1,0:T(8,128)(2,1)S(1)}) custom-call(s32[1]{0:T(128)} %bitcast.place, bf16[4,8,16,1152]{3,2,1,0:T(8,128)(2,1)S(1)} %bitcast.7, bf16[512,2048]{1,0:T(8,128)(2,1)S(1)} %get-tuple-element.28.refs_2_.min_ref.refs_3_, ...), custom_call_target="tpu_custom_call" | custom-call | tf_op jit(solution)/shard_map/raw_send/pallas_call | solution.py:199
  121.0 1.5 %raw_keep.3.keep = f32[128,256]{1,0:T(8,128)S(1)} custom-call(s32[1]{0:T(128)} %bitcast.place, bf16[64,2048]{1,0:T(8,128)(2,1)S(1)} %get-tuple-element.38.img_in, bf16[64,7168]{1,0:T(8,128)(2,1)S(1)} %get-tuple-element.39.img_out, bf16[512,2048]{1,0:T(8,128)(2,1)S(1)} %get-tuple-element.28.refs_2_.min_ref.refs_3_, ...), custom_call_target="tpu_custom_call" | custom-call | flops 536870912 | bytes 4194304 | tf_op jit(solution)/shard_map/raw_keep/pallas_call | solution.py:220
  122.6 2.9 %collective-permute-start.7 = (bf16[224,256]{1,0:T(8,128)(2,1)S(1)}, bf16[224,256]{1,0:T(8,128)(2,1)S(1)}, u32[]{:S(2)}, u32[]{:S(2)}) collective-permute-start(bf16[224,256]{1,0:T(8,128)(2,1)S(1)} %get-tuple-element.42), channel_id=1, source_target_pairs={{0,2},{2,0},{1,3},{3,1},{4,6},{6,4},{5,7},{7,5},{8,10},{10,8},{9,1... | collective-permute-start | bytes 344072 | tf_op jit(solution)/shard_map/ppermute | solution.py:458
  125.5 2.9 %collective-permute-done.7.far = bf16[224,256]{1,0:T(8,128)(2,1)S(1)} collective-permute-done((bf16[224,256]{1,0:T(8,128)(2,1)S(1)}, bf16[224,256]{1,0:T(8,128)(2,1)S(1)}, u32[]{:S(2)}, u32[]{:S(2)}) %collective-permute-start.7) | collective-permute-done | bytes 114720 | tf_op jit(solution)/shard_map/ppermute | solution.py:458
  128.4 1.4 %collective-permute-start.8 = (f32[128,256]{1,0:T(8,128)S(1)}, f32[128,256]{1,0:T(8,128)S(1)}, u32[]{:S(2)}, u32[]{:S(2)}) collective-permute-start(f32[128,256]{1,0:T(8,128)S(1)} %get-tuple-element.44.mine), channel_id=1, source_target_pairs={{0,1},{1,0},{2,3},{3,2},{4,5},{5,4},{6,7},{7,6},{8,9},{9,8},{10,11... | collective-permute-start | bytes 393224 | tf_op jit(solution)/shard_map/ppermute | solution.py:460
  129.8 2.3 %inverse.3 = f32[64,128]{1,0:T(8,128)S(1)} custom-call(f32[32,256]{1,0:T(8,128)S(1)} %get-tuple-element.43.gram), custom_call_target="tpu_custom_call" | custom-call | flops 4194304 | bytes 4194304 | tf_op jit(solution)/shard_map/inverse/pallas_call | solution.py:375
  132.1 2.6 %last.1 = (f32[2,1024]{1,0:T(2,128)}, f32[64,2048]{1,0:T(8,128)}, f32[64,7168]{1,0:T(8,128)}) custom-call(s32[1]{0:T(128)} %bitcast.place, f32[64,128]{1,0:T(8,128)S(1)} %inverse.3, f32[128,256]{1,0:T(8,128)S(1)} %get-tuple-element.44.mine, f32[128,256]{1,0:T(8,128)S(1)} %collective-permute-done.8.other, bf16[64,2048]{1,0:T(8,128)(2,1)S(1)} %get-tuple-element.38.img_in, ...), custom_call_target="tpu_custom_call" | custom-call | tf_op jit(solution)/shard_map/last/pallas_call | solution.py:420
  (16 shorter events, 2.6 us)
Async XLA Ops:
  6.0 2.5 %collective-permute-start = (f32[128,256]{1,0:T(8,128)S(1)}, f32[128,256]{1,0:T(8,128)S(1)}, u32[]{:S(2)}, u32[]{:S(2)}) collective-permute-start(f32[128,256]{1,0:T(8,128)S(1)} %get-tuple-element.25), channel_id=1, source_target_pairs={{0,1},{1,0},{2,3},{3,2},{4,5},{5,4},{6,7},{7,6},{8,9},{9,8},{10,11... | collective-permute-start | bytes 393224 | tf_op jit(solution)/shard_map/ppermute | solution.py:445
  8.5 4.8 %collective-permute-start.1 = (bf16[128,256]{1,0:T(8,128)(2,1)S(1)}, bf16[128,256]{1,0:T(8,128)(2,1)S(1)}, u32[]{:S(2)}, u32[]{:S(2)}) collective-permute-start(bf16[128,256]{1,0:T(8,128)(2,1)S(1)} %get-tuple-element.27), channel_id=1, source_target_pairs={{0,2},{2,0},{1,3},{3,1},{4,6},{6,4},{5,7},{7,5},{8,10},{10,8},{9,1... | collective-permute-start | bytes 196616 | tf_op jit(solution)/shard_map/ppermute | solution.py:446
  13.2 2.4 %collective-permute-start.2 = (bf16[128,256]{1,0:T(8,128)(2,1)S(1)}, bf16[128,256]{1,0:T(8,128)(2,1)S(1)}, u32[]{:S(2)}, u32[]{:S(2)}) collective-permute-start(bf16[128,256]{1,0:T(8,128)(2,1)S(1)} %coords.1.refs_0_), channel_id=1, source_target_pairs={{0,1},{1,0},{2,3},{3,2},{4,5},{5,4},{6,7},{7,6},{8,9},{9,8},{10,11... | collective-permute-start | bytes 196616 | tf_op jit(solution)/shard_map/ppermute | solution.py:447
  63.9 1.6 %collective-permute-start.3 = (f32[160,256]{1,0:T(8,128)S(1)}, f32[160,256]{1,0:T(8,128)S(1)}, u32[]{:S(2)}, u32[]{:S(2)}) collective-permute-start(f32[160,256]{1,0:T(8,128)S(1)} %get-tuple-element.33.refs_0_), channel_id=1, source_target_pairs={{0,1},{1,0},{2,3},{3,2},{4,5},{5,4},{6,7},{7,6},{8,9},{9,8},{10,11... | collective-permute-start | bytes 491528 | tf_op jit(solution)/shard_map/ppermute | solution.py:455
  65.6 5.8 %collective-permute-start.4 = (bf16[224,256]{1,0:T(8,128)(2,1)S(1)}, bf16[224,256]{1,0:T(8,128)(2,1)S(1)}, u32[]{:S(2)}, u32[]{:S(2)}) collective-permute-start(bf16[224,256]{1,0:T(8,128)(2,1)S(1)} %get-tuple-element.35), channel_id=1, source_target_pairs={{0,2},{2,0},{1,3},{3,1},{4,6},{6,4},{5,7},{7,5},{8,10},{10,8},{9,1... | collective-permute-start | bytes 344072 | tf_op jit(solution)/shard_map/ppermute | solution.py:458
  71.4 3.7 %collective-permute-start.5 = (f32[128,256]{1,0:T(8,128)S(1)}, f32[128,256]{1,0:T(8,128)S(1)}, u32[]{:S(2)}, u32[]{:S(2)}) collective-permute-start(f32[128,256]{1,0:T(8,128)S(1)} %get-tuple-element.37.refs_1_), channel_id=1, source_target_pairs={{0,1},{1,0},{2,3},{3,2},{4,5},{5,4},{6,7},{7,6},{8,9},{9,8},{10,11... | collective-permute-start | bytes 393224 | tf_op jit(solution)/shard_map/ppermute | solution.py:460
  120.9 1.6 %collective-permute-start.6 = (f32[160,256]{1,0:T(8,128)S(1)}, f32[160,256]{1,0:T(8,128)S(1)}, u32[]{:S(2)}, u32[]{:S(2)}) collective-permute-start(f32[160,256]{1,0:T(8,128)S(1)} %get-tuple-element.40.refs_0_), channel_id=1, source_target_pairs={{0,1},{1,0},{2,3},{3,2},{4,5},{5,4},{6,7},{7,6},{8,9},{9,8},{10,11... | collective-permute-start | bytes 491528 | tf_op jit(solution)/shard_map/ppermute | solution.py:455
  122.6 5.8 %collective-permute-start.7 = (bf16[224,256]{1,0:T(8,128)(2,1)S(1)}, bf16[224,256]{1,0:T(8,128)(2,1)S(1)}, u32[]{:S(2)}, u32[]{:S(2)}) collective-permute-start(bf16[224,256]{1,0:T(8,128)(2,1)S(1)} %get-tuple-element.42), channel_id=1, source_target_pairs={{0,2},{2,0},{1,3},{3,1},{4,6},{6,4},{5,7},{7,5},{8,10},{10,8},{9,1... | collective-permute-start | bytes 344072 | tf_op jit(solution)/shard_map/ppermute | solution.py:458
  128.4 3.7 %collective-permute-start.8 = (f32[128,256]{1,0:T(8,128)S(1)}, f32[128,256]{1,0:T(8,128)S(1)}, u32[]{:S(2)}, u32[]{:S(2)}) collective-permute-start(f32[128,256]{1,0:T(8,128)S(1)} %get-tuple-element.44.mine), channel_id=1, source_target_pairs={{0,1},{1,0},{2,3},{3,2},{4,5},{5,4},{6,7},{7,6},{8,9},{9,8},{10,11... | collective-permute-start | bytes 393224 | tf_op jit(solution)/shard_map/ppermute | solution.py:460
